TPU v7x, 32 devices: a whole 2x2x4 slice. The times are simulated.
32 devices in a mesh: dp: 8 (over y, x, core), tensor: 4 (over z).
Axes of the slice: x: 2, y: 2, z: 4, core: 2. Of those that a mesh axis runs over, the one named last changes fastest.
Arguments:
- tokens: bfloat16 [2, 4096, 2048], P(None, ('dp', 'tensor')), may hold values from -6 to 6
- cotangent: bfloat16 [2, 4096, 2048], P(None, ('dp', 'tensor')), may hold values from -6 to 6
- doc_lengths: int32 [2, 8, 2], P(None, 'dp'), may hold values from 1 to 448, as said below
- attn_gain: bfloat16 [2048], P('dp'), may hold values from 0.099609375 to 1.8984375
- w_qkv: bfloat16 [2048, 3, 2048], P('dp', None, 'tensor'), may hold values from -0.125 to 0.125
- w_beta: bfloat16 [2048, 16], P('dp', 'tensor'), may hold values from -0.125 to 0.125
- conv_weight: bfloat16 [3, 4, 16, 128], P(None, None, 'tensor', 'dp'), may hold values from -3 to 3
- head_gain: bfloat16 [128], P('dp'), may hold values from 0.099609375 to 1.8984375
- w_out: bfloat16 [2048, 2048], P('tensor', 'dp'), may hold values from -0.125 to 0.125
- ffn_gain: bfloat16 [2048], P('dp'), may hold values from 0.099609375 to 1.8984375
- w_gate_up: bfloat16 [2048, 2, 5632], P('dp', None, 'tensor'), may hold values from -0.125 to 0.125
- w_down: bfloat16 [5632, 2048], P('tensor', 'dp'), may hold values from -0.125 to 0.125
Outputs:
- layer_out: bfloat16 [2, 4096, 2048], P(None, ('dp', 'tensor'))
- tokens_grad: float32 [2, 4096, 2048], P(None, ('dp', 'tensor'))
- attn_gain_grad: float32 [2048], P('dp')
- w_qkv_grad: float32 [2048, 3, 2048], P('dp', None, 'tensor')
- w_beta_grad: float32 [2048, 16], P('dp', 'tensor')
- conv_weight_grad: float32 [3, 4, 16, 128], P(None, None, 'tensor', 'dp')
- head_gain_grad: float32 [128], P('dp')
- w_out_grad: float32 [2048, 2048], P('tensor', 'dp')
- ffn_gain_grad: float32 [2048], P('dp')
- w_gate_up_grad: float32 [2048, 2, 5632], P('dp', None, 'tensor')
- w_down_grad: float32 [5632, 2048], P('tensor', 'dp')
Inputs may be any that keep to these rules, and one draw needn't show every extreme that they name: doc_lengths[m, g] gives the lengths of the two documents packed into buffer g of micro-batch m; each document begins at a multiple of 64 slots, ceil(L1 / 64) + ceil(L2 / 64) is at most 8 and at least half of that, rounded down; the longest reaches the maximum.
All inputs are finite; a program needn't handle non-finite values.
Results may differ from a plain program's by a relative error of at most 0.014.
Values may be sent and summed in bfloat16 or wider, within the bound.
No kernel may reach another device: no remote copies, remote signals or barrier semaphores. Data moves between devices by JAX's collectives and lax.ppermute only.
A program may use at most 320 MiB of HBM per device.

v0:
```python
import jax
import jax.numpy as jnp
from jax import lax
from jax.sharding import PartitionSpec as P

BLOCK = 64


NORM_EPS = 1e-06
HEAD_EPS = 1e-05
HIGHEST = lax.Precision.HIGHEST


def doc_layout(length_pair, slot_count):
    first_end = (length_pair[0] + BLOCK - 1) // BLOCK * BLOCK
    second_end = first_end + (length_pair[1] + BLOCK - 1) // BLOCK * BLOCK
    places = jnp.arange(slot_count, dtype=jnp.int32)
    in_first = places < first_end
    in_second = jnp.logical_and(places >= first_end, places < second_end)
    doc_begin = jnp.where(in_first, 0, jnp.where(in_second, first_end, second_end))
    doc_limit = jnp.where(in_first, length_pair[0], jnp.where(in_second, length_pair[1], 0))
    offset = places - doc_begin
    is_valid = (offset < doc_limit).astype(jnp.float32)
    return (offset, is_valid)


def rms_scale(values, gain_row):
    return values * lax.rsqrt(jnp.mean(values * values, -1, keepdims=True) + NORM_EPS) * gain_row


def swiglu(gate_up):
    return jax.nn.silu(gate_up[:, 0]) * gate_up[:, 1]


def conv_silu(projected, conv_weight, offset):
    slot_count = projected.shape[0]
    channel_count = projected.shape[2]
    conv_taps = jnp.transpose(conv_weight.reshape(3, 4, channel_count), (1, 0, 2))
    convolved = conv_taps[0] * projected
    for lag_step in range(1, 4):
        delayed = jnp.pad(projected[: slot_count - lag_step], ((lag_step, 0), (0, 0), (0, 0)))
        reach_ok = (offset >= lag_step).astype(projected.dtype)[:, None, None]
        convolved = convolved + conv_taps[lag_step] * delayed * reach_ok
    return jax.nn.silu(convolved)


def split_heads(convolved, beta_logit, head_dim, is_valid):
    slot_count = convolved.shape[0]
    head_count = beta_logit.shape[1]
    queries = convolved[:, 0].reshape(slot_count, head_count, head_dim)
    keys_all = convolved[:, 1].reshape(slot_count, head_count, head_dim)
    values_all = convolved[:, 2].reshape(slot_count, head_count, head_dim)
    queries = (
        queries
        * lax.rsqrt(jnp.sum(queries * queries, -1, keepdims=True) + NORM_EPS)
        * head_dim ** (-0.5)
    )
    keys_all = keys_all * lax.rsqrt(jnp.sum(keys_all * keys_all, -1, keepdims=True) + NORM_EPS)
    strength = jax.nn.sigmoid(beta_logit) * is_valid[:, None]
    return (queries, keys_all, values_all, strength)


def mixer_core(projected, beta_logit, conv_weight, head_gain, offset, is_valid):
    slot_count = projected.shape[0]
    head_dim = head_gain.shape[0]
    head_count = beta_logit.shape[1]
    convolved = conv_silu(projected, conv_weight, offset)
    queries, keys_all, values_all, strength = split_heads(convolved, beta_logit, head_dim, is_valid)
    block_count = slot_count // BLOCK

    def blocked(tensor):
        return jnp.transpose(tensor.reshape(block_count, BLOCK, head_count, -1), (0, 2, 1, 3))

    restart = (offset.reshape(block_count, BLOCK)[:, 0] == 0).astype(jnp.float32)
    lower_strict = jnp.tril(jnp.ones((BLOCK, BLOCK), jnp.float32), -1)
    lower_full = jnp.tril(jnp.ones((BLOCK, BLOCK), jnp.float32), 0)
    identity_mat = jnp.eye(BLOCK, dtype=jnp.float32)

    def block_step(memory, inputs):
        q_block, k_block, v_block, b_block, restart_flag = inputs
        memory = memory * (1.0 - restart_flag)
        gram_matrix = jnp.einsum("hik,hjk->hij", k_block, k_block, precision=HIGHEST)
        system = identity_mat + lower_strict * (b_block[:, :, None] * gram_matrix)
        weighted = jax.scipy.linalg.solve_triangular(
            system, b_block[:, :, None] * k_block, lower=True, unit_diagonal=True
        )
        updates = jax.scipy.linalg.solve_triangular(
            system, b_block[:, :, None] * v_block, lower=True, unit_diagonal=True
        )
        updates = updates - jnp.einsum("hik,hvk->hiv", weighted, memory, precision=HIGHEST)
        scores = lower_full * jnp.einsum("hik,hjk->hij", q_block, k_block, precision=HIGHEST)
        output = jnp.einsum("hik,hvk->hiv", q_block, memory, precision=HIGHEST)
        output = output + jnp.einsum("hij,hjv->hiv", scores, updates, precision=HIGHEST)
        memory = memory + jnp.einsum("hiv,hik->hvk", updates, k_block, precision=HIGHEST)
        return (memory, output)

    initial = jnp.zeros((head_count, head_dim, head_dim), jnp.float32)
    strength_blocks = jnp.transpose(strength.reshape(block_count, BLOCK, head_count), (0, 2, 1))
    final_state, outputs = lax.scan(
        block_step,
        initial,
        (blocked(queries), blocked(keys_all), blocked(values_all), strength_blocks, restart),
    )
    recalls = jnp.transpose(outputs, (0, 2, 1, 3)).reshape(slot_count, head_count, head_dim)
    normed = (
        recalls * lax.rsqrt(jnp.mean(recalls * recalls, -1, keepdims=True) + HEAD_EPS) * head_gain
    )
    normed = normed * is_valid[:, None, None]
    return normed.reshape(slot_count, head_count * head_dim)


def fetch_mixer(attn_gain, w_qkv, w_beta, conv_weight, head_gain, w_out):
    return (
        lax.all_gather(attn_gain, "dp", axis=0, tiled=True),
        lax.all_gather(w_qkv, "dp", axis=0, tiled=True),
        lax.all_gather(w_beta, "dp", axis=0, tiled=True),
        lax.all_gather(conv_weight, "dp", axis=3, tiled=True),
        lax.all_gather(head_gain, "dp", axis=0, tiled=True),
        lax.all_gather(w_out, "dp", axis=1, tiled=True),
    )


def fetch_ffn(ffn_gain, w_gate_up, w_down):
    return (
        lax.all_gather(ffn_gain, "dp", axis=0, tiled=True),
        lax.all_gather(w_gate_up, "dp", axis=0, tiled=True),
        lax.all_gather(w_down, "dp", axis=1, tiled=True),
    )


def unpack_sets(mixer_set, ffn_set):
    full_attn_gain, full_qkv, full_beta, full_conv, full_head_gain, full_out = mixer_set
    full_ffn_gain, full_gate_up, full_down = ffn_set
    model_width = full_qkv.shape[0]
    proj_matrix = jnp.concatenate([full_qkv.reshape(model_width, -1), full_beta], axis=1)
    return (
        full_attn_gain.astype(jnp.float32),
        proj_matrix,
        full_conv.astype(jnp.float32),
        full_head_gain.astype(jnp.float32),
        full_out,
        full_ffn_gain.astype(jnp.float32),
        full_gate_up.reshape(model_width, -1),
        full_down,
    )


def per_device(
    tokens,
    cotangent,
    doc_lengths,
    attn_gain,
    w_qkv,
    w_beta,
    conv_weight,
    head_gain,
    w_out,
    ffn_gain,
    w_gate_up,
    w_down,
):
    batches = tokens.shape[0]
    local_rows = tokens.shape[1]
    model_width = tokens.shape[2]
    group_slots = local_rows * lax.axis_size("tensor")
    qkv_cols = 3 * w_qkv.shape[2]
    local_heads = w_beta.shape[1]
    unit_cols = w_gate_up.shape[2]
    head_dim = conv_weight.shape[3] * lax.axis_size("dp")
    mixer_set = None
    ffn_set = None
    grad_proj = jnp.zeros((model_width, qkv_cols + local_heads), jnp.float32)
    grad_conv = jnp.zeros((3, 4, local_heads, head_dim), jnp.float32)
    grad_head_gain = jnp.zeros((head_dim,), jnp.float32)
    grad_out = jnp.zeros((w_out.shape[0], model_width), jnp.float32)
    grad_attn_gain = jnp.zeros((model_width,), jnp.float32)
    grad_ffn_gain = jnp.zeros((model_width,), jnp.float32)
    grad_gate_up = jnp.zeros((model_width, 2 * unit_cols), jnp.float32)
    grad_down = jnp.zeros((unit_cols, model_width), jnp.float32)
    layer_rows = []
    input_rows = []
    for batch_index in range(batches):
        mixer_set = fetch_mixer(attn_gain, w_qkv, w_beta, conv_weight, head_gain, w_out)
        ffn_set = fetch_ffn(ffn_gain, w_gate_up, w_down)
        (
            full_attn_gain,
            proj_matrix,
            full_conv,
            full_head_gain,
            full_out,
            full_ffn_gain,
            gate_up_matrix,
            full_down,
        ) = unpack_sets(mixer_set, ffn_set)
        offset, is_valid = doc_layout(doc_lengths[batch_index, 0], group_slots)
        row_values = tokens[batch_index].astype(jnp.float32)
        attn_norm, attn_pull = jax.vjp(rms_scale, row_values, full_attn_gain)
        attn_full = lax.all_gather(attn_norm.astype(jnp.bfloat16), "tensor", axis=0, tiled=True)
        projections = jnp.dot(attn_full, proj_matrix, preferred_element_type=jnp.float32)
        projected = projections[:, :qkv_cols].reshape(group_slots, 3, -1)
        beta_logit = projections[:, qkv_cols:]

        def core_call(projected_in, logit_in, conv_in, gain_in):
            return mixer_core(projected_in, logit_in, conv_in, gain_in, offset, is_valid)

        mixed, core_pull = jax.vjp(core_call, projected, beta_logit, full_conv, full_head_gain)
        mixed_low = mixed.astype(jnp.bfloat16)
        hidden = row_values + lax.psum_scatter(
            jnp.dot(mixed_low, full_out, preferred_element_type=jnp.float32),
            "tensor",
            scatter_dimension=0,
            tiled=True,
        )
        ffn_norm, ffn_pull = jax.vjp(rms_scale, hidden, full_ffn_gain)
        ffn_full = lax.all_gather(ffn_norm.astype(jnp.bfloat16), "tensor", axis=0, tiled=True)
        gate_up = jnp.dot(ffn_full, gate_up_matrix, preferred_element_type=jnp.float32).reshape(
            group_slots, 2, unit_cols
        )
        activated, swiglu_pull = jax.vjp(swiglu, gate_up)
        act_low = activated.astype(jnp.bfloat16)
        result = hidden + lax.psum_scatter(
            jnp.dot(act_low, full_down, preferred_element_type=jnp.float32).astype(jnp.bfloat16),
            "tensor",
            scatter_dimension=0,
            tiled=True,
        ).astype(jnp.float32)
        layer_rows.append(result.astype(jnp.bfloat16))
        mixer_set = fetch_mixer(attn_gain, w_qkv, w_beta, conv_weight, head_gain, w_out)
        ffn_set = fetch_ffn(ffn_gain, w_gate_up, w_down)
        (
            full_attn_gain,
            proj_matrix,
            full_conv,
            full_head_gain,
            full_out,
            full_ffn_gain,
            gate_up_matrix,
            full_down,
        ) = unpack_sets(mixer_set, ffn_set)
        cot_full = lax.all_gather(cotangent[batch_index], "tensor", axis=0, tiled=True)
        grad_act = jnp.dot(cot_full, full_down.T, preferred_element_type=jnp.float32)
        grad_down = grad_down + jnp.dot(act_low.T, cot_full, preferred_element_type=jnp.float32)
        (grad_gu,) = swiglu_pull(grad_act)
        grad_gu_low = grad_gu.reshape(group_slots, 2 * unit_cols).astype(jnp.bfloat16)
        grad_gate_up = grad_gate_up + jnp.dot(
            ffn_full.T, grad_gu_low, preferred_element_type=jnp.float32
        )
        grad_ffn_norm = lax.psum_scatter(
            jnp.dot(grad_gu_low, gate_up_matrix.T, preferred_element_type=jnp.float32),
            "tensor",
            scatter_dimension=0,
            tiled=True,
        )
        hidden_part, ffn_gain_part = ffn_pull(grad_ffn_norm)
        grad_ffn_gain = grad_ffn_gain + ffn_gain_part
        grad_hidden = cotangent[batch_index].astype(jnp.float32) + hidden_part
        branch_full = lax.all_gather(grad_hidden.astype(jnp.bfloat16), "tensor", axis=0, tiled=True)
        grad_mixed = jnp.dot(branch_full, full_out.T, preferred_element_type=jnp.float32)
        grad_out = grad_out + jnp.dot(mixed_low.T, branch_full, preferred_element_type=jnp.float32)
        proj_part, beta_part, conv_part, gain_part = core_pull(grad_mixed)
        grad_cat = jnp.concatenate(
            [proj_part.reshape(group_slots, qkv_cols), beta_part], axis=1
        ).astype(jnp.bfloat16)
        grad_proj = grad_proj + jnp.dot(attn_full.T, grad_cat, preferred_element_type=jnp.float32)
        grad_conv = grad_conv + conv_part
        grad_head_gain = grad_head_gain + gain_part
        grad_attn_norm = lax.psum_scatter(
            jnp.dot(grad_cat, proj_matrix.T, preferred_element_type=jnp.float32).astype(
                jnp.bfloat16
            ),
            "tensor",
            scatter_dimension=0,
            tiled=True,
        ).astype(jnp.float32)
        rows_part, attn_gain_part = attn_pull(grad_attn_norm)
        grad_attn_gain = grad_attn_gain + attn_gain_part
        input_rows.append(grad_hidden + rows_part)
    summed_gains = lax.psum((grad_attn_gain, grad_head_gain, grad_ffn_gain), "tensor")
    qkv_grad = grad_proj[:, :qkv_cols].reshape(model_width, 3, -1)
    beta_grad = grad_proj[:, qkv_cols:]
    shares = (
        lax.psum_scatter(summed_gains[0], "dp", scatter_dimension=0, tiled=True),
        lax.psum_scatter(qkv_grad, "dp", scatter_dimension=0, tiled=True),
        lax.psum_scatter(beta_grad, "dp", scatter_dimension=0, tiled=True),
        lax.psum_scatter(grad_conv, "dp", scatter_dimension=3, tiled=True),
        lax.psum_scatter(summed_gains[1], "dp", scatter_dimension=0, tiled=True),
        lax.psum_scatter(grad_out, "dp", scatter_dimension=1, tiled=True),
        lax.psum_scatter(summed_gains[2], "dp", scatter_dimension=0, tiled=True),
        lax.psum_scatter(
            grad_gate_up.reshape(model_width, 2, unit_cols), "dp", scatter_dimension=0, tiled=True
        ),
        lax.psum_scatter(grad_down, "dp", scatter_dimension=1, tiled=True),
    )
    return (
        jnp.stack(layer_rows),
        jnp.stack(input_rows),
        shares[0],
        shares[1],
        shares[2],
        shares[3],
        shares[4],
        shares[5],
        shares[6],
        shares[7],
        shares[8],
    )


def solution(mesh):
    return jax.shard_map(
        per_device,
        mesh=mesh,
        in_specs=(
            P(None, ("dp", "tensor"), None),
            P(None, ("dp", "tensor"), None),
            P(None, "dp", None),
            P("dp"),
            P("dp", None, "tensor"),
            P("dp", "tensor"),
            P(None, None, "tensor", "dp"),
            P("dp"),
            P("tensor", "dp"),
            P("dp"),
            P("dp", None, "tensor"),
            P("tensor", "dp"),
        ),
        out_specs=(
            P(None, ("dp", "tensor"), None),
            P(None, ("dp", "tensor"), None),
            P("dp"),
            P("dp", None, "tensor"),
            P("dp", "tensor"),
            P(None, None, "tensor", "dp"),
            P("dp"),
            P("tensor", "dp"),
            P("dp"),
            P("dp", None, "tensor"),
            P("tensor", "dp"),
        ),
        check_vma=False,
    )
```

profile of v0, /device:TPU:0, one launch (start us, length us, event | category | flops | bytes accessed | tf_op | source)
XLA Modules:
  0.0 2905.9 jit_solution(15084550355762813612)
XLA Ops:
  69.1 47.9 %all-gather.19.cloned.1.call-done = bf16[2048,3,512]{0,2,1:T(8,128)(2,1)} async-done(((bf16[256,3,512]{0,2,1:T(8,128)(2,1)}), bf16[2048,3,512]{0,2,1:T(8,128)(2,1)}) %all-gather.19.cloned.1.call-update) | async-done | bytes 6291472 | tf_op jit(solution)/shard_map/all_gather | solution.py:115
  131.6 33.3 %all-gather.29.cloned.1.call-done = bf16[512,2048]{1,0:T(8,128)(2,1)} async-done(((bf16[128,2048]{1,0:T(8,128)(2,1)}), bf16[512,2048]{1,0:T(8,128)(2,1)}) %all-gather.29.cloned.1.call-update) | async-done | bytes 2097168 | tf_op jit(solution)/shard_map/all_gather | solution.py:198
  266.0 269.6 %while.120 = (s32[]{:T(128)}, f32[4,128,128]{2,1,0:T(8,128)S(1)}, f32[8,4,64,128]{3,2,1,0:T(8,128)S(1)}, f32[8]{0:T(128)S(1)}, f32[8,4,64,64]{3,2,1,0:T(8,128)},...) while((s32[]{:T(128)}, f32[4,128,128]{2,1,0:T(8,128)S(1)}, ...), condition=%wide.region_4.6_spmd.clone, body=%wide.region_3.5_spmd.clone.sunk | while | flops 277729344 | bytes 5354505 | solution.py:99
  271.6 19.7 custom-call.30
  558.5 274.6 %while.121 = (s32[]{:T(128)}, f32[4,128,128]{2,1,0:T(8,128)S(1)}, f32[8,4,64,128]{3,2,1,0:T(8,128)}, f32[8]{0:T(128)S(1)}, f32[8,4,64,64]{3,2,1,0:T(8,128)}, /*i...) while((s32[]{:T(128)}, f32[4,128,128]{2,1,0:T(8,128)S(1)}, ...), condition=%wide.region_13.15_spmd.clone, body=%wide.region_12.14_spmd.clone.sunk | while | flops 277729344 | bytes 5354505 | solution.py:99
  863.9 58.6 %reduce-scatter.18.cloned.1.call-done = f32[128,2048]{1,0:T(8,128)} async-done(((f32[512,2048]{1,0:T(8,128)}), f32[128,2048]{1,0:T(8,128)}) %reduce-scatter.18.cloned.1.call-update) | async-done | bytes 1048592 | tf_op jit(solution)/shard_map/reduce_scatter | solution.py:208
  922.5 79.5 %reduce-scatter.22.cloned.1.call-done = f32[128,2048]{1,0:T(8,128)} async-done(((f32[512,2048]{1,0:T(8,128)}), f32[128,2048]{1,0:T(8,128)}) %reduce-scatter.22.cloned.1.call-update) | async-done | bytes 1048592 | tf_op jit(solution)/shard_map/reduce_scatter | solution.py:208
  1008.0 64.5 %all-gather.25.cloned.1.call-done = bf16[2048,2,1408]{2,0,1:T(8,128)(2,1)} async-done(((bf16[256,2,1408]{2,0,1:T(8,128)(2,1)}), bf16[2048,2,1408]{2,0,1:T(8,128)(2,1)}) %all-gather.25.cloned.1.call-update) | async-done | bytes 11534352 | tf_op jit(solution)/shard_map/all_gather | solution.py:126
  1087.9 32.5 %all-gather.23.cloned.1.call-done = bf16[512,2048]{1,0:T(8,128)(2,1)} async-done(((bf16[128,2048]{1,0:T(8,128)(2,1)}), bf16[512,2048]{1,0:T(8,128)(2,1)}) %all-gather.23.cloned.1.call-update) | async-done | bytes 2097168 | tf_op jit(solution)/shard_map/all_gather | solution.py:215
  1132.1 34.9 %all-gather.37.cloned.1.call-done = bf16[1,512,2048]{2,1,0:T(8,128)(2,1)} async-done(((bf16[1,128,2048]{2,1,0:T(8,128)(2,1)}), bf16[1,512,2048]{2,1,0:T(8,128)(2,1)}) %all-gather.37.cloned.1.call-update) | async-done | bytes 2097168 | tf_op jit(solution)/shard_map/all_gather | solution.py:240
  1167.0 44.8 %all-gather.27.cloned.1.call-done = bf16[1408,2048]{1,0:T(8,128)(2,1)} async-done(((bf16[1408,256]{1,0:T(8,128)(2,1)}), bf16[1408,2048]{1,0:T(8,128)(2,1)}) %all-gather.27.cloned.1.call-update) | async-done | bytes 5767184 | tf_op jit(solution)/shard_map/all_gather | solution.py:127
  1234.5 76.9 %reduce-scatter.26.cloned.1.call-done = f32[128,2048]{1,0:T(8,128)} async-done(((f32[512,2048]{1,0:T(8,128)}), f32[128,2048]{1,0:T(8,128)}) %reduce-scatter.26.cloned.1.call-update) | async-done | bytes 1048592 | tf_op jit(solution)/shard_map/reduce_scatter | solution.py:248
  1315.1 45.5 %all-gather.31.cloned.1.call-done = bf16[512,2048]{1,0:T(8,128)(2,1)} async-done(((bf16[128,2048]{1,0:T(8,128)(2,1)}), bf16[512,2048]{1,0:T(8,128)(2,1)}) %all-gather.31.cloned.1.call-update) | async-done | bytes 2097168 | tf_op jit(solution)/shard_map/all_gather | solution.py:215
  1372.8 33.9 %all-gather.39.cloned.1.call-done = bf16[1,512,2048]{2,1,0:T(8,128)(2,1)} async-done(((bf16[1,128,2048]{2,1,0:T(8,128)(2,1)}), bf16[1,512,2048]{2,1,0:T(8,128)(2,1)}) %all-gather.39.cloned.1.call-update) | async-done | bytes 2097168 | tf_op jit(solution)/shard_map/all_gather | solution.py:240
  1437.7 67.5 %reduce-scatter.30.cloned.1.call-done = f32[128,2048]{1,0:T(8,128)} async-done(((f32[512,2048]{1,0:T(8,128)}), f32[128,2048]{1,0:T(8,128)}) %reduce-scatter.30.cloned.1.call-update) | async-done | bytes 1048592 | tf_op jit(solution)/shard_map/reduce_scatter | solution.py:248
  1507.3 44.2 %reduce-scatter.24.cloned.1.call-done = bf16[128,2048]{1,0:T(8,128)(2,1)} async-done(((bf16[512,2048]{1,0:T(8,128)(2,1)}), bf16[128,2048]{1,0:T(8,128)(2,1)}) %reduce-scatter.24.cloned.1.call-update) | async-done | bytes 524304 | tf_op jit(solution)/shard_map/reduce_scatter | solution.py:221
  1603.8 27.0 reshape.891
  1662.9 344.5 %while.122 = (s32[]{:T(128)}, f32[4,128,128]{2,1,0:T(8,128)S(1)}, f32[8,4,64,128]{3,2,1,0:T(8,128)}, f32[8,4,64,128]{3,2,1,0:T(8,128)}, f32[8,4,64,128]{3,2,1,0:...) while((s32[]{:T(128)}, f32[4,128,128]{2,1,0:T(8,128)S(1)}, ...), condition=%wide.region_25.28_spmd.clone.clone, body=%wide.region_21.27_spmd.clone.clone.sunk | while | flops 579907392 | bytes 9333823 | solution.py:99
  2010.8 344.2 %while.123 = (s32[]{:T(128)}, f32[4,128,128]{2,1,0:T(8,128)S(1)}, f32[8,4,64,128]{3,2,1,0:T(8,128)}, f32[8,4,64,128]{3,2,1,0:T(8,128)}, f32[8,4,64,128]{3,2,1,0:...) while((s32[]{:T(128)}, f32[4,128,128]{2,1,0:T(8,128)S(1)}, ...), condition=%wide.region_37.40_spmd.clone.clone, body=%wide.region_33.39_spmd.clone.clone.sunk | while | flops 579907392 | bytes 9333823 | solution.py:99
  2567.5 45.1 %reduce-scatter.32.cloned.1.call-done = bf16[128,2048]{1,0:T(8,128)(2,1)} async-done(((bf16[512,2048]{1,0:T(8,128)(2,1)}), bf16[128,2048]{1,0:T(8,128)(2,1)}) %reduce-scatter.32.cloned.1.call-update) | async-done | bytes 524304 | tf_op jit(solution)/shard_map/reduce_scatter | solution.py:267
  2614.9 24.8 all-reduce.35
  2663.8 84.3 %reduce-scatter.38.cloned.1.call-done = f32[1408,256]{1,0:T(8,128)} async-done(((f32[1408,2048]{1,0:T(8,128)}), f32[1408,256]{1,0:T(8,128)}) %reduce-scatter.38.cloned.1.call-update) | async-done | bytes 1441808 | tf_op jit(solution)/shard_map/reduce_scatter | solution.py:292
  2748.1 55.0 %reduce-scatter.36.cloned.1.call-done = f32[512,256]{1,0:T(8,128)} async-done(((f32[512,2048]{1,0:T(8,128)}), f32[512,256]{1,0:T(8,128)}) %reduce-scatter.36.cloned.1.call-update) | async-done | bytes 524304 | tf_op jit(solution)/shard_map/reduce_scatter | solution.py:287
  2803.1 96.0 %reduce-scatter.34.cloned.1.call-done = f32[256,3,512]{2,0,1:T(8,128)} async-done(((f32[2048,3,512]{2,0,1:T(8,128)}), f32[256,3,512]{2,0,1:T(8,128)}) %reduce-scatter.34.cloned.1.call-update) | async-done | bytes 1572880 | tf_op jit(solution)/shard_map/reduce_scatter | solution.py:283
  (1428 shorter events, 1864.9 us)
Async XLA Ops:
  23.0 94.0 %all-gather.19.cloned.1.call-start = ((), (), s32[]{:S(2)}) async-start(), calls=%async_computation.14 | async-start | bytes 7077888 | tf_op jit(solution)/shard_map/all_gather | solution.py:115
  24.2 140.6 %all-gather.29.cloned.1.call-start = ((), (), s32[]{:S(2)}) async-start(), calls=%async_computation.21 | async-start | bytes 2621440 | tf_op jit(solution)/shard_map/all_gather | solution.py:198
  25.0 816.4 %all-gather.21.cloned.1.call-start = ((), (), s32[]{:S(2)}) async-start(), calls=%async_computation.15 | async-start | bytes 2359296 | tf_op jit(solution)/shard_map/all_gather | solution.py:119
  25.6 896.9 %reduce-scatter.18.cloned.1.call-start = ((), (), s32[]{:S(2)}) async-start(), calls=%async_computation.16 | async-start | bytes 5242880 | tf_op jit(solution)/shard_map/reduce_scatter | solution.py:208
  846.9 155.0 %reduce-scatter.22.cloned.1.call-start = ((), (), s32[]{:S(2)}) async-start(), calls=%async_computation.22 | async-start | bytes 5242880 | tf_op jit(solution)/shard_map/reduce_scatter | solution.py:208
  851.9 220.6 %all-gather.25.cloned.1.call-start = ((), (), s32[]{:S(2)}) async-start(), calls=%async_computation.18 | async-start | bytes 12976128 | tf_op jit(solution)/shard_map/all_gather | solution.py:126
  854.7 265.7 %all-gather.23.cloned.1.call-start = ((), (), s32[]{:S(2)}) async-start(), calls=%async_computation.17 | async-start | bytes 2621440 | tf_op jit(solution)/shard_map/all_gather | solution.py:215
  1005.0 162.0 %all-gather.37.cloned.1.call-start = ((), (), s32[]{:S(2)}) async-start(), calls=%async_computation.34 | async-start | bytes 2621440 | tf_op jit(solution)/shard_map/all_gather | solution.py:240
  1007.4 204.4 %all-gather.27.cloned.1.call-start = ((), (), s32[]{:S(2)}) async-start(), calls=%async_computation.19 | async-start | bytes 6488064 | tf_op jit(solution)/shard_map/all_gather | solution.py:127
  1008.0 303.4 %reduce-scatter.26.cloned.1.call-start = ((), (), s32[]{:S(2)}) async-start(), calls=%async_computation.25 | async-start | bytes 5242880 | tf_op jit(solution)/shard_map/reduce_scatter | solution.py:248
  1234.4 126.2 %all-gather.31.cloned.1.call-start = ((), (), s32[]{:S(2)}) async-start(), calls=%async_computation.23 | async-start | bytes 2621440 | tf_op jit(solution)/shard_map/all_gather | solution.py:215
  1314.3 92.4 %all-gather.39.cloned.1.call-start = ((), (), s32[]{:S(2)}) async-start(), calls=%async_computation.35 | async-start | bytes 2621440 | tf_op jit(solution)/shard_map/all_gather | solution.py:240
  1315.1 190.1 %reduce-scatter.30.cloned.1.call-start = ((), (), s32[]{:S(2)}) async-start(), calls=%async_computation.28 | async-start | bytes 5242880 | tf_op jit(solution)/shard_map/reduce_scatter | solution.py:248
  1429.4 122.1 %reduce-scatter.24.cloned.1.call-start = ((), (), s32[]{:S(2)}) async-start(), calls=%async_computation.24 | async-start | bytes 2621440 | tf_op jit(solution)/shard_map/reduce_scatter | solution.py:221
  1437.4 193.8 %all-gather.33.cloned.1.call-start = ((), (), s32[]{:S(2)}) async-start(), calls=%async_computation.26 | async-start | bytes 2621440 | tf_op jit(solution)/shard_map/all_gather | solution.py:257
  1571.2 969.9 %all-reduce.39.cloned.1.call-start = ((), (), s32[]{:S(2)}) async-start(), calls=%async_computation.38 | async-start | bytes 46137344
  1630.8 914.8 %reduce-scatter.42.cloned.1.call-start = ((), (), s32[]{:S(2)}) async-start(), calls=%async_computation.37 | async-start | bytes 73728
  2449.3 97.9 %reduce-scatter.40.cloned.1.call-start = ((), (), s32[]{:S(2)}) async-start(), calls=%async_computation.36 | async-start | bytes 1179648
  2472.6 94.9 %reduce-scatter.28.cloned.1.call-start = ((), (), s32[]{:S(2)}) async-start(), calls=%async_computation.27 | async-start | bytes 2621440 | tf_op jit(solution)/shard_map/reduce_scatter | solution.py:267
  2480.8 131.8 %reduce-scatter.32.cloned.1.call-start = ((), (), s32[]{:S(2)}) async-start(), calls=%async_computation.30 | async-start | bytes 2621440 | tf_op jit(solution)/shard_map/reduce_scatter | solution.py:267
  2489.4 168.6 %reduce-scatter.20.cloned.1.call-start = ((), (), s32[]{:S(2)}) async-start(), calls=%async_computation.20 | async-start | bytes 2621440 | tf_op jit(solution)/shard_map/reduce_scatter | solution.py:221
  2496.9 251.1 %reduce-scatter.38.cloned.1.call-start = ((), (), s32[]{:S(2)}) async-start(), calls=%async_computation.33 | async-start | bytes 12976128 | tf_op jit(solution)/shard_map/reduce_scatter | solution.py:292
  2508.5 294.5 %reduce-scatter.36.cloned.1.call-start = ((), (), s32[]{:S(2)}) async-start(), calls=%async_computation.32 | async-start | bytes 4718592 | tf_op jit(solution)/shard_map/reduce_scatter | solution.py:287
  2515.3 383.8 %reduce-scatter.34.cloned.1.call-start = ((), (), s32[]{:S(2)}) async-start(), calls=%async_computation.31 | async-start | bytes 14155776 | tf_op jit(solution)/shard_map/reduce_scatter | solution.py:283
  (164 other events, 8572.3 us)
Sparse Core Ops, SparseCore 0:
  23.1 45.9 all-gather.16
  71.6 45.3 all-gather.18
  119.1 45.6 all-gather.28
  847.1 75.3 reduce-scatter.17
  924.6 77.2 reduce-scatter.21
  1004.4 68.0 all-gather.24
  1074.7 45.6 all-gather.22
  1122.5 44.4 all-gather.36
  1168.7 43.0 all-gather.26
  1234.5 76.7 reduce-scatter.25
  1314.5 46.1 all-gather.30
  1362.2 44.4 all-gather.38
  1429.6 75.5 reduce-scatter.29
  1507.3 44.1 reduce-scatter.23
  1555.1 44.8 all-gather.32
  1601.4 44.4 all-gather.34
  1649.5 285.0 all-reduce.38
  2485.0 35.9 reduce-scatter.39
  2523.8 43.5 reduce-scatter.27
  2569.8 42.8 reduce-scatter.31
  2614.9 43.0 reduce-scatter.19
  2662.0 86.0 reduce-scatter.37
  2752.0 51.0 reduce-scatter.35
  2807.0 92.0 reduce-scatter.33
  (2 shorter events, 58.7 us)
where the time goes:
time: 2920 us; the launch traced here: 2910 us
  waiting for transfers between devices  983 us (34%)
  other arithmetic  809 us (28%)
  matrix products  698 us (24%)
  local copies, waits for them, and re-layouts  301 us (10%)
  blocking collectives  87.4 us (3%)
    another operation x64, other arithmetic, block_step(): jax.scipy.linalg.solve_triangular(system, b_block[:, :, None] * k_block,...  331 us
    another operation x64, other arithmetic, block_step(): jax.scipy.linalg.solve_triangular(system, b_block[:, :, None] * v_block,...  318 us
    reduce_scatter x2, waiting for transfers between devices, per_device(): lax.psum_scatter(jnp.dot(grad_gu_low, gate_up_matrix.T, preferred_element...  144 us
    reduce_scatter x2, waiting for transfers between devices, per_device(): lax.psum_scatter(jnp.dot(mixed_low, full_out, preferred_element_type=jnp....  138 us
    reduce_scatter x1, waiting for transfers between devices, per_device(): lax.psum_scatter(qkv_grad, 'dp', scatter_dimension=0, tiled=True)  96 us
    dot_general x48, matrix products, block_step(): output = jnp.einsum('hik,hvk->hiv', q_block, memory, precision=HIGHEST)  95.4 us
    dot_general x48, matrix products, block_step(): jnp.einsum('hik,hvk->hiv', weighted, memory, precision=HIGHEST)  86.1 us
    reduce_scatter x1, waiting for transfers between devices, per_device(): lax.psum_scatter(grad_down, 'dp', scatter_dimension=1, tiled=True)  84.3 us
  transfers between devices with their start and end apart: 26, of which 21 were waited for; matrix products, arithmetic and copies ran while one was open for 59% of the time, Pallas kernels for 0%

commit v1 on v0

v1 whole, which is shorter than its diff:
```python
import jax
import jax.numpy as jnp
from jax import lax
from jax.experimental import pallas as pl
from jax.experimental.pallas import tpu as pltpu
from jax.sharding import PartitionSpec as P

BLOCK = 64
NORM_EPS = 1e-06
HEAD_EPS = 1e-05
F32 = jnp.float32
BF16 = jnp.bfloat16
LANES = 128
HALO = 8


def low_dot(left, right, left_dim, right_dim):
    return lax.dot_general(
        left.astype(BF16),
        right.astype(BF16),
        (((left_dim,), (right_dim,)), ((), ())),
        preferred_element_type=F32,
    )


def sigmoid(value):
    return 1.0 / (1.0 + jnp.exp(-value))


def block_masks(rows):
    row = lax.broadcasted_iota(jnp.int32, (rows, rows), 0)
    col = lax.broadcasted_iota(jnp.int32, (rows, rows), 1)
    same = {size: (row // size) == (col // size) for size in (8, 16, 32, 64)}
    strict = jnp.logical_and(same[64], col < row)
    lower = jnp.logical_and(same[64], col <= row)
    eye = (row == col).astype(F32)
    return same, strict, lower, eye


def unit_inverse(system, same, eye):
    base = jnp.where(same[8], system, 0.0)
    square = low_dot(base, base, 1, 0)
    fourth = low_dot(square, square, 1, 0)
    inverse = eye - base
    inverse = inverse + low_dot(inverse, square, 1, 0)
    inverse = inverse + low_dot(inverse, fourth, 1, 0)
    for size in (8, 16, 32):
        off = jnp.where(jnp.logical_and(same[2 * size], jnp.logical_not(same[size])), system, 0.0)
        inverse = inverse - low_dot(inverse, low_dot(off, inverse, 1, 0), 1, 0)
    return inverse


def delayed_rows(previous, current, lag):
    if lag == 0:
        return current
    rows = current.shape[0]
    joined = jnp.concatenate([previous, current], axis=0)
    return joined[HALO - lag : HALO - lag + rows]


def conv_part(proj_ref, before_ref, conv_ref, reach, part, head, head_dim, heads):
    width = heads * head_dim
    column = part * width + head * head_dim
    current = proj_ref[:, column : column + head_dim]
    previous = before_ref[:, column : column + head_dim]
    taps = [conv_ref[part * 4 + lag : part * 4 + lag + 1, head * head_dim : (head + 1) * head_dim] for lag in range(4)]
    shifted = [current]
    for lag in range(1, 4):
        shifted.append(delayed_rows(previous, current, lag) * reach[lag])
    total = taps[0] * shifted[0]
    for lag in range(1, 4):
        total = total + taps[lag] * shifted[lag]
    return total, shifted, taps


def stack_heads(pieces, index):
    return jnp.concatenate([piece[index * BLOCK : (index + 1) * BLOCK] for piece in pieces], axis=0)


def forward_kernel(
    proj_ref, before_ref, logit_ref, pos_ref, valid_ref, conv_ref, gain_ref,
    mixed_ref, recall_ref, start_ref, inverse_ref, update_ref, weight_ref,
    state_ref, *, heads, head_dim,
):
    rows = proj_ref.shape[0]
    blocks = rows // BLOCK
    stacked = heads * BLOCK

    @pl.when(pl.program_id(0) == 0)
    def _():
        state_ref[...] = jnp.zeros_like(state_ref)

    pos = pos_ref[...]
    valid = valid_ref[...]
    reach = [None] + [(pos >= lag).astype(F32) for lag in range(1, 4)]
    parts = [[], [], []]
    strengths = []
    for head in range(heads):
        for part in range(3):
            total, _, _ = conv_part(proj_ref, before_ref, conv_ref, reach, part, head, head_dim, heads)
            value = total * sigmoid(total)
            if part < 2:
                scale = lax.rsqrt(jnp.sum(value * value, -1, keepdims=True) + NORM_EPS)
                if part == 0:
                    scale = scale * head_dim ** (-0.5)
                value = value * scale
            parts[part].append(value)
        strengths.append(sigmoid(logit_ref[:, head : head + 1]) * valid)
    same, strict, lower, eye = block_masks(stacked)
    local = []
    for index in range(blocks):
        queries = stack_heads(parts[0], index).astype(BF16)
        keys = stack_heads(parts[1], index)
        values = stack_heads(parts[2], index)
        strength = stack_heads(strengths, index)
        keys_low = keys.astype(BF16)
        gram = low_dot(keys_low, keys_low, 1, 1)
        system = jnp.where(strict, strength * gram, 0.0)
        inverse = unit_inverse(system, same, eye).astype(BF16)
        weighted = low_dot(inverse, strength * keys, 1, 0).astype(BF16)
        fresh = low_dot(inverse, strength * values, 1, 0)
        scores = jnp.where(lower, low_dot(queries, keys_low, 1, 1), 0.0).astype(BF16)
        inverse_ref[index] = inverse
        weight_ref[index] = weighted
        local.append((queries, keys_low, weighted, fresh, scores))
    for index in range(blocks):
        queries, keys_low, weighted, fresh, scores = local[index]
        keep = (pos[index * BLOCK : index * BLOCK + 1] != 0).astype(F32)
        updates = []
        carried = []
        for head in range(heads):
            span = slice(head * BLOCK, (head + 1) * BLOCK)
            state = state_ref[head] * keep
            state_low = state.astype(BF16)
            start_ref[index, head] = state_low
            update = fresh[span] - low_dot(weighted[span], state_low, 1, 1)
            update_low = update.astype(BF16)
            updates.append(update_low)
            carried.append(low_dot(queries[span], state_low, 1, 1))
            state_ref[head] = state + low_dot(update_low, keys_low[span], 0, 0)
        update_all = jnp.concatenate(updates, axis=0)
        update_ref[index] = update_all
        recall_all = jnp.concatenate(carried, axis=0) + low_dot(scores, update_all, 1, 0)
        scale = lax.rsqrt(jnp.mean(recall_all * recall_all, -1, keepdims=True) + HEAD_EPS)
        normed = recall_all * scale * gain_ref[...]
        here = slice(index * BLOCK, (index + 1) * BLOCK)
        for head in range(heads):
            span = slice(head * BLOCK, (head + 1) * BLOCK)
            column = slice(head * head_dim, (head + 1) * head_dim)
            recall_ref[here, column] = recall_all[span]
            mixed_ref[here, column] = (normed[span] * valid[here]).astype(BF16)


def backward_kernel(
    proj_ref, before_ref, logit_ref, pos_ref, after_ref, valid_ref, conv_ref, gain_ref,
    recall_ref, start_ref, inverse_ref, update_ref, weight_ref, mixed_grad_ref,
    proj_grad_ref, conv_grad_ref, gain_grad_ref,
    state_ref, halo_ref, *, heads, head_dim,
):
    rows = proj_ref.shape[0]
    blocks = rows // BLOCK
    stacked = heads * BLOCK
    width = heads * head_dim

    @pl.when(pl.program_id(0) == 0)
    def _():
        state_ref[...] = jnp.zeros_like(state_ref)
        halo_ref[...] = jnp.zeros_like(halo_ref)
        conv_grad_ref[...] = jnp.zeros_like(conv_grad_ref)
        gain_grad_ref[...] = jnp.zeros_like(gain_grad_ref)

    pos = pos_ref[...]
    valid = valid_ref[...]
    reach = [None] + [(pos >= lag).astype(F32) for lag in range(1, 4)]
    pos_ahead = jnp.concatenate([pos, after_ref[...]], axis=0)
    reach_ahead = [None] + [(pos_ahead >= lag).astype(F32) for lag in range(1, 4)]
    gain = gain_ref[...]
    parts = [[], [], []]
    gates = []
    recall_grads = []
    gain_grad = jnp.zeros((1, head_dim), F32)
    for head in range(heads):
        for part in range(3):
            total, _, _ = conv_part(proj_ref, before_ref, conv_ref, reach, part, head, head_dim, heads)
            value = total * sigmoid(total)
            if part < 2:
                scale = lax.rsqrt(jnp.sum(value * value, -1, keepdims=True) + NORM_EPS)
                if part == 0:
                    scale = scale * head_dim ** (-0.5)
                value = value * scale
            parts[part].append(value)
        gates.append(sigmoid(logit_ref[:, head : head + 1]))
        column = slice(head * head_dim, (head + 1) * head_dim)
        recall = recall_ref[:, column]
        pulled = mixed_grad_ref[:, column] * valid
        scale = lax.rsqrt(jnp.mean(recall * recall, -1, keepdims=True) + HEAD_EPS)
        normed = recall * scale
        gain_grad = gain_grad + jnp.sum(pulled * normed, 0, keepdims=True)
        pulled = pulled * gain
        recall_grads.append(
            scale * (pulled - normed * jnp.mean(normed * pulled, -1, keepdims=True))
        )
    gain_grad_ref[...] += gain_grad
    strengths = [gate * valid for gate in gates]
    same, strict, lower, eye = block_masks(stacked)
    query_grads = [None] * blocks
    key_grads = [None] * blocks
    value_grads = [None] * blocks
    strength_grads = [None] * blocks
    for index in range(blocks - 1, -1, -1):
        queries = stack_heads(parts[0], index).astype(BF16)
        keys = stack_heads(parts[1], index).astype(BF16)
        values = stack_heads(parts[2], index)
        strength = stack_heads(strengths, index)
        out_grad = stack_heads(recall_grads, index).astype(BF16)
        inverse = inverse_ref[index]
        weighted = weight_ref[index]
        update = update_ref[index]
        gram = low_dot(keys, keys, 1, 1)
        scores = jnp.where(lower, low_dot(queries, keys, 1, 1), 0.0).astype(BF16)
        local_grad = low_dot(scores, out_grad, 0, 0)
        score_grad = jnp.where(lower, low_dot(out_grad, update, 1, 1), 0.0).astype(BF16)
        keep = (pos[index * BLOCK : index * BLOCK + 1] != 0).astype(F32)
        update_grads = []
        query_carried = []
        key_carried = []
        misses = []
        starts = []
        for head in range(heads):
            span = slice(head * BLOCK, (head + 1) * BLOCK)
            ahead = state_ref[head]
            ahead_low = ahead.astype(BF16)
            start = start_ref[index, head]
            starts.append(start)
            update_grad = local_grad[span] + low_dot(keys[span], ahead_low, 1, 1)
            update_grad_low = update_grad.astype(BF16)
            update_grads.append(update_grad_low)
            carried = ahead + low_dot(out_grad[span], queries[span], 0, 0)
            carried = carried - low_dot(update_grad_low, weighted[span], 0, 0)
            state_ref[head] = carried * keep
            query_carried.append(low_dot(out_grad[span], start, 1, 0))
            key_carried.append(low_dot(update[span], ahead_low, 1, 0))
            misses.append(values[span] - low_dot(keys[span], start, 1, 1))
        miss_grad = low_dot(inverse, jnp.concatenate(update_grads, axis=0), 0, 0)
        miss = jnp.concatenate(misses, axis=0)
        system_grad = jnp.where(strict, -low_dot(miss_grad, update, 1, 1), 0.0)
        strength_grads[index] = jnp.sum(miss_grad * miss, -1, keepdims=True) + jnp.sum(
            system_grad * gram, -1, keepdims=True
        )
        gram_grad = (strength * system_grad).astype(BF16)
        value_grad = strength * miss_grad
        value_low = value_grad.astype(BF16)
        value_grads[index] = value_grad
        query_grads[index] = jnp.concatenate(query_carried, axis=0) + low_dot(score_grad, keys, 1, 0)
        key_grad = jnp.concatenate(key_carried, axis=0) + low_dot(score_grad, queries, 0, 0)
        key_grad = key_grad + low_dot(gram_grad, keys, 1, 0) + low_dot(gram_grad, keys, 0, 0)
        key_state = [
            low_dot(value_low[head * BLOCK : (head + 1) * BLOCK], starts[head], 1, 0)
            for head in range(heads)
        ]
        key_grads[index] = key_grad - jnp.concatenate(key_state, axis=0)
    grads = [query_grads, key_grads, value_grads]
    logit_grads = []
    for head in range(heads):
        span = slice(head * BLOCK, (head + 1) * BLOCK)
        gate = gates[head]
        pulled = jnp.concatenate([strength_grads[index][span] for index in range(blocks)], axis=0)
        logit_grads.append(pulled * valid * gate * (1.0 - gate))
        for part in range(3):
            pulled = jnp.concatenate([grads[part][index][span] for index in range(blocks)], axis=0)
            total, shifted, taps = conv_part(
                proj_ref, before_ref, conv_ref, reach, part, head, head_dim, heads
            )
            gate_part = sigmoid(total)
            value = total * gate_part
            if part < 2:
                scale = lax.rsqrt(jnp.sum(value * value, -1, keepdims=True) + NORM_EPS)
                normed = value * scale
                pulled = scale * (pulled - normed * jnp.sum(normed * pulled, -1, keepdims=True))
                if part == 0:
                    pulled = pulled * head_dim ** (-0.5)
            pre_grad = pulled * gate_part * (1.0 + total * (1.0 - gate_part))
            column = slice(part * width + head * head_dim, part * width + (head + 1) * head_dim)
            tap_column = slice(head * head_dim, (head + 1) * head_dim)
            for lag in range(4):
                conv_grad_ref[part * 4 + lag : part * 4 + lag + 1, tap_column] += jnp.sum(
                    pre_grad * shifted[lag], 0, keepdims=True
                )
            joined = jnp.concatenate([pre_grad, halo_ref[:, column]], axis=0)
            total_grad = taps[0] * pre_grad
            for lag in range(1, 4):
                total_grad = total_grad + taps[lag] * (joined * reach_ahead[lag])[lag : lag + rows]
            proj_grad_ref[:, column] = total_grad.astype(BF16)
            halo_ref[:, column] = pre_grad[:HALO]
    blank = jnp.zeros((rows, LANES - heads), F32)
    proj_grad_ref[:, 3 * width :] = jnp.concatenate(logit_grads + [blank], axis=1).astype(BF16)


def mixer_specs(rows, columns, order):
    blocks = rows // BLOCK
    ratio = rows // HALO

    def whole(*shape):
        return pl.BlockSpec(shape, lambda step: (0,) * len(shape))

    def by_rows(size, column=0):
        return pl.BlockSpec((rows, size), lambda step: (order(step), column))

    def by_blocks(*tail):
        return pl.BlockSpec((blocks,) + tail, lambda step: (order(step),) + (0,) * len(tail))

    before = pl.BlockSpec(
        (HALO, columns), lambda step: (jnp.maximum(order(step) * ratio - 1, 0), 0)
    )
    return whole, by_rows, by_blocks, before


def mixer_forward(projected, conv_rows, head_gain, pos, valid, heads):
    slots = projected.shape[0]
    head_dim = head_gain.shape[1]
    width = heads * head_dim
    columns = 3 * width
    rows = slots // lax.axis_size("tensor")
    steps = slots // rows
    stacked = heads * BLOCK
    block_count = slots // BLOCK
    whole, by_rows, by_blocks, before = mixer_specs(rows, columns, lambda step: step)
    return pl.pallas_call(
        lambda *refs: forward_kernel(*refs, heads=heads, head_dim=head_dim),
        grid=(steps,),
        in_specs=[
            by_rows(columns),
            before,
            by_rows(LANES, columns // LANES),
            by_rows(1),
            by_rows(1),
            whole(12, width),
            whole(1, head_dim),
        ],
        out_specs=[
            by_rows(width),
            by_rows(width),
            by_blocks(heads, head_dim, head_dim),
            by_blocks(stacked, stacked),
            by_blocks(stacked, head_dim),
            by_blocks(stacked, head_dim),
        ],
        scratch_shapes=[pltpu.VMEM((heads, head_dim, head_dim), F32)],
        out_shape=[
            jax.ShapeDtypeStruct((slots, width), BF16),
            jax.ShapeDtypeStruct((slots, width), F32),
            jax.ShapeDtypeStruct((block_count, heads, head_dim, head_dim), BF16),
            jax.ShapeDtypeStruct((block_count, stacked, stacked), BF16),
            jax.ShapeDtypeStruct((block_count, stacked, head_dim), BF16),
            jax.ShapeDtypeStruct((block_count, stacked, head_dim), BF16),
        ],
        name="mixer_forward",
    )(projected, projected, projected, pos, valid, conv_rows, head_gain)


def mixer_backward(projected, conv_rows, head_gain, pos, valid, heads, kept, mixed_grad):
    slots = projected.shape[0]
    head_dim = head_gain.shape[1]
    width = heads * head_dim
    columns = 3 * width
    rows = slots // lax.axis_size("tensor")
    steps = slots // rows
    stacked = heads * BLOCK
    ratio = rows // HALO
    recall, start, inverse, update, weighted = kept
    pos_padded = jnp.pad(pos, ((0, HALO), (0, 0)))
    whole, by_rows, by_blocks, before = mixer_specs(rows, columns, lambda step: steps - 1 - step)
    return pl.pallas_call(
        lambda *refs: backward_kernel(*refs, heads=heads, head_dim=head_dim),
        grid=(steps,),
        in_specs=[
            by_rows(columns),
            before,
            by_rows(LANES, columns // LANES),
            by_rows(1),
            pl.BlockSpec((HALO, 1), lambda step: ((steps - step) * ratio, 0)),
            by_rows(1),
            whole(12, width),
            whole(1, head_dim),
            by_rows(width),
            by_blocks(heads, head_dim, head_dim),
            by_blocks(stacked, stacked),
            by_blocks(stacked, head_dim),
            by_blocks(stacked, head_dim),
            by_rows(width),
        ],
        out_specs=[by_rows(columns + LANES), whole(12, width), whole(1, head_dim)],
        scratch_shapes=[
            pltpu.VMEM((heads, head_dim, head_dim), F32),
            pltpu.VMEM((HALO, columns), F32),
        ],
        out_shape=[
            jax.ShapeDtypeStruct((slots, columns + LANES), BF16),
            jax.ShapeDtypeStruct((12, width), F32),
            jax.ShapeDtypeStruct((1, head_dim), F32),
        ],
        name="mixer_backward",
    )(
        projected, projected, projected, pos, pos_padded, valid, conv_rows, head_gain,
        recall, start, inverse, update, weighted, mixed_grad,
    )


def doc_layout(length_pair, slot_count):
    first_end = (length_pair[0] + BLOCK - 1) // BLOCK * BLOCK
    second_end = first_end + (length_pair[1] + BLOCK - 1) // BLOCK * BLOCK
    places = jnp.arange(slot_count, dtype=jnp.int32)
    in_first = places < first_end
    in_second = jnp.logical_and(places >= first_end, places < second_end)
    doc_begin = jnp.where(in_first, 0, jnp.where(in_second, first_end, second_end))
    doc_limit = jnp.where(in_first, length_pair[0], jnp.where(in_second, length_pair[1], 0))
    offset = places - doc_begin
    is_valid = (offset < doc_limit).astype(F32)
    return offset.astype(F32)[:, None], is_valid[:, None]


def ring_shift(value, step):
    size = lax.axis_size("tensor")
    return lax.ppermute(value, "tensor", [(place, (place + step) % size) for place in range(size)])


def held(value, *others):
    return lax.optimization_barrier((value, others))[0]


def piece_start(step, count):
    size = lax.axis_size("tensor")
    return lax.rem(lax.axis_index("tensor") + step, size) * count


def gather_rows(rows, *token, mid=()):
    size = lax.axis_size("tensor")
    count = rows.shape[0]
    half = count // 2
    rows = held(rows, token)
    full = jnp.zeros((size * count, rows.shape[1]), rows.dtype)

    def put(full, piece, step, at=0):
        return lax.dynamic_update_slice(full, piece, (piece_start(step, count) + at, 0))

    full = put(full, rows, 0)
    from_left = rows
    from_right = rows
    for step in range(1, size // 2):
        from_left = ring_shift(from_left, 1)
        from_right = ring_shift(from_right, -1)
        full = put(full, from_left, size - step)
        full = put(full, from_right, step)
    from_left_half, from_right_half = from_left[:half], from_right[half:]
    if mid:
        from_left_half, from_right_half = held((from_left_half, from_right_half), mid)
    far = ring_shift(from_left_half, 1), ring_shift(from_right_half, -1)
    full = put(full, far[0], size // 2)
    full = put(full, far[1], size // 2, half)
    return full, (from_left, from_right), far


def scatter_rows(partial, *token, mid=()):
    size = lax.axis_size("tensor")
    count = partial.shape[0] // size
    half = count // 2
    low = held(partial, token)

    def take(step, at=0, length=count):
        start = piece_start(step, count) + at
        return lax.dynamic_slice(low, (start, 0), (length, low.shape[1])).astype(F32)

    to_right = ring_shift(take(size // 2, 0, half).astype(BF16), 1)
    to_left = ring_shift(take(size // 2, half, half).astype(BF16), -1)
    first = to_right, to_left
    if mid:
        to_right, to_left = held(first, mid)
    for step in range(size // 2 - 1, 0, -1):
        right = take(step)
        left = take(size - step)
        if step == size // 2 - 1:
            right = joined([right[:half] + to_right.astype(F32), right[half:]])
            left = joined([left[:half], left[half:] + to_left.astype(F32)])
        else:
            right = right + to_right.astype(F32)
            left = left + to_left.astype(F32)
        to_right = ring_shift(right.astype(BF16), 1)
        to_left = ring_shift(left.astype(BF16), -1)
    total = take(0) + to_right.astype(F32) + to_left.astype(F32)
    return total, first, (to_right, to_left)


def dot(left, right, left_dim, right_dim, out_type=F32):
    return lax.dot_general(
        left, right, (((left_dim,), (right_dim,)), ((), ())), preferred_element_type=out_type
    )


def gather_dp(value):
    return lax.all_gather(value, "dp", axis=0, tiled=True)


def scatter_dp(value):
    return lax.psum_scatter(value, "dp", scatter_dimension=0, tiled=True)


def row_scale(values):
    return lax.rsqrt(jnp.mean(values * values, -1, keepdims=True) + NORM_EPS)


def norm_pull(values, pulled):
    scale = row_scale(values)
    normed = values * scale
    return scale * (pulled - normed * jnp.mean(normed * pulled, -1, keepdims=True))


def joined(parts):
    return jnp.concatenate(parts, axis=0)


def per_device(
    tokens, cotangent, doc_lengths, attn_gain, w_qkv, w_beta, conv_weight, head_gain,
    w_out, ffn_gain, w_gate_up, w_down,
):
    batches, local_rows, width = tokens.shape
    size = lax.axis_size("tensor")
    dp_size = lax.axis_size("dp")
    slots = local_rows * size
    shard = w_qkv.shape[0]
    heads = w_beta.shape[1]
    units = w_down.shape[0]
    head_share = head_gain.shape[0]
    head_dim = head_share * dp_size
    columns = 3 * heads * head_dim
    conv_share = 12 * heads * head_share
    small_share = conv_share + head_share
    extra = -(-small_share // shard)
    small_at = columns + heads

    attn_column = attn_gain.astype(F32)[:, None]
    ffn_column = ffn_gain.astype(F32)[:, None]
    qkv_rows = jnp.concatenate([w_qkv.reshape(shard, columns), w_beta], axis=1).astype(F32)
    small = jnp.concatenate(
        [conv_weight.reshape(-1), head_gain, jnp.zeros((extra * shard - small_share,), BF16)]
    ).reshape(shard, extra)
    blank = jnp.zeros((shard, LANES - heads - extra), BF16)
    full_proj = gather_dp(
        jnp.concatenate([(attn_column * qkv_rows).astype(BF16), small, blank], axis=1)
    )
    full_out = gather_dp(w_out.T)
    gate_up_rows = w_gate_up.reshape(shard, 2 * units).astype(F32)
    full_gate_up = gather_dp((ffn_column * gate_up_rows).astype(BF16))
    full_down = gather_dp(w_down.T)
    small = full_proj[:, small_at : small_at + extra].astype(F32).reshape(dp_size, extra * shard)
    full_conv = small[:, :conv_share].reshape(dp_size, 12, heads, head_share)
    full_conv = jnp.transpose(full_conv, (1, 2, 0, 3)).reshape(12, heads * head_dim)
    full_head_gain = small[:, conv_share:small_share].reshape(1, head_dim)

    rows = [tokens[index].astype(F32) for index in range(batches)]
    layouts = [doc_layout(doc_lengths[index, 0], slots) for index in range(batches)]

    def mix(index, projected):
        mixed, *kept = mixer_forward(
            projected, full_conv, full_head_gain, *layouts[index], heads
        )
        return mixed, kept, dot(mixed, full_out, 1, 1, BF16)

    def after_mixer(index, branch):
        hidden = rows[index] + branch
        return hidden, (hidden * row_scale(hidden)).astype(BF16)

    def feed(ffn_full):
        gate_up = dot(ffn_full, full_gate_up, 1, 0)
        gate = gate_up[:, :units]
        activated = (gate * sigmoid(gate) * gate_up[:, units:]).astype(BF16)
        return gate_up, activated

    def feed_back(gate_up, cot_full):
        grad_act = dot(cot_full, full_down, 1, 0)
        gate = gate_up[:, :units]
        up = gate_up[:, units:]
        opened = sigmoid(gate)
        grad_gate = grad_act * up * opened * (1.0 + gate * (1.0 - opened))
        grad_up = grad_act * (gate * opened)
        grad_gate_up = jnp.concatenate([grad_gate, grad_up], axis=1).astype(BF16)
        return grad_gate_up, dot(grad_gate_up, full_gate_up, 1, 1, BF16)

    def before_ffn(index, hidden, pulled):
        return cotangent[index].astype(F32) + norm_pull(hidden, pulled)

    def mix_back(index, grad_mixed, projected, kept):
        grad_proj, conv_grad, gain_grad = mixer_backward(
            projected, full_conv, full_head_gain, *layouts[index], heads, kept, grad_mixed
        )
        return grad_proj, conv_grad, gain_grad, dot(grad_proj, full_proj, 1, 1, BF16)

    attn_in = [(rows[index] * row_scale(rows[index])).astype(BF16) for index in range(batches)]
    attn_0, first, last = gather_rows(attn_in[0])
    attn_1, first, last = gather_rows(attn_in[1], last)
    proj_0 = dot(held(attn_0, first), full_proj, 1, 0)
    cot_0, cot_first, last = gather_rows(cotangent[0], first, proj_0)
    mixed_0, kept_0, part_0 = mix(0, held(proj_0, attn_1))

    proj_1 = dot(held(attn_1, part_0), full_proj, 1, 0)
    branch, first, last = scatter_rows(part_0, mid=(proj_1,))
    cot_1, cot_first, cot_last = gather_rows(cotangent[1], first, cot_first)
    mixed_1, kept_1, part_1 = mix(1, held(proj_1, first, cot_0))
    hidden_0, ffn_in = after_mixer(0, branch)

    ffn_0, first, last = gather_rows(ffn_in, cot_first, part_1, full_gate_up)
    gate_up_0, act_0 = feed(ffn_0)
    branch, first, last = scatter_rows(part_1, first, mid=(gate_up_0, full_down))
    grad_gate_up_0, part_0 = feed_back(gate_up_0, cot_0)
    hidden_1, ffn_in = after_mixer(1, branch)

    ffn_1, ffn_first, last = gather_rows(ffn_in, part_0)
    pulled, first, last = scatter_rows(part_0, ffn_first)
    down_0 = dot(held(act_0, ffn_first), full_down, 1, 1, BF16)
    down_grad = dot(held(cot_0, down_0), act_0, 0, 0, BF16)
    gate_up_grad = dot(held(ffn_0, down_grad), grad_gate_up_0, 0, 0, BF16)
    gate_up_1, act_1 = feed(held(ffn_1, first, gate_up_grad))
    grad_gate_up_1, part_1 = feed_back(gate_up_1, cot_1)
    grad_hidden_0 = before_ffn(0, hidden_0, pulled)

    branch_0, first, last = gather_rows(grad_hidden_0.astype(BF16))
    act_1_held = held(act_1, part_1, first)
    down_1 = dot(act_1_held, full_down, 1, 1, BF16)
    down_grad = (down_grad + dot(cot_1, act_1_held, 0, 0)).astype(BF16)
    gate_up_grad = gate_up_grad + dot(held(ffn_1, down_1, down_grad), grad_gate_up_1, 0, 0)
    gate_up_grad = gate_up_grad.astype(BF16)
    pulled, first, last = scatter_rows(part_1, first, mid=(gate_up_grad,))
    grad_hidden_1 = before_ffn(1, hidden_1, pulled)
    down_grad = scatter_dp(down_grad)

    branch_in = held(grad_hidden_1.astype(BF16), gate_up_grad)
    branch_1, first, last = gather_rows(branch_in)
    gate_up_grad = scatter_dp(gate_up_grad)
    grad_mixed = dot(held(branch_0, branch_in), full_out, 1, 0)
    grad_proj_0, conv_grad_0, gain_grad_0, part_0 = mix_back(0, grad_mixed, proj_0, kept_0)
    lower_0, down_first, down_last = scatter_rows(down_0, branch_in, mid=(part_0,))

    pulled, first, last = scatter_rows(part_0, last)
    out_grad = dot(
        joined([held(branch_0, part_0), branch_1]), joined([mixed_0, mixed_1]), 0, 0, BF16
    )
    grad_mixed = dot(held(branch_1, part_0), full_out, 1, 0)
    input_rows_0 = grad_hidden_0 + norm_pull(rows[0], pulled)
    grad_mixed = held(grad_mixed, first, down_first, out_grad)
    grad_proj_1, conv_grad_1, gain_grad_1, part_1 = mix_back(1, grad_mixed, proj_1, kept_1)

    attn_all = joined([held(attn_0, part_1, last, down_last), attn_1])
    pulled, first, last = scatter_rows(part_1, last, down_last, down_grad)
    proj_grad = dot(attn_all, joined([grad_proj_0, grad_proj_1]), 0, 0, BF16)
    conv_grad = (conv_grad_0 + conv_grad_1).reshape(12, heads, dp_size, head_share)
    conv_grad = jnp.transpose(conv_grad, (2, 0, 1, 3)).reshape(dp_size, conv_share)
    head_gain_grad = (gain_grad_0 + gain_grad_1).reshape(dp_size, head_share)
    small_grad = jnp.concatenate(
        [conv_grad, head_gain_grad, jnp.zeros((dp_size, extra * shard - small_share), F32)], axis=1
    )
    small_grad = small_grad.reshape(dp_size * shard, extra).astype(BF16)
    small_grad = jnp.pad(small_grad, ((0, 0), (small_at, LANES - heads - extra)))
    mixer_grad = scatter_dp(jnp.concatenate([proj_grad + small_grad, out_grad], axis=1))
    lower_1, first, last = scatter_rows(down_1, last, gate_up_grad)
    mixer_grad = held(mixer_grad, last)
    input_rows_1 = grad_hidden_1 + norm_pull(rows[1], pulled)
    layer_rows_0 = (hidden_0 + lower_0).astype(BF16)
    layer_rows_1 = (hidden_1 + lower_1).astype(BF16)

    proj_grad = mixer_grad[:, : columns + LANES].astype(F32)
    out_grad = mixer_grad[:, columns + LANES :]
    gate_up_grad = gate_up_grad.astype(F32)
    small_grad = proj_grad[:, small_at : small_at + extra].reshape(extra * shard)
    gain_grads = jnp.concatenate(
        [
            jnp.sum(proj_grad[:, :small_at] * qkv_rows, axis=1),
            jnp.sum(gate_up_grad * gate_up_rows, axis=1),
            small_grad[conv_share:small_share],
        ]
    )[None]
    total = gain_grads
    for step in range(1, size):
        total = total + ring_shift(gain_grads, step)
    total = total[0]
    proj_grad = proj_grad[:, :small_at] * attn_column
    return (
        jnp.stack([layer_rows_0, layer_rows_1]),
        jnp.stack([input_rows_0, input_rows_1]),
        total[:shard],
        proj_grad[:, :columns].reshape(shard, 3, -1),
        proj_grad[:, columns:],
        small_grad[:conv_share].reshape(3, 4, heads, head_share),
        total[2 * shard :],
        out_grad.T.astype(F32),
        total[shard : 2 * shard],
        (gate_up_grad * ffn_column).reshape(shard, 2, units),
        down_grad.T.astype(F32),
    )


def solution(mesh):
    return jax.shard_map(
        per_device,
        mesh=mesh,
        in_specs=(
            P(None, ("dp", "tensor"), None),
            P(None, ("dp", "tensor"), None),
            P(None, "dp", None),
            P("dp"),
            P("dp", None, "tensor"),
            P("dp", "tensor"),
            P(None, None, "tensor", "dp"),
            P("dp"),
            P("tensor", "dp"),
            P("dp"),
            P("dp", None, "tensor"),
            P("tensor", "dp"),
        ),
        out_specs=(
            P(None, ("dp", "tensor"), None),
            P(None, ("dp", "tensor"), None),
            P("dp"),
            P("dp", None, "tensor"),
            P("dp", "tensor"),
            P(None, None, "tensor", "dp"),
            P("dp"),
            P("tensor", "dp"),
            P("dp"),
            P("dp", None, "tensor"),
            P("tensor", "dp"),
        ),
        check_vma=False,
    )
```

time: 2920 us -> 780 us (0.27)
  other arithmetic: 809 us -> 56.2 us
  waiting for transfers between devices: 983 us -> 234 us
  matrix products: 698 us -> 170 us
  local copies, waits for them, and re-layouts: 301 us -> 79.3 us
  starting transfers between devices: 2.29 us -> 120 us
  Pallas kernels: 0 us -> 94.3 us
  blocking collectives: 87.4 us -> 0 us
    another operation x134 -> x15, other arithmetic: 655 us -> 16.9 us  [the longest x64 331 us: block_step(): jax.scipy.linalg.solve_triangular(system, b_block[:, :, None] * k_block,...]
    reduce_scatter x11 -> x3, waiting for transfers between devices: 633 us -> 0.06 us  [scatter_dp(): return lax.psum_scatter(value, 'dp', scatter_dimension=0, tiled=True)]
    dot_general x344 -> x22, matrix products: 601 us -> 170 us  [dot(): lax.dot_general(left, right, (((left_dim,), (right_dim,)), ((), ())), pre...]
    all_gather x12 -> x4, waiting for transfers between devices: 348 us -> 0.03 us  [gather_dp(): return lax.all_gather(value, 'dp', axis=0, tiled=True)]
    ppermute x0 -> x67, waiting for transfers between devices: none -> 233 us  [ring_shift(): lax.ppermute(value, 'tensor', [(place, (place + step) % size) for place i...]
    ppermute x0 -> x67, starting transfers between devices: none -> 120 us  [ring_shift(): lax.ppermute(value, 'tensor', [(place, (place + step) % size) for place i...]
    another operation x96 -> x0, matrix products: 97.5 us -> none  [the longest x48 68.4 us: block_step(): jax.scipy.linalg.solve_triangular(system, b_block[:, :, None] * v_block,...]
    pallas_call x0 -> x4, Pallas kernels: none -> 94.3 us  [the longest x2 49.2 us: mixer_forward(): pl.pallas_call(lambda *refs: forward_kernel(*refs, heads=heads, head_dim=...]
  transfers between devices with their start and end apart: 26 -> 74, of which waited for: 21 -> 36; matrix products, arithmetic and copies ran while one was open for 59% -> 35% of each run, Pallas kernels for 0% -> 12%
where the time goes in v1:
time: 780 us; the launch traced here: 773 us
  waiting for transfers between devices  234 us (30%)
  matrix products  170 us (22%)
  starting transfers between devices  120 us (15%)
  Pallas kernels  94.3 us (12%)
  local copies, waits for them, and re-layouts  79.3 us (10%)
  other arithmetic  56.2 us (7%)
  between operations  18.8 us (2%)
    ppermute x67, waiting for transfers between devices, ring_shift(): lax.ppermute(value, 'tensor', [(place, (place + step) % size) for place i...  233 us
    dot_general x22, matrix products, dot(): lax.dot_general(left, right, (((left_dim,), (right_dim,)), ((), ())), pre...  170 us
    ppermute x67, starting transfers between devices, ring_shift(): lax.ppermute(value, 'tensor', [(place, (place + step) % size) for place i...  120 us
    pallas_call x2, Pallas kernels, mixer_forward(): pl.pallas_call(lambda *refs: forward_kernel(*refs, heads=heads, head_dim=...  49.2 us
    pallas_call x2, Pallas kernels, mixer_backward(): pl.pallas_call(lambda *refs: backward_kernel(*refs, heads=heads, head_dim...  45.1 us
    dynamic_update_slice x40, local copies, waits for them, and re-layouts, put(): lax.dynamic_update_slice(full, piece, (piece_start(step, count) + at, 0))  24.9 us
  transfers between devices with their start and end apart: 74, of which 36 were waited for; matrix products, arithmetic and copies ran while one was open for 35% of the time, Pallas kernels for 12%

profile of v1, /device:TPU:0, one launch (start us, length us, event | category | flops | bytes accessed | tf_op | source)
XLA Modules:
  0.0 772.8 jit_solution(6502358186089912767)
XLA Ops:
  41.5 9.0 %collective-permute-done.1 = bf16[128,2048]{1,0:T(8,128)(2,1)} collective-permute-done((bf16[128,2048]{1,0:T(8,128)(2,1)S(1)}, bf16[128,2048]{1,0:T(8,128)(2,1)}, u32[]{:S(2)}, u32[]{:S(2)}) %collective-permute-start.1) | collective-permute-done | bytes 524320 | tf_op jit(solution)/shard_map/ppermute | solution.py:424
  70.1 8.9 %collective-permute-done.4 = bf16[128,2048]{1,0:T(8,128)(2,1)S(1)} collective-permute-done((bf16[128,2048]{1,0:T(8,128)(2,1)S(1)}, bf16[128,2048]{1,0:T(8,128)(2,1)S(1)}, u32[]{:S(2)}, u32[]{:S(2)}) %collective-permute-start.4) | collective-permute-done | bytes 524320 | tf_op jit(solution)/shard_map/ppermute | solution.py:424
  79.1 10.1 %collective-permute-done.5 = bf16[128,2048]{1,0:T(8,128)(2,1)S(1)} collective-permute-done((bf16[128,2048]{1,0:T(8,128)(2,1)S(1)}, bf16[128,2048]{1,0:T(8,128)(2,1)S(1)}, u32[]{:S(2)}, u32[]{:S(2)}) %collective-permute-start.5) | collective-permute-done | bytes 524320 | tf_op jit(solution)/shard_map/ppermute | solution.py:424
  100.8 9.4 %fusion.58.refs_0_.refs_1_.refs_2_ = f32[512,1664]{1,0:T(8,128)} fusion(bf16[512,2048]{1,0:T(8,128)(2,1)} %constant_dynamic-update-slice_fusion.35, bf16[2048,1664]{0,1:T(8,128)(2,1)} %all-gather.5.cloned.1.call-done), kind=kOutput, calls=%fused_computation.238 | convolution fusion | flops 3489660928 | bytes 12320768 | tf_op jit(solution)/shard_map/dot_general | solution.py:494
  117.6 24.6 %mixer_forward.2 = (bf16[512,512]{1,0:T(8,128)(2,1)}, f32[512,512]{1,0:T(8,128)}, bf16[8,4,128,128]{3,2,1,0:T(8,128)(2,1)}, bf16[8,256,256]{2,1,0:T(8,128)(2,1)}...) custom-call(f32[512,1664]{1,0:T(8,128)} %fusion.58.refs_0_.refs_1_.refs_2_, ...), custom_call_target="tpu_custom_call" | custom-call | tf_op jit(solution)/shard_map/mixer_forward/pallas_call | solution.py:328
  149.3 9.2 %fusion.60.refs_0_.refs_1_.refs_2_ = f32[512,1664]{1,0:T(8,128)} fusion(bf16[512,2048]{1,0:T(8,128)(2,1)} %constant_dynamic-update-slice_fusion.30, bf16[2048,1664]{0,1:T(8,128)(2,1)} %all-gather.5.cloned.1.call-done), kind=kOutput, calls=%fused_computation.240 | convolution fusion | flops 3489660928 | bytes 12320768 | tf_op jit(solution)/shard_map/dot_general | solution.py:494
  176.7 30.2 %collective-permute-done.16 = bf16[64,2048]{1,0:T(8,128)(2,1)S(1)} collective-permute-done((bf16[64,2048]{1,0:T(8,128)(2,1)S(1)}, bf16[64,2048]{1,0:T(8,128)(2,1)S(1)}, u32[]{:S(2)}, u32[]{:S(2)}) %collective-permute-start.16) | collective-permute-done | bytes 262176 | tf_op jit(solution)/shard_map/ppermute | solution.py:424
  211.1 24.6 %mixer_forward.3 = (bf16[512,512]{1,0:T(8,128)(2,1)}, f32[512,512]{1,0:T(8,128)}, bf16[8,4,128,128]{3,2,1,0:T(8,128)(2,1)}, bf16[8,256,256]{2,1,0:T(8,128)(2,1)}...) custom-call(f32[512,1664]{1,0:T(8,128)} %fusion.60.refs_0_.refs_1_.refs_2_, ...), custom_call_target="tpu_custom_call" | custom-call | tf_op jit(solution)/shard_map/mixer_forward/pallas_call | solution.py:328
  255.5 14.6 %collective-permute-done.18 = bf16[128,2048]{1,0:T(8,128)(2,1)S(1)} collective-permute-done((bf16[128,2048]{1,0:T(8,128)(2,1)S(1)}, bf16[128,2048]{1,0:T(8,128)(2,1)S(1)}, u32[]{:S(2)}, u32[]{:S(2)}) %collective-permute-start.18) | collective-permute-done | bytes 524320 | tf_op jit(solution)/shard_map/ppermute | solution.py:424
  270.2 10.8 %collective-permute-done.19 = bf16[128,2048]{1,0:T(8,128)(2,1)S(1)} collective-permute-done((bf16[128,2048]{1,0:T(8,128)(2,1)S(1)}, bf16[128,2048]{1,0:T(8,128)(2,1)S(1)}, u32[]{:S(2)}, u32[]{:S(2)}) %collective-permute-start.19) | collective-permute-done | bytes 524320 | tf_op jit(solution)/shard_map/ppermute | solution.py:424
  287.0 8.9 %collective-permute-done.21 = bf16[64,2048]{1,0:T(8,128)(2,1)S(1)} collective-permute-done((bf16[64,2048]{1,0:T(8,128)(2,1)S(1)}, bf16[64,2048]{1,0:T(8,128)(2,1)S(1)}, u32[]{:S(2)}, u32[]{:S(2)}) %collective-permute-start.21) | collective-permute-done | bytes 262176 | tf_op jit(solution)/shard_map/ppermute | solution.py:424
  297.2 11.1 %fusion.62 = f32[512,2816]{1,0:T(8,128)} fusion(bf16[512,2048]{1,0:T(8,128)(2,1)S(1)} %constant_dynamic-update-slice_fusion.20, bf16[2048,2816]{1,0:T(8,128)(2,1)} %all-gather.9.cloned.1.call-done), kind=kOutput, calls=%fused_computation.242 | convolution fusion | flops 5905580032 | bytes 19398656 | tf_op jit(solution)/shard_map/dot_general | solution.py:494
  314.2 10.4 %multiply_convert_fusion.4 = (bf16[512,1408]{1,0:T(8,128)(2,1)S(1)}, bf16[512,1408]{1,0:T(8,128)(2,1)S(1)}, bf16[512,1408]{1,0:T(8,128)(2,1)}) fusion(f32[512,2816]{1,0:T(8,128)} %fusion.62, bf16[512,2048]{1,0:T(8,128)(2,1)} %constant_dynamic-update-slice_fusion.25, bf16[2048,1408]{0,1:T(8,128)(2,1)} %all-gather.11.cloned.1.call-done), kind=kOutput, calls=%fused_computation.25 | convolution fusion | flops 2963603456 | bytes 17956864 | tf_op jit(solution)/shard_map/dot_general | solution.py:494
  340.3 9.1 %collective-permute-done.26 = bf16[128,2048]{1,0:T(8,128)(2,1)S(1)} collective-permute-done((bf16[128,2048]{1,0:T(8,128)(2,1)S(1)}, bf16[128,2048]{1,0:T(8,128)(2,1)S(1)}, u32[]{:S(2)}, u32[]{:S(2)}) %collective-permute-start.26) | collective-permute-done | bytes 524320 | tf_op jit(solution)/shard_map/ppermute | solution.py:424
  376.1 10.8 %fusion.14 = bf16[2048,2816]{1,0:T(8,128)(2,1)} fusion(bf16[512,2048]{1,0:T(8,128)(2,1)S(1)} %copy-done.21, bf16[512,1408]{1,0:T(8,128)(2,1)} %copy-done.63, bf16[512,1408]{1,0:T(8,128)(2,1)} %copy-done.62), kind=kOutput, calls=%fused_computation.34 | convolution fusion | flops 5911347200 | bytes 16515072 | tf_op jit(solution)/shard_map/dot_general | solution.py:494
  398.0 10.5 %collective-permute-done.31 = bf16[64,2048]{1,0:T(8,128)(2,1)S(1)} collective-permute-done((bf16[64,2048]{1,0:T(8,128)(2,1)S(1)}, bf16[64,2048]{1,0:T(8,128)(2,1)S(1)}, u32[]{:S(2)}, u32[]{:S(2)}) %collective-permute-start.31) | collective-permute-done | bytes 262176 | tf_op jit(solution)/shard_map/ppermute | solution.py:424
  416.5 11.6 %multiply_convert_fusion.2 = (bf16[512,1408]{1,0:T(8,128)(2,1)}, bf16[512,1408]{1,0:T(8,128)(2,1)}, bf16[512,1408]{1,0:T(8,128)(2,1)}) fusion(f32[512,2816]{1,0:T(8,128)} %fusion.65, bf16[512,2048]{1,0:T(8,128)(2,1)} %constant_dynamic-update-slice_fusion.15, bf16[2048,1408]{0,1:T(8,128)(2,1)} %all-gather.11.cloned.1.call-done), kind=kOutput, calls=%fused_computation.21 | convolution fusion | flops 2963603456 | bytes 17956864 | tf_op jit(solution)/shard_map/dot_general | solution.py:494
  464.0 12.4 %add_convert_fusion = bf16[2048,2816]{1,0:T(8,128)(2,1)} fusion(bf16[2048,2816]{1,0:T(8,128)(2,1)} %fusion.14, bf16[512,2048]{1,0:T(8,128)(2,1)S(1)} %copy-done.23, bf16[512,1408]{1,0:T(8,128)(2,1)S(1)} %copy-done.65, bf16[512,1408]{1,0:T(8,128)(2,1)S(1)} %copy-done.64), kind=kOutput, calls=%fused_computation | convolution fusion | flops 5928648704 | bytes 28049408 | tf_op jit(solution)/shard_map/dot_general | solution.py:494
  490.0 11.8 %collective-permute-done.39 = bf16[64,2048]{1,0:T(8,128)(2,1)S(1)} collective-permute-done((bf16[64,2048]{1,0:T(8,128)(2,1)S(1)}, bf16[64,2048]{1,0:T(8,128)(2,1)S(1)}, u32[]{:S(2)}, u32[]{:S(2)}) %collective-permute-start.39) | collective-permute-done | bytes 262176 | tf_op jit(solution)/shard_map/ppermute | solution.py:424
  536.5 22.6 %mixer_backward.2 = (bf16[512,1664]{1,0:T(8,128)(2,1)}, f32[12,512]{1,0:T(8,128)}, f32[1,128]{1,0:T(1,128)}) custom-call(f32[512,1664]{1,0:T(8,128)} %fusion.58.refs_0_.refs_1_.refs_2_, f32[512,1664]{1,0:T(8,128)} %fusion.58.refs_0_.refs_1_.refs_2_, f32[512,1664]{1,0:T(8,128)} %fusion.58.refs_0_.refs_1_.refs_2_, f32[512,1]{1,0:T(8,128)} %fusion.42.refs_3_, ...), custom_call_target="tpu_custom_call" | custom-call | tf_op jit(solution)/shard_map/mixer_backward/pallas_call | solution.py:373
  579.0 17.0 %collective-permute-done.50 = bf16[64,2048]{1,0:T(8,128)(2,1)S(1)} collective-permute-done((bf16[64,2048]{1,0:T(8,128)(2,1)S(1)}, bf16[64,2048]{1,0:T(8,128)(2,1)S(1)}, u32[]{:S(2)}, u32[]{:S(2)}) %collective-permute-start.50) | collective-permute-done | bytes 262176 | tf_op jit(solution)/shard_map/ppermute | solution.py:424
  595.9 9.0 %collective-permute-done.51 = bf16[64,2048]{1,0:T(8,128)(2,1)S(1)} collective-permute-done((bf16[64,2048]{1,0:T(8,128)(2,1)S(1)}, bf16[64,2048]{1,0:T(8,128)(2,1)S(1)}, u32[]{:S(2)}, u32[]{:S(2)}) %collective-permute-start.51) | collective-permute-done | bytes 262176 | tf_op jit(solution)/shard_map/ppermute | solution.py:424
  622.9 22.5 %mixer_backward.3 = (bf16[512,1664]{1,0:T(8,128)(2,1)}, f32[12,512]{1,0:T(8,128)}, f32[1,128]{1,0:T(1,128)}) custom-call(f32[512,1664]{1,0:T(8,128)} %fusion.60.refs_0_.refs_1_.refs_2_, f32[512,1664]{1,0:T(8,128)} %fusion.60.refs_0_.refs_1_.refs_2_, f32[512,1664]{1,0:T(8,128)} %fusion.60.refs_0_.refs_1_.refs_2_, f32[512,1]{1,0:T(8,128)} %fusion.41.refs_3_, ...), custom_call_target="tpu_custom_call" | custom-call | tf_op jit(solution)/shard_map/mixer_backward/pallas_call | solution.py:373
  657.5 9.8 %pad_add_fusion = bf16[2048,1664]{0,1:T(8,128)(2,1)S(1)} fusion(bf16[2048,4]{0,1:T(4,128)(2,1)S(1)} %copy.33, bf16[512,2048]{1,0:T(8,128)(2,1)} %constant_dynamic-update-slice_fusion.30, bf16[512,2048]{1,0:T(8,128)(2,1)} %constant_dynamic-update-slice_fusion.35, bf16[512,1664]{1,0:T(8,128)(2,1)S(1)} %copy-done.55, bf16[512,1664]{1,0:T(8,128)(2,1)S(1)} %copy-done.54), kind=kOutput, calls=%fused_computation.3 | convolution fusion | flops 7008157696 | bytes 14434304 | tf_op jit(solution)/shard_map/dot_general | solution.py:494
  (481 shorter events, 425.1 us)
Async XLA Ops:
  7.2 93.6 %all-gather.5.cloned.1.call-start = ((), (), s32[]{:S(2)}) async-start(), calls=%async_computation.3 | async-start | bytes 7667712 | tf_op jit(solution)/shard_map/all_gather | solution.py:500
  17.4 124.9 %all-gather.7.cloned.1.call-start = ((), (), s32[]{:S(2)}) async-start(), calls=%async_computation.4 | async-start | bytes 2359296 | tf_op jit(solution)/shard_map/all_gather | solution.py:500
  18.1 229.5 %all-gather.9.cloned.1.call-start = ((), (), s32[]{:S(2)}) async-start(), calls=%async_computation.5 | async-start | bytes 12976128 | tf_op jit(solution)/shard_map/all_gather | solution.py:500
  21.8 286.6 %all-gather.11.cloned.1.call-start = ((), (), s32[]{:S(2)}) async-start(), calls=%async_computation.6 | async-start | bytes 6488064 | tf_op jit(solution)/shard_map/all_gather | solution.py:500
  27.6 643.9 %reduce-scatter.4.cloned.1.call-start = ((), (), s32[]{:S(2)}) async-start(), calls=%async_computation.7 | async-start | bytes 6488064 | tf_op jit(solution)/shard_map/reduce_scatter | solution.py:504
  110.2 56.4 %collective-permute-start.12 = (bf16[128,2048]{1,0:T(8,128)(2,1)S(1)}, bf16[128,2048]{1,0:T(8,128)(2,1)S(1)}, u32[]{:S(2)}, u32[]{:S(2)}) collective-permute-start(bf16[128,2048]{1,0:T(8,128)(2,1)S(1)} %copy-done.30), channel_id=1, source_target_pairs={{0,1},{1,2},{2,3},{3,0},{4,5},{5,6},{6,7},{7,4},{8,9},{9,10},{10,1... | collective-permute-start | bytes 1572872 | tf_op jit(solution)/shard_map/ppermute | solution.py:424
  110.5 56.1 %collective-permute-start.13 = (bf16[128,2048]{1,0:T(8,128)(2,1)S(1)}, bf16[128,2048]{1,0:T(8,128)(2,1)}, u32[]{:S(2)}, u32[]{:S(2)}) collective-permute-start(bf16[128,2048]{1,0:T(8,128)(2,1)S(1)} %copy-done.30), channel_id=1, source_target_pairs={{0,3},{1,0},{2,1},{3,2},{4,7},{5,4},{6,5},{7,6},{8,11},{9,8},{10,9... | collective-permute-start | bytes 1572872 | tf_op jit(solution)/shard_map/ppermute | solution.py:424
  161.9 73.8 %collective-permute-start.10 = (bf16[128,2048]{1,0:T(8,128)(2,1)}, bf16[128,2048]{1,0:T(8,128)(2,1)}, u32[]{:S(2)}, u32[]{:S(2)}) collective-permute-start(bf16[128,2048]{1,0:T(8,128)(2,1)} %pad_maximum_fusion.10), channel_id=1, source_target_pairs={{0,1},{1,2},{2,3},{3,0},{4,5},{5,6},{6,7},{7,4},{8,9},{9,10},{10,1... | collective-permute-start | bytes 1572872 | tf_op jit(solution)/shard_map/ppermute | solution.py:424
  162.7 73.0 %collective-permute-start.11 = (bf16[128,2048]{1,0:T(8,128)(2,1)}, bf16[128,2048]{1,0:T(8,128)(2,1)S(1)}, u32[]{:S(2)}, u32[]{:S(2)}) collective-permute-start(bf16[128,2048]{1,0:T(8,128)(2,1)} %pad_maximum_fusion.11), channel_id=1, source_target_pairs={{0,3},{1,0},{2,1},{3,2},{4,7},{5,4},{6,5},{7,6},{8,11},{9,8},{10,9... | collective-permute-start | bytes 1572872 | tf_op jit(solution)/shard_map/ppermute | solution.py:424
  166.6 73.8 %collective-permute-start.14 = (bf16[128,2048]{1,0:T(8,128)(2,1)S(1)}, bf16[128,2048]{1,0:T(8,128)(2,1)}, u32[]{:S(2)}, u32[]{:S(2)}) collective-permute-start(bf16[128,2048]{1,0:T(8,128)(2,1)S(1)} %copy-done.27), channel_id=1, source_target_pairs={{0,1},{1,2},{2,3},{3,0},{4,5},{5,6},{6,7},{7,4},{8,9},{9,10},{10,1... | collective-permute-start | bytes 1572872 | tf_op jit(solution)/shard_map/ppermute | solution.py:424
  166.7 40.2 %collective-permute-start.16 = (bf16[64,2048]{1,0:T(8,128)(2,1)S(1)}, bf16[64,2048]{1,0:T(8,128)(2,1)S(1)}, u32[]{:S(2)}, u32[]{:S(2)}) collective-permute-start(bf16[64,2048]{1,0:T(8,128)(2,1)S(1)} %slice.420), channel_id=1, source_target_pairs={{0,1},{1,2},{2,3},{3,0},{4,5},{5,6},{6,7},{7,4},{8,9},{9,10},{10,1... | collective-permute-start | bytes 786440 | tf_op jit(solution)/shard_map/ppermute | solution.py:424
  167.7 42.7 %collective-permute-start.17 = (bf16[64,2048]{1,0:T(8,128)(2,1)S(1)}, bf16[64,2048]{1,0:T(8,128)(2,1)S(1)}, u32[]{:S(2)}, u32[]{:S(2)}) collective-permute-start(bf16[64,2048]{1,0:T(8,128)(2,1)S(1)} %slice.421), channel_id=1, source_target_pairs={{0,3},{1,0},{2,1},{3,2},{4,7},{5,4},{6,5},{7,6},{8,11},{9,8},{10,9... | collective-permute-start | bytes 786440 | tf_op jit(solution)/shard_map/ppermute | solution.py:424
  242.1 94.6 %collective-permute-start.28 = (bf16[64,2048]{1,0:T(8,128)(2,1)}, bf16[64,2048]{1,0:T(8,128)(2,1)}, u32[]{:S(2)}, u32[]{:S(2)}) collective-permute-start(bf16[64,2048]{1,0:T(8,128)(2,1)} %slice.426), channel_id=1, source_target_pairs={{0,1},{1,2},{2,3},{3,0},{4,5},{5,6},{6,7},{7,4},{8,9},{9,10},{10,1... | collective-permute-start | bytes 786440 | tf_op jit(solution)/shard_map/ppermute | solution.py:424
  244.4 93.9 %collective-permute-start.29 = (bf16[64,2048]{1,0:T(8,128)(2,1)}, bf16[64,2048]{1,0:T(8,128)(2,1)}, u32[]{:S(2)}, u32[]{:S(2)}) collective-permute-start(bf16[64,2048]{1,0:T(8,128)(2,1)} %slice.427), channel_id=1, source_target_pairs={{0,3},{1,0},{2,1},{3,2},{4,7},{5,4},{6,5},{7,6},{8,11},{9,8},{10,9... | collective-permute-start | bytes 786440 | tf_op jit(solution)/shard_map/ppermute | solution.py:424
  391.2 36.9 %collective-permute-start.34 = (bf16[128,2048]{1,0:T(8,128)(2,1)S(1)}, bf16[128,2048]{1,0:T(8,128)(2,1)S(1)}, u32[]{:S(2)}, u32[]{:S(2)}) collective-permute-start(bf16[128,2048]{1,0:T(8,128)(2,1)S(1)} %pad_maximum_fusion.14), channel_id=1, source_target_pairs={{0,1},{1,2},{2,3},{3,0},{4,5},{5,6},{6,7},{7,4},{8,9},{9,10},{10,1... | collective-permute-start | bytes 1572872 | tf_op jit(solution)/shard_map/ppermute | solution.py:424
  456.0 259.8 %reduce-scatter.6.cloned.1.call-start = ((), (), s32[]{:S(2)}) async-start(), calls=%async_computation.8 | async-start | bytes 12976128 | tf_op jit(solution)/shard_map/reduce_scatter | solution.py:504
  476.4 269.0 %reduce-scatter.8.cloned.1.call-start = ((), (), s32[]{:S(2)}) async-start(), calls=%async_computation.9 | async-start | bytes 10027008 | tf_op jit(solution)/shard_map/reduce_scatter | solution.py:504
  525.2 47.6 %collective-permute-start.48 = (bf16[128,2048]{1,0:T(8,128)(2,1)S(1)}, bf16[128,2048]{1,0:T(8,128)(2,1)S(1)}, u32[]{:S(2)}, u32[]{:S(2)}) collective-permute-start(bf16[128,2048]{1,0:T(8,128)(2,1)S(1)} %get-tuple-element.92), channel_id=1, source_target_pairs={{0,1},{1,2},{2,3},{3,0},{4,5},{5,6},{6,7},{7,4},{8,9},{9,10},{10,1... | collective-permute-start | bytes 1572872 | tf_op jit(solution)/shard_map/ppermute | solution.py:424
  525.2 47.7 %collective-permute-start.49 = (bf16[128,2048]{1,0:T(8,128)(2,1)S(1)}, bf16[128,2048]{1,0:T(8,128)(2,1)}, u32[]{:S(2)}, u32[]{:S(2)}) collective-permute-start(bf16[128,2048]{1,0:T(8,128)(2,1)S(1)} %get-tuple-element.92), channel_id=1, source_target_pairs={{0,3},{1,0},{2,1},{3,2},{4,7},{5,4},{6,5},{7,6},{8,11},{9,8},{10,9... | collective-permute-start | bytes 1572872 | tf_op jit(solution)/shard_map/ppermute | solution.py:424
  530.4 36.8 %collective-permute-start.42 = (bf16[64,2048]{1,0:T(8,128)(2,1)}, bf16[64,2048]{1,0:T(8,128)(2,1)}, u32[]{:S(2)}, u32[]{:S(2)}) collective-permute-start(bf16[64,2048]{1,0:T(8,128)(2,1)} %get-tuple-element.175), channel_id=1, source_target_pairs={{0,1},{1,2},{2,3},{3,0},{4,5},{5,6},{6,7},{7,4},{8,9},{9,10},{10,1... | collective-permute-start | bytes 786440 | tf_op jit(solution)/shard_map/ppermute | solution.py:424
  530.4 36.8 %collective-permute-start.43 = (bf16[64,2048]{1,0:T(8,128)(2,1)}, bf16[64,2048]{1,0:T(8,128)(2,1)}, u32[]{:S(2)}, u32[]{:S(2)}) collective-permute-start(bf16[64,2048]{1,0:T(8,128)(2,1)} %get-tuple-element.174), channel_id=1, source_target_pairs={{0,3},{1,0},{2,1},{3,2},{4,7},{5,4},{6,5},{7,6},{8,11},{9,8},{10,9... | collective-permute-start | bytes 786440 | tf_op jit(solution)/shard_map/ppermute | solution.py:424
  569.9 87.6 %collective-permute-start.47 = (bf16[128,2048]{1,0:T(8,128)(2,1)}, bf16[128,2048]{1,0:T(8,128)(2,1)}, u32[]{:S(2)}, u32[]{:S(2)}) collective-permute-start(bf16[128,2048]{1,0:T(8,128)(2,1)} %pad_maximum_fusion.19), channel_id=1, source_target_pairs={{0,3},{1,0},{2,1},{3,2},{4,7},{5,4},{6,5},{7,6},{8,11},{9,8},{10,9... | collective-permute-start | bytes 1572872 | tf_op jit(solution)/shard_map/ppermute | solution.py:424
  571.6 85.9 %collective-permute-start.46 = (bf16[128,2048]{1,0:T(8,128)(2,1)}, bf16[128,2048]{1,0:T(8,128)(2,1)}, u32[]{:S(2)}, u32[]{:S(2)}) collective-permute-start(bf16[128,2048]{1,0:T(8,128)(2,1)} %pad_maximum_fusion.18), channel_id=1, source_target_pairs={{0,1},{1,2},{2,3},{3,0},{4,5},{5,6},{6,7},{7,4},{8,9},{9,10},{10,1... | collective-permute-start | bytes 1572872 | tf_op jit(solution)/shard_map/ppermute | solution.py:424
  618.1 39.3 %collective-permute-start.55 = (bf16[128,2048]{1,0:T(8,128)(2,1)}, bf16[128,2048]{1,0:T(8,128)(2,1)S(1)}, u32[]{:S(2)}, u32[]{:S(2)}) collective-permute-start(bf16[128,2048]{1,0:T(8,128)(2,1)} %pad_maximum_fusion.21), channel_id=1, source_target_pairs={{0,3},{1,0},{2,1},{3,2},{4,7},{5,4},{6,5},{7,6},{8,11},{9,8},{10,9... | collective-permute-start | bytes 1572872 | tf_op jit(solution)/shard_map/ppermute | solution.py:424
  (121 other events, 1624.1 us)
Sparse Core Ops, SparseCore 0:
  17.5 51.6 all-gather.4
  71.0 28.0 all-gather.6
  101.6 67.6 all-gather.8
  171.0 44.3 all-gather.10
  456.1 58.1 reduce-scatter.3
  517.6 87.1 reduce-scatter.5
  671.6 73.7 reduce-scatter.7

commit v2 on v1

--- a/solution.py
+++ b/solution.py
@@ -559,11 +559,11 @@
     rows = [tokens[index].astype(F32) for index in range(batches)]
     layouts = [doc_layout(doc_lengths[index, 0], slots) for index in range(batches)]
 
-    def mix(index, projected):
+    def mix(index, projected, *beside):
         mixed, *kept = mixer_forward(
             projected, full_conv, full_head_gain, *layouts[index], heads
         )
-        return mixed, kept, dot(mixed, full_out, 1, 1, BF16)
+        return mixed, kept, dot(held(mixed, beside), full_out, 1, 1, BF16)
 
     def after_mixer(index, branch):
         hidden = rows[index] + branch
@@ -575,7 +575,7 @@
         activated = (gate * sigmoid(gate) * gate_up[:, units:]).astype(BF16)
         return gate_up, activated
 
-    def feed_back(gate_up, cot_full):
+    def feed_back(gate_up, cot_full, *beside):
         grad_act = dot(cot_full, full_down, 1, 0)
         gate = gate_up[:, :units]
         up = gate_up[:, units:]
@@ -583,7 +583,7 @@
         grad_gate = grad_act * up * opened * (1.0 + gate * (1.0 - opened))
         grad_up = grad_act * (gate * opened)
         grad_gate_up = jnp.concatenate([grad_gate, grad_up], axis=1).astype(BF16)
-        return grad_gate_up, dot(grad_gate_up, full_gate_up, 1, 1, BF16)
+        return grad_gate_up, dot(held(grad_gate_up, beside), full_gate_up, 1, 1, BF16)
 
     def before_ffn(index, hidden, pulled):
         return cotangent[index].astype(F32) + norm_pull(hidden, pulled)
@@ -596,48 +596,47 @@
 
     attn_in = [(rows[index] * row_scale(rows[index])).astype(BF16) for index in range(batches)]
     attn_0, first, last = gather_rows(attn_in[0])
-    attn_1, first, last = gather_rows(attn_in[1], last)
-    proj_0 = dot(held(attn_0, first), full_proj, 1, 0)
-    cot_0, cot_first, last = gather_rows(cotangent[0], first, proj_0)
-    mixed_0, kept_0, part_0 = mix(0, held(proj_0, attn_1))
-
-    proj_1 = dot(held(attn_1, part_0), full_proj, 1, 0)
-    branch, first, last = scatter_rows(part_0, mid=(proj_1,))
-    cot_1, cot_first, cot_last = gather_rows(cotangent[1], first, cot_first)
-    mixed_1, kept_1, part_1 = mix(1, held(proj_1, first, cot_0))
+    attn_1, attn_first, _ = gather_rows(attn_in[1], last, full_proj)
+    cot_0, cot_first, _ = gather_rows(cotangent[0], last, full_proj)
+    proj_0 = dot(attn_0, full_proj, 1, 0)
+    mixed_0, kept_0, part_0 = mix(0, proj_0, attn_first, cot_first)
+
+    branch, first, last = scatter_rows(part_0)
+    proj_1 = dot(attn_1, full_proj, 1, 0)
+    mixed_1, kept_1, part_1 = mix(1, held(proj_1, first), last, cot_0)
     hidden_0, ffn_in = after_mixer(0, branch)
 
-    ffn_0, first, last = gather_rows(ffn_in, cot_first, part_1, full_gate_up)
-    gate_up_0, act_0 = feed(ffn_0)
-    branch, first, last = scatter_rows(part_1, first, mid=(gate_up_0, full_down))
-    grad_gate_up_0, part_0 = feed_back(gate_up_0, cot_0)
+    ffn_0, ffn_first, _ = gather_rows(ffn_in, part_1, full_gate_up)
+    branch, first, last = scatter_rows(part_1, ffn_first)
+    gate_up_0, act_0 = feed(held(ffn_0, first))
+    grad_gate_up_0, part_0 = feed_back(gate_up_0, cot_0, last)
     hidden_1, ffn_in = after_mixer(1, branch)
 
-    ffn_1, ffn_first, last = gather_rows(ffn_in, part_0)
+    ffn_1, ffn_first, _ = gather_rows(ffn_in)
+    down_0 = dot(held(act_0, part_0), full_down, 1, 1, BF16)
+    down_grad = dot(held(cot_0, down_0), act_0, 0, 0, BF16)
+    cot_1, cot_first, _ = gather_rows(cotangent[1], ffn_first)
     pulled, first, last = scatter_rows(part_0, ffn_first)
-    down_0 = dot(held(act_0, ffn_first), full_down, 1, 1, BF16)
-    down_grad = dot(held(cot_0, down_0), act_0, 0, 0, BF16)
-    gate_up_grad = dot(held(ffn_0, down_grad), grad_gate_up_0, 0, 0, BF16)
+    gate_up_grad = dot(held(ffn_0, down_grad, ffn_first), grad_gate_up_0, 0, 0, BF16)
     gate_up_1, act_1 = feed(held(ffn_1, first, gate_up_grad))
-    grad_gate_up_1, part_1 = feed_back(gate_up_1, cot_1)
+    grad_gate_up_1, part_1 = feed_back(gate_up_1, cot_1, last)
     grad_hidden_0 = before_ffn(0, hidden_0, pulled)
 
     branch_0, first, last = gather_rows(grad_hidden_0.astype(BF16))
-    act_1_held = held(act_1, part_1, first)
-    down_1 = dot(act_1_held, full_down, 1, 1, BF16)
-    down_grad = (down_grad + dot(cot_1, act_1_held, 0, 0)).astype(BF16)
-    gate_up_grad = gate_up_grad + dot(held(ffn_1, down_1, down_grad), grad_gate_up_1, 0, 0)
+    pulled, first, last = scatter_rows(part_1, first)
+    gate_up_grad = gate_up_grad + dot(held(ffn_1, first, branch_0), grad_gate_up_1, 0, 0)
     gate_up_grad = gate_up_grad.astype(BF16)
-    pulled, first, last = scatter_rows(part_1, first, mid=(gate_up_grad,))
     grad_hidden_1 = before_ffn(1, hidden_1, pulled)
-    down_grad = scatter_dp(down_grad)
 
     branch_in = held(grad_hidden_1.astype(BF16), gate_up_grad)
-    branch_1, first, last = gather_rows(branch_in)
+    branch_1, branch_first, last = gather_rows(branch_in)
     gate_up_grad = scatter_dp(gate_up_grad)
     grad_mixed = dot(held(branch_0, branch_in), full_out, 1, 0)
     grad_proj_0, conv_grad_0, gain_grad_0, part_0 = mix_back(0, grad_mixed, proj_0, kept_0)
     lower_0, down_first, down_last = scatter_rows(down_0, branch_in, mid=(part_0,))
+    act_1_held = held(act_1, part_0, branch_first)
+    down_1 = dot(act_1_held, full_down, 1, 1, BF16)
+    down_grad = (down_grad + dot(cot_1, act_1_held, 0, 0)).astype(BF16)
 
     pulled, first, last = scatter_rows(part_0, last)
     out_grad = dot(
@@ -645,11 +644,12 @@
     )
     grad_mixed = dot(held(branch_1, part_0), full_out, 1, 0)
     input_rows_0 = grad_hidden_0 + norm_pull(rows[0], pulled)
-    grad_mixed = held(grad_mixed, first, down_first, out_grad)
+    grad_mixed = held(grad_mixed, first, down_first, out_grad, down_1, down_grad)
+    down_grad = scatter_dp(down_grad)
     grad_proj_1, conv_grad_1, gain_grad_1, part_1 = mix_back(1, grad_mixed, proj_1, kept_1)
 
     attn_all = joined([held(attn_0, part_1, last, down_last), attn_1])
-    pulled, first, last = scatter_rows(part_1, last, down_last, down_grad)
+    pulled, first, last = scatter_rows(part_1, last, down_last)
     proj_grad = dot(attn_all, joined([grad_proj_0, grad_proj_1]), 0, 0, BF16)
     conv_grad = (conv_grad_0 + conv_grad_1).reshape(12, heads, dp_size, head_share)
     conv_grad = jnp.transpose(conv_grad, (2, 0, 1, 3)).reshape(dp_size, conv_share)
@@ -660,7 +660,7 @@
     small_grad = small_grad.reshape(dp_size * shard, extra).astype(BF16)
     small_grad = jnp.pad(small_grad, ((0, 0), (small_at, LANES - heads - extra)))
     mixer_grad = scatter_dp(jnp.concatenate([proj_grad + small_grad, out_grad], axis=1))
-    lower_1, first, last = scatter_rows(down_1, last, gate_up_grad)
+    lower_1, first, last = scatter_rows(down_1, last, mid=(gate_up_grad,))
     mixer_grad = held(mixer_grad, last)
     input_rows_1 = grad_hidden_1 + norm_pull(rows[1], pulled)
     layer_rows_0 = (hidden_0 + lower_0).astype(BF16)

time: 780 us -> 718 us (0.921)
  waiting for transfers between devices: 234 us -> 179 us
    ppermute x67, waiting for transfers between devices: 233 us -> 160 us  [ring_shift(): lax.ppermute(value, 'tensor', [(place, (place + step) % size) for place i...]
    reduce_scatter x3, waiting for transfers between devices: 0.06 us -> 12.9 us  [scatter_dp(): return lax.psum_scatter(value, 'dp', scatter_dimension=0, tiled=True)]
  transfers between devices with their start and end apart: 74 -> 74, of which waited for: 36 -> 29; matrix products, arithmetic and copies ran while one was open for 35% -> 38% of each run, Pallas kernels for 12% -> 13%
where the time goes in v2:
time: 718 us; the launch traced here: 713 us
  waiting for transfers between devices  179 us (25%)
  matrix products  168 us (23%)
  starting transfers between devices  118 us (16%)
  Pallas kernels  94.3 us (13%)
  local copies, waits for them, and re-layouts  75.3 us (10%)
  other arithmetic  60.5 us (8%)
  between operations  18.6 us (3%)
    dot_general x22, matrix products, dot(): lax.dot_general(left, right, (((left_dim,), (right_dim,)), ((), ())), pre...  168 us
    ppermute x67, waiting for transfers between devices, ring_shift(): lax.ppermute(value, 'tensor', [(place, (place + step) % size) for place i...  160 us
    ppermute x67, starting transfers between devices, ring_shift(): lax.ppermute(value, 'tensor', [(place, (place + step) % size) for place i...  117 us
    pallas_call x2, Pallas kernels, mixer_forward(): pl.pallas_call(lambda *refs: forward_kernel(*refs, heads=heads, head_dim=...  49.4 us
    pallas_call x2, Pallas kernels, mixer_backward(): pl.pallas_call(lambda *refs: backward_kernel(*refs, heads=heads, head_dim...  44.9 us
    dynamic_update_slice x40, local copies, waits for them, and re-layouts, put(): lax.dynamic_update_slice(full, piece, (piece_start(step, count) + at, 0))  25 us
  transfers between devices with their start and end apart: 74, of which 29 were waited for; matrix products, arithmetic and copies ran while one was open for 38% of the time, Pallas kernels for 13%

profile of v2, /device:TPU:0, one launch (start us, length us, event | category | flops | bytes accessed | tf_op | source)
XLA Modules:
  0.0 713.0 jit_solution(2898743235524614697)
XLA Ops:
  41.1 10.0 %collective-permute-done.1 = bf16[128,2048]{1,0:T(8,128)(2,1)} collective-permute-done((bf16[128,2048]{1,0:T(8,128)(2,1)S(1)}, bf16[128,2048]{1,0:T(8,128)(2,1)}, u32[]{:S(2)}, u32[]{:S(2)}) %collective-permute-start.1) | collective-permute-done | bytes 524320 | tf_op jit(solution)/shard_map/ppermute | solution.py:424
  76.9 9.5 %fusion.53.refs_0_.refs_1_.refs_2_ = f32[512,1664]{1,0:T(8,128)} fusion(bf16[512,2048]{1,0:T(8,128)(2,1)} %constant_dynamic-update-slice_fusion.35, bf16[2048,1664]{0,1:T(8,128)(2,1)} %all-gather.5.cloned.1.call-done), kind=kOutput, calls=%fused_computation.233 | convolution fusion | flops 3489660928 | bytes 12320768 | tf_op jit(solution)/shard_map/dot_general | solution.py:494
  89.8 24.7 %mixer_forward.2 = (bf16[512,512]{1,0:T(8,128)(2,1)}, f32[512,512]{1,0:T(8,128)}, bf16[8,4,128,128]{3,2,1,0:T(8,128)(2,1)}, bf16[8,256,256]{2,1,0:T(8,128)(2,1)}...) custom-call(f32[512,1664]{1,0:T(8,128)} %fusion.53.refs_0_.refs_1_.refs_2_, ...), custom_call_target="tpu_custom_call" | custom-call | tf_op jit(solution)/shard_map/mixer_forward/pallas_call | solution.py:328
  160.0 24.7 %mixer_forward.3 = (bf16[512,512]{1,0:T(8,128)(2,1)}, f32[512,512]{1,0:T(8,128)}, bf16[8,4,128,128]{3,2,1,0:T(8,128)(2,1)}, bf16[8,256,256]{2,1,0:T(8,128)(2,1)}...) custom-call(f32[512,1664]{1,0:T(8,128)} %fusion.55.refs_0_.refs_1_.refs_2_, ...), custom_call_target="tpu_custom_call" | custom-call | tf_op jit(solution)/shard_map/mixer_forward/pallas_call | solution.py:328
  196.1 9.4 %collective-permute-done.16 = bf16[128,2048]{1,0:T(8,128)(2,1)S(1)} collective-permute-done((bf16[128,2048]{1,0:T(8,128)(2,1)S(1)}, bf16[128,2048]{1,0:T(8,128)(2,1)S(1)}, u32[]{:S(2)}, u32[]{:S(2)}) %collective-permute-start.16) | collective-permute-done | bytes 524320 | tf_op jit(solution)/shard_map/ppermute | solution.py:424
  240.4 11.1 %fusion.57 = f32[512,2816]{1,0:T(8,128)} fusion(bf16[512,2048]{1,0:T(8,128)(2,1)S(1)} %constant_dynamic-update-slice_fusion.20, bf16[2048,2816]{1,0:T(8,128)(2,1)} %all-gather.9.cloned.1.call-done), kind=kOutput, calls=%fused_computation.237 | convolution fusion | flops 5905580032 | bytes 19398656 | tf_op jit(solution)/shard_map/dot_general | solution.py:494
  251.5 9.3 %multiply_convert_fusion.4 = (bf16[512,1408]{1,0:T(8,128)(2,1)S(1)}, bf16[512,1408]{1,0:T(8,128)(2,1)S(1)}, bf16[512,1408]{1,0:T(8,128)(2,1)S(1)}) fusion(f32[512,2816]{1,0:T(8,128)} %fusion.57, bf16[512,2048]{1,0:T(8,128)(2,1)} %constant_dynamic-update-slice_fusion.25, bf16[2048,1408]{0,1:T(8,128)(2,1)} %all-gather.11.cloned.1.call-done), kind=kOutput, calls=%fused_computation.25 | convolution fusion | flops 2963603456 | bytes 17956864 | tf_op jit(solution)/shard_map/dot_general | solution.py:494
  267.2 9.0 %fusion.58 = bf16[512,2048]{1,0:T(8,128)(2,1)S(1)} fusion(bf16[512,2816]{1,0:T(8,128)(2,1)S(1)} %pad_maximum_fusion.1, bf16[2048,2816]{1,0:T(8,128)(2,1)} %all-gather.9.cloned.1.call-done), kind=kOutput, calls=%fused_computation.238 | convolution fusion | flops 5905580032 | bytes 16515072 | tf_op jit(solution)/shard_map/dot_general | solution.py:494
  294.1 9.0 %fusion.47 = bf16[2048,2816]{1,0:T(8,128)(2,1)} fusion(bf16[512,2048]{1,0:T(8,128)(2,1)S(1)} %copy-done.22, bf16[512,1408]{1,0:T(8,128)(2,1)S(1)} %get-tuple-element.152, bf16[512,1408]{1,0:T(8,128)(2,1)S(1)} %get-tuple-element.151), kind=kOutput, calls=%fused_computation.227 | convolution fusion | flops 5911347200 | bytes 16515072 | tf_op jit(solution)/shard_map/dot_general | solution.py:494
  307.4 21.7 %collective-permute-done.30 = bf16[64,2048]{1,0:T(8,128)(2,1)S(1)} collective-permute-done((bf16[64,2048]{1,0:T(8,128)(2,1)S(1)}, bf16[64,2048]{1,0:T(8,128)(2,1)S(1)}, u32[]{:S(2)}, u32[]{:S(2)}) %collective-permute-start.30) | collective-permute-done | bytes 262176 | tf_op jit(solution)/shard_map/ppermute | solution.py:424
  329.4 13.7 %collective-permute-done.33 = bf16[64,2048]{1,0:T(8,128)(2,1)S(1)} collective-permute-done((bf16[64,2048]{1,0:T(8,128)(2,1)S(1)}, bf16[64,2048]{1,0:T(8,128)(2,1)S(1)}, u32[]{:S(2)}, u32[]{:S(2)}) %collective-permute-start.33) | collective-permute-done | bytes 262176 | tf_op jit(solution)/shard_map/ppermute | solution.py:424
  347.5 11.1 %fusion.61 = f32[512,2816]{1,0:T(8,128)} fusion(bf16[512,2048]{1,0:T(8,128)(2,1)S(1)} %constant_dynamic-update-slice_fusion.10, bf16[2048,2816]{1,0:T(8,128)(2,1)} %all-gather.9.cloned.1.call-done), kind=kOutput, calls=%fused_computation.241 | convolution fusion | flops 5905580032 | bytes 19398656 | tf_op jit(solution)/shard_map/dot_general | solution.py:494
  362.7 10.7 %collective-permute-done.35 = bf16[128,2048]{1,0:T(8,128)(2,1)S(1)} collective-permute-done((bf16[128,2048]{1,0:T(8,128)(2,1)S(1)}, bf16[128,2048]{1,0:T(8,128)(2,1)S(1)}, u32[]{:S(2)}, u32[]{:S(2)}) %collective-permute-start.35) | collective-permute-done | bytes 524320 | tf_op jit(solution)/shard_map/ppermute | solution.py:424
  380.4 9.7 %multiply_convert_fusion.2 = (bf16[512,1408]{1,0:T(8,128)(2,1)S(1)}, bf16[512,1408]{1,0:T(8,128)(2,1)S(1)}, bf16[512,1408]{1,0:T(8,128)(2,1)}) fusion(f32[512,2816]{1,0:T(8,128)} %fusion.61, bf16[512,2048]{1,0:T(8,128)(2,1)S(1)} %constant_dynamic-update-slice_fusion.15, bf16[2048,1408]{0,1:T(8,128)(2,1)} %all-gather.11.cloned.1.call-done), kind=kOutput, calls=%fused_computation.21 | convolution fusion | flops 2963603456 | bytes 17956864 | tf_op jit(solution)/shard_map/dot_general | solution.py:494
  390.2 9.0 %fusion.62 = bf16[512,2048]{1,0:T(8,128)(2,1)S(1)} fusion(bf16[512,2816]{1,0:T(8,128)(2,1)S(1)} %pad_maximum_fusion.2, bf16[2048,2816]{1,0:T(8,128)(2,1)} %all-gather.9.cloned.1.call-done), kind=kOutput, calls=%fused_computation.242 | convolution fusion | flops 5905580032 | bytes 16515072 | tf_op jit(solution)/shard_map/dot_general | solution.py:494
  418.1 11.5 %add_convert_fusion = bf16[2048,2816]{1,0:T(8,128)(2,1)} fusion(bf16[2048,2816]{1,0:T(8,128)(2,1)} %fusion.47, bf16[512,2048]{1,0:T(8,128)(2,1)S(1)} %constant_dynamic-update-slice_fusion.10, bf16[512,1408]{1,0:T(8,128)(2,1)S(1)} %get-tuple-element.150, bf16[512,1408]{1,0:T(8,128)(2,1)S(1)} %get-tuple-element.149), kind=kOutput, calls=%fused_computation | convolution fusion | flops 5928648704 | bytes 28049408 | tf_op jit(solution)/shard_map/dot_general | solution.py:494
  437.1 9.9 %collective-permute-done.39 = bf16[128,2048]{1,0:T(8,128)(2,1)S(1)} collective-permute-done((bf16[128,2048]{1,0:T(8,128)(2,1)S(1)}, bf16[128,2048]{1,0:T(8,128)(2,1)S(1)}, u32[]{:S(2)}, u32[]{:S(2)}) %collective-permute-start.39) | collective-permute-done | bytes 524320 | tf_op jit(solution)/shard_map/ppermute | solution.py:424
  447.0 12.4 %collective-permute-done.41 = bf16[128,2048]{1,0:T(8,128)(2,1)S(1)} collective-permute-done((bf16[128,2048]{1,0:T(8,128)(2,1)S(1)}, bf16[128,2048]{1,0:T(8,128)(2,1)S(1)}, u32[]{:S(2)}, u32[]{:S(2)}) %collective-permute-start.41) | collective-permute-done | bytes 524320 | tf_op jit(solution)/shard_map/ppermute | solution.py:424
  473.7 22.5 %mixer_backward.2 = (bf16[512,1664]{1,0:T(8,128)(2,1)}, f32[12,512]{1,0:T(8,128)}, f32[1,128]{1,0:T(1,128)}) custom-call(f32[512,1664]{1,0:T(8,128)} %fusion.53.refs_0_.refs_1_.refs_2_, f32[512,1664]{1,0:T(8,128)} %fusion.53.refs_0_.refs_1_.refs_2_, f32[512,1664]{1,0:T(8,128)} %fusion.53.refs_0_.refs_1_.refs_2_, f32[512,1]{1,0:T(8,128)} %fusion.39.refs_3_, ...), custom_call_target="tpu_custom_call" | custom-call | tf_op jit(solution)/shard_map/mixer_backward/pallas_call | solution.py:373
  496.1 9.8 %fusion.64 = bf16[512,2048]{1,0:T(8,128)(2,1)} fusion(bf16[512,1664]{1,0:T(8,128)(2,1)} %get-tuple-element.91, bf16[2048,1664]{0,1:T(8,128)(2,1)} %all-gather.5.cloned.1.call-done), kind=kOutput, calls=%fused_computation.244 | convolution fusion | flops 3489660928 | bytes 10616832 | tf_op jit(solution)/shard_map/dot_general | solution.py:494
  564.5 22.5 %mixer_backward.3 = (bf16[512,1664]{1,0:T(8,128)(2,1)}, f32[12,512]{1,0:T(8,128)}, f32[1,128]{1,0:T(1,128)}) custom-call(f32[512,1664]{1,0:T(8,128)} %fusion.55.refs_0_.refs_1_.refs_2_, f32[512,1664]{1,0:T(8,128)} %fusion.55.refs_0_.refs_1_.refs_2_, f32[512,1664]{1,0:T(8,128)} %fusion.55.refs_0_.refs_1_.refs_2_, f32[512,1]{1,0:T(8,128)} %fusion.38.refs_3_, ...), custom_call_target="tpu_custom_call" | custom-call | tf_op jit(solution)/shard_map/mixer_backward/pallas_call | solution.py:373
  592.0 8.9 %fusion.67 = bf16[512,2048]{1,0:T(8,128)(2,1)} fusion(bf16[512,1664]{1,0:T(8,128)(2,1)} %get-tuple-element.104, bf16[2048,1664]{0,1:T(8,128)(2,1)} %all-gather.5.cloned.1.call-done), kind=kOutput, calls=%fused_computation.247 | convolution fusion | flops 3489660928 | bytes 10616832 | tf_op jit(solution)/shard_map/dot_general | solution.py:494
  600.9 9.3 %pad_add_fusion = bf16[2048,1664]{0,1:T(8,128)(2,1)S(1)} fusion(bf16[2048,4]{0,1:T(4,128)(2,1)S(1)} %copy.33, bf16[512,2048]{1,0:T(8,128)(2,1)S(1)} %copy-done.20, bf16[512,2048]{1,0:T(8,128)(2,1)} %constant_dynamic-update-slice_fusion.35, bf16[512,1664]{1,0:T(8,128)(2,1)S(1)} %copy-done.49, bf16[512,1664]{1,0:T(8,128)(2,1)S(1)} %copy-done.48), kind=kOutput, calls=%fused_computation.3 | convolution fusion | flops 7008157696 | bytes 14434304 | tf_op jit(solution)/shard_map/dot_general | solution.py:494
  674.8 12.9 %reduce-scatter.6.cloned.1.call-done = bf16[256,2176]{0,1:T(8,128)(2,1)} async-done(((bf16[2048,2176]{0,1:T(8,128)(2,1)}), bf16[256,2176]{0,1:T(8,128)(2,1)}) %reduce-scatter.6.cloned.1.call-update) | async-done | bytes 1114128 | tf_op jit(solution)/shard_map/reduce_scatter | solution.py:504
  (467 shorter events, 382.1 us)
Async XLA Ops:
  7.2 61.9 %all-gather.5.cloned.1.call-start = ((), (), s32[]{:S(2)}) async-start(), calls=%async_computation.3 | async-start | bytes 7667712 | tf_op jit(solution)/shard_map/all_gather | solution.py:500
  17.4 102.0 %all-gather.7.cloned.1.call-start = ((), (), s32[]{:S(2)}) async-start(), calls=%async_computation.4 | async-start | bytes 2359296 | tf_op jit(solution)/shard_map/all_gather | solution.py:500
  18.1 173.7 %all-gather.9.cloned.1.call-start = ((), (), s32[]{:S(2)}) async-start(), calls=%async_computation.5 | async-start | bytes 12976128 | tf_op jit(solution)/shard_map/all_gather | solution.py:500
  21.8 229.7 %all-gather.11.cloned.1.call-start = ((), (), s32[]{:S(2)}) async-start(), calls=%async_computation.6 | async-start | bytes 6488064 | tf_op jit(solution)/shard_map/all_gather | solution.py:500
  28.2 627.9 %reduce-scatter.4.cloned.1.call-start = ((), (), s32[]{:S(2)}) async-start(), calls=%async_computation.7 | async-start | bytes 12976128 | tf_op jit(solution)/shard_map/reduce_scatter | solution.py:504
  69.1 50.2 %collective-permute-start.4 = (bf16[128,2048]{1,0:T(8,128)(2,1)}, bf16[128,2048]{1,0:T(8,128)(2,1)}, u32[]{:S(2)}, u32[]{:S(2)}) collective-permute-start(bf16[128,2048]{1,0:T(8,128)(2,1)} %get-tuple-element.64), channel_id=1, source_target_pairs={{0,1},{1,2},{2,3},{3,0},{4,5},{5,6},{6,7},{7,4},{8,9},{9,10},{10,1... | collective-permute-start | bytes 1572872 | tf_op jit(solution)/shard_map/ppermute | solution.py:424
  70.6 48.7 %collective-permute-start.5 = (bf16[128,2048]{1,0:T(8,128)(2,1)}, bf16[128,2048]{1,0:T(8,128)(2,1)}, u32[]{:S(2)}, u32[]{:S(2)}) collective-permute-start(bf16[128,2048]{1,0:T(8,128)(2,1)} %get-tuple-element.64), channel_id=1, source_target_pairs={{0,3},{1,0},{2,1},{3,2},{4,7},{5,4},{6,5},{7,6},{8,11},{9,8},{10,9... | collective-permute-start | bytes 1572872 | tf_op jit(solution)/shard_map/ppermute | solution.py:424
  72.9 46.3 %collective-permute-start.6 = (bf16[128,2048]{1,0:T(8,128)(2,1)}, bf16[128,2048]{1,0:T(8,128)(2,1)}, u32[]{:S(2)}, u32[]{:S(2)}) collective-permute-start(bf16[128,2048]{1,0:T(8,128)(2,1)} %get-tuple-element.65), channel_id=1, source_target_pairs={{0,1},{1,2},{2,3},{3,0},{4,5},{5,6},{6,7},{7,4},{8,9},{9,10},{10,1... | collective-permute-start | bytes 1572872 | tf_op jit(solution)/shard_map/ppermute | solution.py:424
  73.0 46.3 %collective-permute-start.7 = (bf16[128,2048]{1,0:T(8,128)(2,1)}, bf16[128,2048]{1,0:T(8,128)(2,1)}, u32[]{:S(2)}, u32[]{:S(2)}) collective-permute-start(bf16[128,2048]{1,0:T(8,128)(2,1)} %get-tuple-element.65), channel_id=1, source_target_pairs={{0,3},{1,0},{2,1},{3,2},{4,7},{5,4},{6,5},{7,6},{8,11},{9,8},{10,9... | collective-permute-start | bytes 1572872 | tf_op jit(solution)/shard_map/ppermute | solution.py:424
  132.2 52.5 %collective-permute-start.14 = (bf16[64,2048]{1,0:T(8,128)(2,1)}, bf16[64,2048]{1,0:T(8,128)(2,1)S(1)}, u32[]{:S(2)}, u32[]{:S(2)}) collective-permute-start(bf16[64,2048]{1,0:T(8,128)(2,1)} %slice.420), channel_id=1, source_target_pairs={{0,1},{1,2},{2,3},{3,0},{4,5},{5,6},{6,7},{7,4},{8,9},{9,10},{10,1... | collective-permute-start | bytes 786440 | tf_op jit(solution)/shard_map/ppermute | solution.py:424
  143.0 42.5 %collective-permute-start.15 = (bf16[64,2048]{1,0:T(8,128)(2,1)}, bf16[64,2048]{1,0:T(8,128)(2,1)}, u32[]{:S(2)}, u32[]{:S(2)}) collective-permute-start(bf16[64,2048]{1,0:T(8,128)(2,1)} %slice.421), channel_id=1, source_target_pairs={{0,3},{1,0},{2,1},{3,2},{4,7},{5,4},{6,5},{7,6},{8,11},{9,8},{10,9... | collective-permute-start | bytes 786440 | tf_op jit(solution)/shard_map/ppermute | solution.py:424
  145.0 42.3 %collective-permute-start.11 = (bf16[128,2048]{1,0:T(8,128)(2,1)}, bf16[128,2048]{1,0:T(8,128)(2,1)}, u32[]{:S(2)}, u32[]{:S(2)}) collective-permute-start(bf16[128,2048]{1,0:T(8,128)(2,1)} %pad_maximum_fusion.7), channel_id=1, source_target_pairs={{0,3},{1,0},{2,1},{3,2},{4,7},{5,4},{6,5},{7,6},{8,11},{9,8},{10,9... | collective-permute-start | bytes 1572872 | tf_op jit(solution)/shard_map/ppermute | solution.py:424
  145.9 41.4 %collective-permute-start.9 = (bf16[128,2048]{1,0:T(8,128)(2,1)}, bf16[128,2048]{1,0:T(8,128)(2,1)}, u32[]{:S(2)}, u32[]{:S(2)}) collective-permute-start(bf16[128,2048]{1,0:T(8,128)(2,1)} %pad_maximum_fusion.6), channel_id=1, source_target_pairs={{0,1},{1,2},{2,3},{3,0},{4,5},{5,6},{6,7},{7,4},{8,9},{9,10},{10,1... | collective-permute-start | bytes 1572872 | tf_op jit(solution)/shard_map/ppermute | solution.py:424
  289.9 68.6 %collective-permute-start.26 = (bf16[128,2048]{1,0:T(8,128)(2,1)S(1)}, bf16[128,2048]{1,0:T(8,128)(2,1)S(1)}, u32[]{:S(2)}, u32[]{:S(2)}) collective-permute-start(bf16[128,2048]{1,0:T(8,128)(2,1)S(1)} %copy-done.29), channel_id=1, source_target_pairs={{0,1},{1,2},{2,3},{3,0},{4,5},{5,6},{6,7},{7,4},{8,9},{9,10},{10,1... | collective-permute-start | bytes 1572872 | tf_op jit(solution)/shard_map/ppermute | solution.py:424
  290.0 68.7 %collective-permute-start.27 = (bf16[128,2048]{1,0:T(8,128)(2,1)S(1)}, bf16[128,2048]{1,0:T(8,128)(2,1)S(1)}, u32[]{:S(2)}, u32[]{:S(2)}) collective-permute-start(bf16[128,2048]{1,0:T(8,128)(2,1)S(1)} %copy-done.29), channel_id=1, source_target_pairs={{0,3},{1,0},{2,1},{3,2},{4,7},{5,4},{6,5},{7,6},{8,11},{9,8},{10,9... | collective-permute-start | bytes 1572872 | tf_op jit(solution)/shard_map/ppermute | solution.py:424
  429.7 233.1 %reduce-scatter.8.cloned.1.call-start = ((), (), s32[]{:S(2)}) async-start(), calls=%async_computation.9 | async-start | bytes 6488064 | tf_op jit(solution)/shard_map/reduce_scatter | solution.py:504
  461.2 44.8 %collective-permute-start.48 = (bf16[128,2048]{1,0:T(8,128)(2,1)}, bf16[128,2048]{1,0:T(8,128)(2,1)}, u32[]{:S(2)}, u32[]{:S(2)}) collective-permute-start(bf16[128,2048]{1,0:T(8,128)(2,1)} %get-tuple-element.83), channel_id=1, source_target_pairs={{0,1},{1,2},{2,3},{3,0},{4,5},{5,6},{6,7},{7,4},{8,9},{9,10},{10,1... | collective-permute-start | bytes 1572872 | tf_op jit(solution)/shard_map/ppermute | solution.py:424
  461.8 44.2 %collective-permute-start.49 = (bf16[128,2048]{1,0:T(8,128)(2,1)}, bf16[128,2048]{1,0:T(8,128)(2,1)}, u32[]{:S(2)}, u32[]{:S(2)}) collective-permute-start(bf16[128,2048]{1,0:T(8,128)(2,1)} %get-tuple-element.83), channel_id=1, source_target_pairs={{0,3},{1,0},{2,1},{3,2},{4,7},{5,4},{6,5},{7,6},{8,11},{9,8},{10,9... | collective-permute-start | bytes 1572872 | tf_op jit(solution)/shard_map/ppermute | solution.py:424
  466.0 48.8 %collective-permute-start.44 = (bf16[64,2048]{1,0:T(8,128)(2,1)}, bf16[64,2048]{1,0:T(8,128)(2,1)}, u32[]{:S(2)}, u32[]{:S(2)}) collective-permute-start(bf16[64,2048]{1,0:T(8,128)(2,1)} %get-tuple-element.169), channel_id=1, source_target_pairs={{0,1},{1,2},{2,3},{3,0},{4,5},{5,6},{6,7},{7,4},{8,9},{9,10},{10,1... | collective-permute-start | bytes 786440 | tf_op jit(solution)/shard_map/ppermute | solution.py:424
  466.0 48.8 %collective-permute-start.45 = (bf16[64,2048]{1,0:T(8,128)(2,1)}, bf16[64,2048]{1,0:T(8,128)(2,1)}, u32[]{:S(2)}, u32[]{:S(2)}) collective-permute-start(bf16[64,2048]{1,0:T(8,128)(2,1)} %get-tuple-element.168), channel_id=1, source_target_pairs={{0,3},{1,0},{2,1},{3,2},{4,7},{5,4},{6,5},{7,6},{8,11},{9,8},{10,9... | collective-permute-start | bytes 786440 | tf_op jit(solution)/shard_map/ppermute | solution.py:424
  513.2 174.5 %reduce-scatter.6.cloned.1.call-start = ((), (), s32[]{:S(2)}) async-start(), calls=%async_computation.8 | async-start | bytes 10027008 | tf_op jit(solution)/shard_map/reduce_scatter | solution.py:504
  517.0 83.8 %collective-permute-start.47 = (bf16[128,2048]{1,0:T(8,128)(2,1)}, bf16[128,2048]{1,0:T(8,128)(2,1)}, u32[]{:S(2)}, u32[]{:S(2)}) collective-permute-start(bf16[128,2048]{1,0:T(8,128)(2,1)} %pad_maximum_fusion.15), channel_id=1, source_target_pairs={{0,3},{1,0},{2,1},{3,2},{4,7},{5,4},{6,5},{7,6},{8,11},{9,8},{10,9... | collective-permute-start | bytes 1572872 | tf_op jit(solution)/shard_map/ppermute | solution.py:424
  517.9 83.0 %collective-permute-start.46 = (bf16[128,2048]{1,0:T(8,128)(2,1)}, bf16[128,2048]{1,0:T(8,128)(2,1)}, u32[]{:S(2)}, u32[]{:S(2)}) collective-permute-start(bf16[128,2048]{1,0:T(8,128)(2,1)} %pad_maximum_fusion.14), channel_id=1, source_target_pairs={{0,1},{1,2},{2,3},{3,0},{4,5},{5,6},{6,7},{7,4},{8,9},{9,10},{10,1... | collective-permute-start | bytes 1572872 | tf_op jit(solution)/shard_map/ppermute | solution.py:424
  561.6 39.3 %collective-permute-start.55 = (bf16[128,2048]{1,0:T(8,128)(2,1)}, bf16[128,2048]{1,0:T(8,128)(2,1)}, u32[]{:S(2)}, u32[]{:S(2)}) collective-permute-start(bf16[128,2048]{1,0:T(8,128)(2,1)} %pad_maximum_fusion.17), channel_id=1, source_target_pairs={{0,3},{1,0},{2,1},{3,2},{4,7},{5,4},{6,5},{7,6},{8,11},{9,8},{10,9... | collective-permute-start | bytes 1572872 | tf_op jit(solution)/shard_map/ppermute | solution.py:424
  (113 other events, 1659.2 us)
Sparse Core Ops, SparseCore 0:
  17.5 51.6 all-gather.4
  71.0 28.0 all-gather.6
  101.6 67.5 all-gather.8
  170.9 44.2 all-gather.10
  429.8 86.4 reduce-scatter.3
  519.6 59.0 reduce-scatter.7
  614.5 73.1 reduce-scatter.5

commit v3 on v2

--- a/solution.py
+++ b/solution.py
@@ -460,24 +460,31 @@
     return full, (from_left, from_right), far
 
 
-def scatter_rows(partial, *token, mid=()):
+def ring_rows(low, step, at, length):
+    count = low.shape[0] // lax.axis_size("tensor")
+    start = piece_start(step, count) + at
+    return lax.dynamic_slice(low, (start, 0), (length, low.shape[1])).astype(F32)
+
+
+def scatter_rows_begin(partial, *token):
     size = lax.axis_size("tensor")
-    count = partial.shape[0] // size
+    half = partial.shape[0] // size // 2
+    low = held(partial, token)
+    to_right = ring_shift(ring_rows(low, size // 2, 0, half).astype(BF16), 1)
+    to_left = ring_shift(ring_rows(low, size // 2, half, half).astype(BF16), -1)
+    return low, (to_right, to_left)
+
+
+def scatter_rows_end(state, *token):
+    size = lax.axis_size("tensor")
+    low, (to_right, to_left) = state
+    count = low.shape[0] // size
     half = count // 2
-    low = held(partial, token)
-
-    def take(step, at=0, length=count):
-        start = piece_start(step, count) + at
-        return lax.dynamic_slice(low, (start, 0), (length, low.shape[1])).astype(F32)
-
-    to_right = ring_shift(take(size // 2, 0, half).astype(BF16), 1)
-    to_left = ring_shift(take(size // 2, half, half).astype(BF16), -1)
-    first = to_right, to_left
-    if mid:
-        to_right, to_left = held(first, mid)
+    if token:
+        to_right, to_left = held((to_right, to_left), token)
     for step in range(size // 2 - 1, 0, -1):
-        right = take(step)
-        left = take(size - step)
+        right = ring_rows(low, step, 0, count)
+        left = ring_rows(low, size - step, 0, count)
         if step == size // 2 - 1:
             right = joined([right[:half] + to_right.astype(F32), right[half:]])
             left = joined([left[:half], left[half:] + to_left.astype(F32)])
@@ -486,8 +493,14 @@
             left = left + to_left.astype(F32)
         to_right = ring_shift(right.astype(BF16), 1)
         to_left = ring_shift(left.astype(BF16), -1)
-    total = take(0) + to_right.astype(F32) + to_left.astype(F32)
-    return total, first, (to_right, to_left)
+    total = ring_rows(low, 0, 0, count) + to_right.astype(F32) + to_left.astype(F32)
+    return total, (to_right, to_left)
+
+
+def scatter_rows(partial, *token, mid=()):
+    state = scatter_rows_begin(partial, *token)
+    total, last = scatter_rows_end(state, *mid)
+    return total, state[1], last
 
 
 def dot(left, right, left_dim, right_dim, out_type=F32):
@@ -588,12 +601,6 @@
     def before_ffn(index, hidden, pulled):
         return cotangent[index].astype(F32) + norm_pull(hidden, pulled)
 
-    def mix_back(index, grad_mixed, projected, kept):
-        grad_proj, conv_grad, gain_grad = mixer_backward(
-            projected, full_conv, full_head_gain, *layouts[index], heads, kept, grad_mixed
-        )
-        return grad_proj, conv_grad, gain_grad, dot(grad_proj, full_proj, 1, 1, BF16)
-
     attn_in = [(rows[index] * row_scale(rows[index])).astype(BF16) for index in range(batches)]
     attn_0, first, last = gather_rows(attn_in[0])
     attn_1, attn_first, _ = gather_rows(attn_in[1], last, full_proj)
@@ -619,37 +626,45 @@
     pulled, first, last = scatter_rows(part_0, ffn_first)
     gate_up_grad = dot(held(ffn_0, down_grad, ffn_first), grad_gate_up_0, 0, 0, BF16)
     gate_up_1, act_1 = feed(held(ffn_1, first, gate_up_grad))
-    grad_gate_up_1, part_1 = feed_back(gate_up_1, cot_1, last)
+    down_state = scatter_rows_begin(down_0, first)
+    grad_gate_up_1, part_1 = feed_back(gate_up_1, cot_1, last, down_state[1])
     grad_hidden_0 = before_ffn(0, hidden_0, pulled)
 
     branch_0, first, last = gather_rows(grad_hidden_0.astype(BF16))
+    down_grad = (down_grad + dot(held(cot_1, part_1, first), act_1, 0, 0)).astype(BF16)
     pulled, first, last = scatter_rows(part_1, first)
-    gate_up_grad = gate_up_grad + dot(held(ffn_1, first, branch_0), grad_gate_up_1, 0, 0)
+    gate_up_grad = gate_up_grad + dot(held(ffn_1, first, branch_0, down_grad), grad_gate_up_1, 0, 0)
     gate_up_grad = gate_up_grad.astype(BF16)
     grad_hidden_1 = before_ffn(1, hidden_1, pulled)
 
     branch_in = held(grad_hidden_1.astype(BF16), gate_up_grad)
-    branch_1, branch_first, last = gather_rows(branch_in)
+    branch_1, branch_first, _ = gather_rows(branch_in)
+    down_grad = scatter_dp(down_grad)
     gate_up_grad = scatter_dp(gate_up_grad)
+    down_1 = dot(held(act_1, branch_in), full_down, 1, 1, BF16)
     grad_mixed = dot(held(branch_0, branch_in), full_out, 1, 0)
-    grad_proj_0, conv_grad_0, gain_grad_0, part_0 = mix_back(0, grad_mixed, proj_0, kept_0)
-    lower_0, down_first, down_last = scatter_rows(down_0, branch_in, mid=(part_0,))
-    act_1_held = held(act_1, part_0, branch_first)
-    down_1 = dot(act_1_held, full_down, 1, 1, BF16)
-    down_grad = (down_grad + dot(cot_1, act_1_held, 0, 0)).astype(BF16)
-
-    pulled, first, last = scatter_rows(part_0, last)
+    grad_mixed = held(grad_mixed, branch_first, down_1)
+    grad_proj_0, conv_grad_0, gain_grad_0 = mixer_backward(
+        proj_0, full_conv, full_head_gain, *layouts[0], heads, kept_0, grad_mixed
+    )
+    lower_0, down_last = scatter_rows_end(down_state, branch_first)
+    part_0 = dot(held(grad_proj_0, branch_1, down_last), full_proj, 1, 1, BF16)
+
+    pulled, first, last = scatter_rows(part_0)
     out_grad = dot(
         joined([held(branch_0, part_0), branch_1]), joined([mixed_0, mixed_1]), 0, 0, BF16
     )
     grad_mixed = dot(held(branch_1, part_0), full_out, 1, 0)
     input_rows_0 = grad_hidden_0 + norm_pull(rows[0], pulled)
-    grad_mixed = held(grad_mixed, first, down_first, out_grad, down_1, down_grad)
-    down_grad = scatter_dp(down_grad)
-    grad_proj_1, conv_grad_1, gain_grad_1, part_1 = mix_back(1, grad_mixed, proj_1, kept_1)
-
-    attn_all = joined([held(attn_0, part_1, last, down_last), attn_1])
-    pulled, first, last = scatter_rows(part_1, last, down_last)
+    grad_mixed = held(grad_mixed, first, out_grad)
+    out_grad = scatter_dp(out_grad)
+    grad_proj_1, conv_grad_1, gain_grad_1 = mixer_backward(
+        proj_1, full_conv, full_head_gain, *layouts[1], heads, kept_1, grad_mixed
+    )
+    part_1 = dot(held(grad_proj_1, last), full_proj, 1, 1, BF16)
+    attn_all = joined([held(attn_0, last), attn_1])
+    pulled, first, last = scatter_rows(part_1, last, down_grad, gate_up_grad)
+    down_out = down_grad.T.astype(F32)
     proj_grad = dot(attn_all, joined([grad_proj_0, grad_proj_1]), 0, 0, BF16)
     conv_grad = (conv_grad_0 + conv_grad_1).reshape(12, heads, dp_size, head_share)
     conv_grad = jnp.transpose(conv_grad, (2, 0, 1, 3)).reshape(dp_size, conv_share)
@@ -659,24 +674,29 @@
     )
     small_grad = small_grad.reshape(dp_size * shard, extra).astype(BF16)
     small_grad = jnp.pad(small_grad, ((0, 0), (small_at, LANES - heads - extra)))
-    mixer_grad = scatter_dp(jnp.concatenate([proj_grad + small_grad, out_grad], axis=1))
-    lower_1, first, last = scatter_rows(down_1, last, mid=(gate_up_grad,))
-    mixer_grad = held(mixer_grad, last)
+    proj_grad = scatter_dp(proj_grad + small_grad)
+    gate_up_grad = gate_up_grad.astype(F32)
+    gate_up_out = (gate_up_grad * ffn_column).reshape(shard, 2, units)
+    ffn_gain_grad = jnp.sum(gate_up_grad * gate_up_rows, axis=1)
+    out_out = out_grad.T.astype(F32)
+    lower_1, first, last = scatter_rows(
+        down_1, last, down_out, mid=(gate_up_out, ffn_gain_grad, out_out)
+    )
+    proj_grad = held(proj_grad, first)
     input_rows_1 = grad_hidden_1 + norm_pull(rows[1], pulled)
     layer_rows_0 = (hidden_0 + lower_0).astype(BF16)
     layer_rows_1 = (hidden_1 + lower_1).astype(BF16)
 
-    proj_grad = mixer_grad[:, : columns + LANES].astype(F32)
-    out_grad = mixer_grad[:, columns + LANES :]
-    gate_up_grad = gate_up_grad.astype(F32)
+    proj_grad = proj_grad.astype(F32)
     small_grad = proj_grad[:, small_at : small_at + extra].reshape(extra * shard)
     gain_grads = jnp.concatenate(
         [
             jnp.sum(proj_grad[:, :small_at] * qkv_rows, axis=1),
-            jnp.sum(gate_up_grad * gate_up_rows, axis=1),
+            ffn_gain_grad,
             small_grad[conv_share:small_share],
         ]
     )[None]
+    gain_grads = held(gain_grads, last)
     total = gain_grads
     for step in range(1, size):
         total = total + ring_shift(gain_grads, step)
@@ -690,10 +710,10 @@
         proj_grad[:, columns:],
         small_grad[:conv_share].reshape(3, 4, heads, head_share),
         total[2 * shard :],
-        out_grad.T.astype(F32),
+        out_out,
         total[shard : 2 * shard],
-        (gate_up_grad * ffn_column).reshape(shard, 2, units),
-        down_grad.T.astype(F32),
+        gate_up_out,
+        down_out,
     )
 
 

time: 718 us -> 714 us (level)
  waiting for transfers between devices: 179 us -> 148 us
  local copies, waits for them, and re-layouts: 75.3 us -> 93.9 us
  starting transfers between devices: 118 us -> 129 us
  other arithmetic: 60.5 us -> 52 us
    ppermute x67, waiting for transfers between devices: 160 us -> 142 us  [ring_shift(): lax.ppermute(value, 'tensor', [(place, (place + step) % size) for place i...]
    reduce_scatter x3 -> x4, waiting for transfers between devices: 12.9 us -> 0.01 us  [scatter_dp(): return lax.psum_scatter(value, 'dp', scatter_dimension=0, tiled=True)]
    ppermute x67, starting transfers between devices: 117 us -> 129 us  [ring_shift(): lax.ppermute(value, 'tensor', [(place, (place + step) % size) for place i...]
    unnamed x130 -> x175, local copies, waits for them, and re-layouts: 9.54 us -> 18.5 us
    dynamic_update_slice x40, local copies, waits for them, and re-layouts: 25 us -> 32.5 us  [put(): lax.dynamic_update_slice(full, piece, (piece_start(step, count) + at, 0))]
  transfers between devices with their start and end apart: 74 -> 75, of which waited for: 29 -> 32; matrix products, arithmetic and copies ran while one was open for 38% -> 42% of each run, Pallas kernels for 13% -> 13%
where the time goes in v3:
time: 714 us; the launch traced here: 709 us
  matrix products  173 us (24%)
  waiting for transfers between devices  148 us (21%)
  starting transfers between devices  129 us (18%)
  Pallas kernels  94.3 us (13%)
  local copies, waits for them, and re-layouts  93.9 us (13%)
  other arithmetic  52 us (7%)
  between operations  18.9 us (3%)
    dot_general x22, matrix products, dot(): lax.dot_general(left, right, (((left_dim,), (right_dim,)), ((), ())), pre...  173 us
    ppermute x67, waiting for transfers between devices, ring_shift(): lax.ppermute(value, 'tensor', [(place, (place + step) % size) for place i...  142 us
    ppermute x67, starting transfers between devices, ring_shift(): lax.ppermute(value, 'tensor', [(place, (place + step) % size) for place i...  129 us
    pallas_call x2, Pallas kernels, mixer_forward(): pl.pallas_call(lambda *refs: forward_kernel(*refs, heads=heads, head_dim=...  49.2 us
    pallas_call x2, Pallas kernels, mixer_backward(): pl.pallas_call(lambda *refs: backward_kernel(*refs, heads=heads, head_dim...  45.1 us
    dynamic_update_slice x40, local copies, waits for them, and re-layouts, put(): lax.dynamic_update_slice(full, piece, (piece_start(step, count) + at, 0))  32.5 us
    unnamed x175, local copies, waits for them, and re-layouts  18.5 us
  transfers between devices with their start and end apart: 75, of which 32 were waited for; matrix products, arithmetic and copies ran while one was open for 42% of the time, Pallas kernels for 13%

profile of v3, /device:TPU:0, one launch (start us, length us, event | category | flops | bytes accessed | tf_op | source)
XLA Modules:
  0.0 708.7 jit_solution(7143881484803010099)
XLA Ops:
  37.2 9.0 %collective-permute-done.1 = bf16[128,2048]{1,0:T(8,128)(2,1)} collective-permute-done((bf16[128,2048]{1,0:T(8,128)(2,1)S(1)}, bf16[128,2048]{1,0:T(8,128)(2,1)}, u32[]{:S(2)}, u32[]{:S(2)}) %collective-permute-start.1) | collective-permute-done | bytes 524320 | tf_op jit(solution)/shard_map/ppermute | solution.py:424
  71.1 9.4 %fusion.53.refs_0_.refs_1_.refs_2_ = f32[512,1664]{1,0:T(8,128)} fusion(bf16[512,2048]{1,0:T(8,128)(2,1)} %constant_dynamic-update-slice_fusion.35, bf16[2048,1664]{1,0:T(8,128)(2,1)} %all-gather.5.cloned.1.call-done), kind=kOutput, calls=%fused_computation.231 | convolution fusion | flops 3489660928 | bytes 12320768 | tf_op jit(solution)/shard_map/dot_general | solution.py:507
  84.1 24.6 %mixer_forward.2 = (bf16[512,512]{1,0:T(8,128)(2,1)}, f32[512,512]{1,0:T(8,128)}, bf16[8,4,128,128]{3,2,1,0:T(8,128)(2,1)}, bf16[8,256,256]{2,1,0:T(8,128)(2,1)}...) custom-call(f32[512,1664]{1,0:T(8,128)} %fusion.53.refs_0_.refs_1_.refs_2_, ...), custom_call_target="tpu_custom_call" | custom-call | tf_op jit(solution)/shard_map/mixer_forward/pallas_call | solution.py:328
  157.8 24.6 %mixer_forward.3 = (bf16[512,512]{1,0:T(8,128)(2,1)}, f32[512,512]{1,0:T(8,128)}, bf16[8,4,128,128]{3,2,1,0:T(8,128)(2,1)}, bf16[8,256,256]{2,1,0:T(8,128)(2,1)}...) custom-call(f32[512,1664]{1,0:T(8,128)} %fusion.55.refs_0_.refs_1_.refs_2_, ...), custom_call_target="tpu_custom_call" | custom-call | tf_op jit(solution)/shard_map/mixer_forward/pallas_call | solution.py:328
  196.3 12.5 %collective-permute-done.16 = bf16[128,2048]{1,0:T(8,128)(2,1)S(1)} collective-permute-done((bf16[128,2048]{1,0:T(8,128)(2,1)S(1)}, bf16[128,2048]{1,0:T(8,128)(2,1)S(1)}, u32[]{:S(2)}, u32[]{:S(2)}) %collective-permute-start.16) | collective-permute-done | bytes 524320 | tf_op jit(solution)/shard_map/ppermute | solution.py:424
  208.7 7.8 %collective-permute-done.17 = bf16[128,2048]{1,0:T(8,128)(2,1)S(1)} collective-permute-done((bf16[128,2048]{1,0:T(8,128)(2,1)S(1)}, bf16[128,2048]{1,0:T(8,128)(2,1)S(1)}, u32[]{:S(2)}, u32[]{:S(2)}) %collective-permute-start.17) | collective-permute-done | bytes 524320 | tf_op jit(solution)/shard_map/ppermute | solution.py:424
  243.5 11.1 %fusion.57 = f32[512,2816]{1,0:T(8,128)} fusion(bf16[512,2048]{1,0:T(8,128)(2,1)S(1)} %constant_dynamic-update-slice_fusion.20, bf16[2048,2816]{1,0:T(8,128)(2,1)} %all-gather.9.cloned.1.call-done), kind=kOutput, calls=%fused_computation.235 | convolution fusion | flops 5905580032 | bytes 19398656 | tf_op jit(solution)/shard_map/dot_general | solution.py:507
  254.6 9.3 %multiply_convert_fusion.4 = (bf16[512,1408]{1,0:T(8,128)(2,1)S(1)}, bf16[512,1408]{1,0:T(8,128)(2,1)S(1)}, bf16[512,1408]{1,0:T(8,128)(2,1)S(1)}) fusion(f32[512,2816]{1,0:T(8,128)} %fusion.57, bf16[512,2048]{1,0:T(8,128)(2,1)} %constant_dynamic-update-slice_fusion.25, bf16[2048,1408]{0,1:T(8,128)(2,1)} %all-gather.11.cloned.1.call-done), kind=kOutput, calls=%fused_computation.24 | convolution fusion | flops 2963603456 | bytes 17956864 | tf_op jit(solution)/shard_map/dot_general | solution.py:507
  266.5 9.9 %collective-permute-start.24 = (bf16[128,2048]{1,0:T(8,128)(2,1)S(1)}, bf16[128,2048]{1,0:T(8,128)(2,1)S(1)}, u32[]{:S(2)}, u32[]{:S(2)}) collective-permute-start(bf16[128,2048]{1,0:T(8,128)(2,1)S(1)} %multiply_convert_fusion.7), channel_id=1, source_target_pairs={{0,1},{1,2},{2,3},{3,0},{4,5},{5,6},{6,7},{7,4},{8,9},{9,10},{10,1... | collective-permute-start | bytes 1572872 | tf_op jit(solution)/shard_map/ppermute | solution.py:424
  277.5 9.2 %fusion.58 = bf16[512,2048]{1,0:T(8,128)(2,1)S(1)} fusion(bf16[512,2816]{1,0:T(8,128)(2,1)S(1)} %pad_maximum_fusion, bf16[2048,2816]{1,0:T(8,128)(2,1)} %all-gather.9.cloned.1.call-done), kind=kOutput, calls=%fused_computation.236 | convolution fusion | flops 5905580032 | bytes 16515072 | tf_op jit(solution)/shard_map/dot_general | solution.py:507
  290.4 8.3 %fusion.60 = bf16[2048,1408]{1,0:T(8,128)(2,1)} fusion(bf16[512,2048]{1,0:T(8,128)(2,1)} %constant_dynamic-update-slice_fusion.25, bf16[512,1408]{1,0:T(8,128)(2,1)S(1)} %get-tuple-element.78), kind=kOutput, calls=%fused_computation.238 | convolution fusion | flops 2952790016 | bytes 9306112 | tf_op jit(solution)/shard_map/dot_general | solution.py:507
  306.8 9.0 %fusion.47 = bf16[2048,2816]{1,0:T(8,128)(2,1)} fusion(bf16[512,2048]{1,0:T(8,128)(2,1)S(1)} %copy-done.17, bf16[512,1408]{1,0:T(8,128)(2,1)S(1)} %get-tuple-element.160, bf16[512,1408]{1,0:T(8,128)(2,1)S(1)} %get-tuple-element.159), kind=kOutput, calls=%fused_computation.225 | convolution fusion | flops 5911347200 | bytes 16515072 | tf_op jit(solution)/shard_map/dot_general | solution.py:507
  316.2 15.0 %collective-permute-done.34 = bf16[64,2048]{1,0:T(8,128)(2,1)S(1)} collective-permute-done((bf16[64,2048]{1,0:T(8,128)(2,1)S(1)}, bf16[64,2048]{1,0:T(8,128)(2,1)S(1)}, u32[]{:S(2)}, u32[]{:S(2)}) %collective-permute-start.34) | collective-permute-done | bytes 262176 | tf_op jit(solution)/shard_map/ppermute | solution.py:424
  351.7 11.2 %fusion.61 = f32[512,2816]{1,0:T(8,128)} fusion(bf16[512,2048]{1,0:T(8,128)(2,1)S(1)} %constant_dynamic-update-slice_fusion.10, bf16[2048,2816]{1,0:T(8,128)(2,1)} %all-gather.9.cloned.1.call-done), kind=kOutput, calls=%fused_computation.239 | convolution fusion | flops 5905580032 | bytes 19398656 | tf_op jit(solution)/shard_map/dot_general | solution.py:507
  366.9 8.2 %collective-permute-start.33 = (bf16[64,2048]{1,0:T(8,128)(2,1)S(1)}, bf16[64,2048]{1,0:T(8,128)(2,1)S(1)}, u32[]{:S(2)}, u32[]{:S(2)}) collective-permute-start(bf16[64,2048]{1,0:T(8,128)(2,1)S(1)} %slice.419), channel_id=1, source_target_pairs={{0,3},{1,0},{2,1},{3,2},{4,7},{5,4},{6,5},{7,6},{8,11},{9,8},{10,9... | collective-permute-start | bytes 786440 | tf_op jit(solution)/shard_map/ppermute | solution.py:424
  377.1 14.4 %collective-permute-done.32 = bf16[64,2048]{1,0:T(8,128)(2,1)S(1)} collective-permute-done((bf16[64,2048]{1,0:T(8,128)(2,1)S(1)}, bf16[64,2048]{1,0:T(8,128)(2,1)S(1)}, u32[]{:S(2)}, u32[]{:S(2)}) %collective-permute-start.32) | collective-permute-done | bytes 262176 | tf_op jit(solution)/shard_map/ppermute | solution.py:424
  401.4 11.4 %fusion.62 = bf16[512,2048]{1,0:T(8,128)(2,1)} fusion(bf16[512,2816]{1,0:T(8,128)(2,1)S(1)} %pad_maximum_fusion.1, bf16[2048,2816]{1,0:T(8,128)(2,1)} %all-gather.9.cloned.1.call-done), kind=kOutput, calls=%fused_computation.240 | convolution fusion | flops 5905580032 | bytes 16515072 | tf_op jit(solution)/shard_map/dot_general | solution.py:507
  441.3 12.2 %add_convert_fusion = bf16[2048,2816]{1,0:T(8,128)(2,1)} fusion(bf16[2048,2816]{1,0:T(8,128)(2,1)} %fusion.47, bf16[512,2048]{1,0:T(8,128)(2,1)S(1)} %copy-done.19, bf16[512,1408]{1,0:T(8,128)(2,1)S(1)} %copy-done.35, bf16[512,1408]{1,0:T(8,128)(2,1)S(1)} %copy-done.33), kind=kOutput, calls=%fused_computation | convolution fusion | flops 5928648704 | bytes 28049408 | tf_op jit(solution)/shard_map/dot_general | solution.py:507
  470.8 12.0 %collective-permute-done.41 = bf16[128,2048]{1,0:T(8,128)(2,1)S(1)} collective-permute-done((bf16[128,2048]{1,0:T(8,128)(2,1)S(1)}, bf16[128,2048]{1,0:T(8,128)(2,1)S(1)}, u32[]{:S(2)}, u32[]{:S(2)}) %collective-permute-start.41) | collective-permute-done | bytes 524320 | tf_op jit(solution)/shard_map/ppermute | solution.py:424
  488.8 8.9 %fusion.63 = bf16[512,2048]{1,0:T(8,128)(2,1)} fusion(bf16[512,1408]{1,0:T(8,128)(2,1)S(1)} %copy-done.75, bf16[2048,1408]{0,1:T(8,128)(2,1)} %all-gather.11.cloned.1.call-done), kind=kOutput, calls=%fused_computation.241 | convolution fusion | flops 2952790016 | bytes 9306112 | tf_op jit(solution)/shard_map/dot_general | solution.py:507
  517.9 22.5 %mixer_backward.2 = (bf16[512,1664]{1,0:T(8,128)(2,1)}, f32[12,512]{1,0:T(8,128)}, f32[1,128]{1,0:T(1,128)}) custom-call(f32[512,1664]{1,0:T(8,128)} %fusion.53.refs_0_.refs_1_.refs_2_, f32[512,1664]{1,0:T(8,128)} %fusion.53.refs_0_.refs_1_.refs_2_, f32[512,1664]{1,0:T(8,128)} %fusion.53.refs_0_.refs_1_.refs_2_, f32[512,1]{1,0:T(8,128)} %fusion.39.refs_3_, ...), custom_call_target="tpu_custom_call" | custom-call | tf_op jit(solution)/shard_map/mixer_backward/pallas_call | solution.py:373
  574.9 22.6 %mixer_backward.3 = (bf16[512,1664]{1,0:T(8,128)(2,1)}, f32[12,512]{1,0:T(8,128)}, f32[1,128]{1,0:T(1,128)}) custom-call(f32[512,1664]{1,0:T(8,128)} %fusion.55.refs_0_.refs_1_.refs_2_, f32[512,1664]{1,0:T(8,128)} %fusion.55.refs_0_.refs_1_.refs_2_, f32[512,1664]{1,0:T(8,128)} %fusion.55.refs_0_.refs_1_.refs_2_, f32[512,1]{1,0:T(8,128)} %fusion.38.refs_3_, ...), custom_call_target="tpu_custom_call" | custom-call | tf_op jit(solution)/shard_map/mixer_backward/pallas_call | solution.py:373
  601.4 13.2 %pad_add_fusion = bf16[2048,1664]{1,0:T(8,128)(2,1)} fusion(bf16[2048,4]{1,0:T(8,128)(2,1)} %convert_element_type.411, bf16[512,2048]{1,0:T(8,128)(2,1)} %constant_dynamic-update-slice_fusion.30, bf16[512,2048]{1,0:T(8,128)(2,1)} %constant_dynamic-update-slice_fusion.35, bf16[512,1664]{1,0:T(8,128)(2,1)} %get-tuple-element.111, ...), kind=kOutput, calls=%fused_computation.2 | convolution fusion | flops 7008157696 | bytes 14434304 | tf_op jit(solution)/shard_map/dot_general | solution.py:507
  614.6 8.8 %fusion.67 = bf16[512,2048]{1,0:T(8,128)(2,1)} fusion(bf16[512,1664]{1,0:T(8,128)(2,1)} %get-tuple-element.111, bf16[2048,1664]{1,0:T(8,128)(2,1)} %all-gather.5.cloned.1.call-done), kind=kOutput, calls=%fused_computation.245 | convolution fusion | flops 3489660928 | bytes 10616832 | tf_op jit(solution)/shard_map/dot_general | solution.py:507
  (513 shorter events, 384.8 us)
Async XLA Ops:
  7.2 56.1 %all-gather.5.cloned.1.call-start = ((), (), s32[]{:S(2)}) async-start(), calls=%async_computation.4 | async-start | bytes 7667712 | tf_op jit(solution)/shard_map/all_gather | solution.py:513
  12.8 107.3 %all-gather.7.cloned.1.call-start = ((), (), s32[]{:S(2)}) async-start(), calls=%async_computation.5 | async-start | bytes 2359296 | tf_op jit(solution)/shard_map/all_gather | solution.py:513
  13.6 178.5 %all-gather.9.cloned.1.call-start = ((), (), s32[]{:S(2)}) async-start(), calls=%async_computation.6 | async-start | bytes 12976128 | tf_op jit(solution)/shard_map/all_gather | solution.py:513
  17.3 237.3 %all-gather.11.cloned.1.call-start = ((), (), s32[]{:S(2)}) async-start(), calls=%async_computation.7 | async-start | bytes 6488064 | tf_op jit(solution)/shard_map/all_gather | solution.py:513
  23.3 600.1 %reduce-scatter.5.cloned.1.call-start = ((), (), s32[]{:S(2)}) async-start(), calls=%async_computation.8 | async-start | bytes 6488064 | tf_op jit(solution)/shard_map/reduce_scatter | solution.py:517
  63.3 51.2 %collective-permute-start.4 = (bf16[128,2048]{1,0:T(8,128)(2,1)S(1)}, bf16[128,2048]{1,0:T(8,128)(2,1)S(1)}, u32[]{:S(2)}, u32[]{:S(2)}) collective-permute-start(bf16[128,2048]{1,0:T(8,128)(2,1)S(1)} %get-tuple-element.68), channel_id=1, source_target_pairs={{0,1},{1,2},{2,3},{3,0},{4,5},{5,6},{6,7},{7,4},{8,9},{9,10},{10,1... | collective-permute-start | bytes 1572872 | tf_op jit(solution)/shard_map/ppermute | solution.py:424
  64.8 49.9 %collective-permute-start.5 = (bf16[128,2048]{1,0:T(8,128)(2,1)S(1)}, bf16[128,2048]{1,0:T(8,128)(2,1)}, u32[]{:S(2)}, u32[]{:S(2)}) collective-permute-start(bf16[128,2048]{1,0:T(8,128)(2,1)S(1)} %get-tuple-element.68), channel_id=1, source_target_pairs={{0,3},{1,0},{2,1},{3,2},{4,7},{5,4},{6,5},{7,6},{8,11},{9,8},{10,9... | collective-permute-start | bytes 1572872 | tf_op jit(solution)/shard_map/ppermute | solution.py:424
  67.1 53.0 %collective-permute-start.6 = (bf16[128,2048]{1,0:T(8,128)(2,1)}, bf16[128,2048]{1,0:T(8,128)(2,1)}, u32[]{:S(2)}, u32[]{:S(2)}) collective-permute-start(bf16[128,2048]{1,0:T(8,128)(2,1)} %get-tuple-element.69), channel_id=1, source_target_pairs={{0,1},{1,2},{2,3},{3,0},{4,5},{5,6},{6,7},{7,4},{8,9},{9,10},{10,1... | collective-permute-start | bytes 1572872 | tf_op jit(solution)/shard_map/ppermute | solution.py:424
  67.1 53.0 %collective-permute-start.7 = (bf16[128,2048]{1,0:T(8,128)(2,1)}, bf16[128,2048]{1,0:T(8,128)(2,1)}, u32[]{:S(2)}, u32[]{:S(2)}) collective-permute-start(bf16[128,2048]{1,0:T(8,128)(2,1)} %get-tuple-element.69), channel_id=1, source_target_pairs={{0,3},{1,0},{2,1},{3,2},{4,7},{5,4},{6,5},{7,6},{8,11},{9,8},{10,9... | collective-permute-start | bytes 1572872 | tf_op jit(solution)/shard_map/ppermute | solution.py:424
  128.8 53.6 %collective-permute-start.14 = (bf16[64,2048]{1,0:T(8,128)(2,1)}, bf16[64,2048]{1,0:T(8,128)(2,1)}, u32[]{:S(2)}, u32[]{:S(2)}) collective-permute-start(bf16[64,2048]{1,0:T(8,128)(2,1)} %slice.412), channel_id=1, source_target_pairs={{0,1},{1,2},{2,3},{3,0},{4,5},{5,6},{6,7},{7,4},{8,9},{9,10},{10,1... | collective-permute-start | bytes 786440 | tf_op jit(solution)/shard_map/ppermute | solution.py:424
  137.0 47.2 %collective-permute-start.15 = (bf16[64,2048]{1,0:T(8,128)(2,1)}, bf16[64,2048]{1,0:T(8,128)(2,1)}, u32[]{:S(2)}, u32[]{:S(2)}) collective-permute-start(bf16[64,2048]{1,0:T(8,128)(2,1)} %slice.413), channel_id=1, source_target_pairs={{0,3},{1,0},{2,1},{3,2},{4,7},{5,4},{6,5},{7,6},{8,11},{9,8},{10,9... | collective-permute-start | bytes 786440 | tf_op jit(solution)/shard_map/ppermute | solution.py:424
  142.8 43.1 %collective-permute-start.9 = (bf16[128,2048]{1,0:T(8,128)(2,1)S(1)}, bf16[128,2048]{1,0:T(8,128)(2,1)S(1)}, u32[]{:S(2)}, u32[]{:S(2)}) collective-permute-start(bf16[128,2048]{1,0:T(8,128)(2,1)S(1)} %pad_maximum_fusion.5), channel_id=1, source_target_pairs={{0,1},{1,2},{2,3},{3,0},{4,5},{5,6},{6,7},{7,4},{8,9},{9,10},{10,1... | collective-permute-start | bytes 1572872 | tf_op jit(solution)/shard_map/ppermute | solution.py:424
  143.3 42.6 %collective-permute-start.11 = (bf16[128,2048]{1,0:T(8,128)(2,1)S(1)}, bf16[128,2048]{1,0:T(8,128)(2,1)S(1)}, u32[]{:S(2)}, u32[]{:S(2)}) collective-permute-start(bf16[128,2048]{1,0:T(8,128)(2,1)S(1)} %pad_maximum_fusion.6), channel_id=1, source_target_pairs={{0,3},{1,0},{2,1},{3,2},{4,7},{5,4},{6,5},{7,6},{8,11},{9,8},{10,9... | collective-permute-start | bytes 1572872 | tf_op jit(solution)/shard_map/ppermute | solution.py:424
  298.8 64.2 %collective-permute-start.30 = (bf16[128,2048]{1,0:T(8,128)(2,1)S(1)}, bf16[128,2048]{1,0:T(8,128)(2,1)S(1)}, u32[]{:S(2)}, u32[]{:S(2)}) collective-permute-start(bf16[128,2048]{1,0:T(8,128)(2,1)S(1)} %copy-done.23), channel_id=1, source_target_pairs={{0,1},{1,2},{2,3},{3,0},{4,5},{5,6},{6,7},{7,4},{8,9},{9,10},{10,1... | collective-permute-start | bytes 1572872 | tf_op jit(solution)/shard_map/ppermute | solution.py:424
  301.2 65.5 %collective-permute-start.31 = (bf16[128,2048]{1,0:T(8,128)(2,1)S(1)}, bf16[128,2048]{1,0:T(8,128)(2,1)S(1)}, u32[]{:S(2)}, u32[]{:S(2)}) collective-permute-start(bf16[128,2048]{1,0:T(8,128)(2,1)S(1)} %copy-done.23), channel_id=1, source_target_pairs={{0,3},{1,0},{2,1},{3,2},{4,7},{5,4},{6,5},{7,6},{8,11},{9,8},{10,9... | collective-permute-start | bytes 1572872 | tf_op jit(solution)/shard_map/ppermute | solution.py:424
  306.7 35.7 %collective-permute-start.26 = (bf16[64,2048]{1,0:T(8,128)(2,1)S(1)}, bf16[64,2048]{1,0:T(8,128)(2,1)S(1)}, u32[]{:S(2)}, u32[]{:S(2)}) collective-permute-start(bf16[64,2048]{1,0:T(8,128)(2,1)S(1)} %get-tuple-element.196), channel_id=1, source_target_pairs={{0,1},{1,2},{2,3},{3,0},{4,5},{5,6},{6,7},{7,4},{8,9},{9,10},{10,1... | collective-permute-start | bytes 786440 | tf_op jit(solution)/shard_map/ppermute | solution.py:424
  351.5 49.8 %collective-permute-start.28 = (bf16[64,2048]{1,0:T(8,128)(2,1)S(1)}, bf16[64,2048]{1,0:T(8,128)(2,1)S(1)}, u32[]{:S(2)}, u32[]{:S(2)}) collective-permute-start(bf16[64,2048]{1,0:T(8,128)(2,1)S(1)} %get-tuple-element.183), channel_id=1, source_target_pairs={{0,1},{1,2},{2,3},{3,0},{4,5},{5,6},{6,7},{7,4},{8,9},{9,10},{10,1... | collective-permute-start | bytes 786440 | tf_op jit(solution)/shard_map/ppermute | solution.py:424
  363.0 38.4 %collective-permute-start.29 = (bf16[64,2048]{1,0:T(8,128)(2,1)S(1)}, bf16[64,2048]{1,0:T(8,128)(2,1)S(1)}, u32[]{:S(2)}, u32[]{:S(2)}) collective-permute-start(bf16[64,2048]{1,0:T(8,128)(2,1)S(1)} %get-tuple-element.182), channel_id=1, source_target_pairs={{0,3},{1,0},{2,1},{3,2},{4,7},{5,4},{6,5},{7,6},{8,11},{9,8},{10,9... | collective-permute-start | bytes 786440 | tf_op jit(solution)/shard_map/ppermute | solution.py:424
  376.9 35.9 %collective-permute-start.38 = (bf16[128,2048]{1,0:T(8,128)(2,1)S(1)}, bf16[128,2048]{1,0:T(8,128)(2,1)S(1)}, u32[]{:S(2)}, u32[]{:S(2)}) collective-permute-start(bf16[128,2048]{1,0:T(8,128)(2,1)S(1)} %get-tuple-element.151), channel_id=1, source_target_pairs={{0,1},{1,2},{2,3},{3,0},{4,5},{5,6},{6,7},{7,4},{8,9},{9,10},{10,1... | collective-permute-start | bytes 1572872 | tf_op jit(solution)/shard_map/ppermute | solution.py:424
  418.4 205.0 %reduce-scatter.7.cloned.1.call-start = ((), (), s32[]{:S(2)}) async-start(), calls=%async_computation.9 | async-start | bytes 12976128 | tf_op jit(solution)/shard_map/reduce_scatter | solution.py:517
  453.6 176.6 %reduce-scatter.9.cloned.1.call-start = ((), (), s32[]{:S(2)}) async-start(), calls=%async_computation.10 | async-start | bytes 2359296 | tf_op jit(solution)/shard_map/reduce_scatter | solution.py:517
  504.9 35.5 %collective-permute-start.50 = (bf16[64,2048]{1,0:T(8,128)(2,1)}, bf16[64,2048]{1,0:T(8,128)(2,1)}, u32[]{:S(2)}, u32[]{:S(2)}) collective-permute-start(bf16[64,2048]{1,0:T(8,128)(2,1)} %slice.426), channel_id=1, source_target_pairs={{0,1},{1,2},{2,3},{3,0},{4,5},{5,6},{6,7},{7,4},{8,9},{9,10},{10,1... | collective-permute-start | bytes 786440 | tf_op jit(solution)/shard_map/ppermute | solution.py:424
  507.1 34.9 %collective-permute-start.51 = (bf16[64,2048]{1,0:T(8,128)(2,1)}, bf16[64,2048]{1,0:T(8,128)(2,1)}, u32[]{:S(2)}, u32[]{:S(2)}) collective-permute-start(bf16[64,2048]{1,0:T(8,128)(2,1)} %slice.427), channel_id=1, source_target_pairs={{0,3},{1,0},{2,1},{3,2},{4,7},{5,4},{6,5},{7,6},{8,11},{9,8},{10,9... | collective-permute-start | bytes 786440 | tf_op jit(solution)/shard_map/ppermute | solution.py:424
  563.4 118.5 %reduce-scatter.11.cloned.1.call-start = ((), (), s32[]{:S(2)}) async-start(), calls=%async_computation.11 | async-start | bytes 7667712 | tf_op jit(solution)/shard_map/reduce_scatter | solution.py:517
  (135 other events, 1862.6 us)
Sparse Core Ops, SparseCore 0:
  12.9 50.3 all-gather.4
  65.2 28.0 all-gather.6
  95.8 67.6 all-gather.8
  165.2 44.2 all-gather.10
  418.5 58.8 reduce-scatter.4
  480.7 87.0 reduce-scatter.6
  571.1 41.1 reduce-scatter.8
  615.7 64.2 reduce-scatter.10

commit v4 on v3

--- a/solution.py
+++ b/solution.py
@@ -612,6 +612,7 @@
     proj_1 = dot(attn_1, full_proj, 1, 0)
     mixed_1, kept_1, part_1 = mix(1, held(proj_1, first), last, cot_0)
     hidden_0, ffn_in = after_mixer(0, branch)
+    cot_1 = lax.all_gather(held(cotangent[1], full_down, part_1), "tensor", axis=0, tiled=True)
 
     ffn_0, ffn_first, _ = gather_rows(ffn_in, part_1, full_gate_up)
     branch, first, last = scatter_rows(part_1, ffn_first)
@@ -622,7 +623,6 @@
     ffn_1, ffn_first, _ = gather_rows(ffn_in)
     down_0 = dot(held(act_0, part_0), full_down, 1, 1, BF16)
     down_grad = dot(held(cot_0, down_0), act_0, 0, 0, BF16)
-    cot_1, cot_first, _ = gather_rows(cotangent[1], ffn_first)
     pulled, first, last = scatter_rows(part_0, ffn_first)
     gate_up_grad = dot(held(ffn_0, down_grad, ffn_first), grad_gate_up_0, 0, 0, BF16)
     gate_up_1, act_1 = feed(held(ffn_1, first, gate_up_grad))

time: 714 us -> 718 us (level)
  waiting for transfers between devices: 148 us -> 167 us
  starting transfers between devices: 129 us -> 117 us
    all_gather x4, waiting for transfers between devices: 4.47 us -> 21.1 us  [gather_dp(): return lax.all_gather(value, 'dp', axis=0, tiled=True)]
    ppermute x67 -> x63, starting transfers between devices: 129 us -> 116 us  [ring_shift(): lax.ppermute(value, 'tensor', [(place, (place + step) % size) for place i...]
    dynamic_update_slice x40 -> x35, local copies, waits for them, and re-layouts: 32.5 us -> 29.7 us  [put(): lax.dynamic_update_slice(full, piece, (piece_start(step, count) + at, 0))]
    ppermute x67 -> x63, waiting for transfers between devices: 142 us -> 145 us  [ring_shift(): lax.ppermute(value, 'tensor', [(place, (place + step) % size) for place i...]
    unnamed x175 -> x143, local copies, waits for them, and re-layouts: 18.5 us -> 17.9 us
  transfers between devices with their start and end apart: 75 -> 72, of which waited for: 32 -> 30; matrix products, arithmetic and copies ran while one was open for 42% -> 41% of each run, Pallas kernels for 13% -> 13%
where the time goes in v4:
time: 718 us; the launch traced here: 712 us
  matrix products  169 us (24%)
  waiting for transfers between devices  167 us (23%)
  starting transfers between devices  117 us (16%)
  Pallas kernels  94.7 us (13%)
  local copies, waits for them, and re-layouts  92.4 us (13%)
  other arithmetic  54 us (8%)
  between operations  18.4 us (3%)
    dot_general x22, matrix products, dot(): lax.dot_general(left, right, (((left_dim,), (right_dim,)), ((), ())), pre...  169 us
    ppermute x63, waiting for transfers between devices, ring_shift(): lax.ppermute(value, 'tensor', [(place, (place + step) % size) for place i...  145 us
    ppermute x63, starting transfers between devices, ring_shift(): lax.ppermute(value, 'tensor', [(place, (place + step) % size) for place i...  116 us
    pallas_call x2, Pallas kernels, mixer_forward(): pl.pallas_call(lambda *refs: forward_kernel(*refs, heads=heads, head_dim=...  49.3 us
    pallas_call x2, Pallas kernels, mixer_backward(): pl.pallas_call(lambda *refs: backward_kernel(*refs, heads=heads, head_dim...  45.4 us
    dynamic_update_slice x35, local copies, waits for them, and re-layouts, put(): lax.dynamic_update_slice(full, piece, (piece_start(step, count) + at, 0))  29.7 us
    all_gather x4, waiting for transfers between devices, gather_dp(): return lax.all_gather(value, 'dp', axis=0, tiled=True)  21.1 us
    unnamed x143, local copies, waits for them, and re-layouts  17.9 us
  transfers between devices with their start and end apart: 72, of which 30 were waited for; matrix products, arithmetic and copies ran while one was open for 41% of the time, Pallas kernels for 13%

profile of v4, /device:TPU:0, one launch (start us, length us, event | category | flops | bytes accessed | tf_op | source)
XLA Modules:
  0.0 712.1 jit_solution(15099627114026950862)
XLA Ops:
  36.6 10.0 %collective-permute-done.1 = bf16[128,2048]{1,0:T(8,128)(2,1)} collective-permute-done((bf16[128,2048]{1,0:T(8,128)(2,1)S(1)}, bf16[128,2048]{1,0:T(8,128)(2,1)}, u32[]{:S(2)}, u32[]{:S(2)}) %collective-permute-start.1) | collective-permute-done | bytes 524320 | tf_op jit(solution)/shard_map/ppermute | solution.py:424
  71.1 9.4 %fusion.53.refs_0_.refs_1_.refs_2_ = f32[512,1664]{1,0:T(8,128)} fusion(bf16[512,2048]{1,0:T(8,128)(2,1)} %constant_dynamic-update-slice_fusion.30, bf16[2048,1664]{1,0:T(8,128)(2,1)} %all-gather.6.cloned.1.call-done), kind=kOutput, calls=%fused_computation.226 | convolution fusion | flops 3489660928 | bytes 12320768 | tf_op jit(solution)/shard_map/dot_general | solution.py:507
  84.1 24.7 %mixer_forward.2 = (bf16[512,512]{1,0:T(8,128)(2,1)}, f32[512,512]{1,0:T(8,128)}, bf16[8,4,128,128]{3,2,1,0:T(8,128)(2,1)}, bf16[8,256,256]{2,1,0:T(8,128)(2,1)}...) custom-call(f32[512,1664]{1,0:T(8,128)} %fusion.53.refs_0_.refs_1_.refs_2_, ...), custom_call_target="tpu_custom_call" | custom-call | tf_op jit(solution)/shard_map/mixer_forward/pallas_call | solution.py:328
  156.2 24.6 %mixer_forward.3 = (bf16[512,512]{1,0:T(8,128)(2,1)}, f32[512,512]{1,0:T(8,128)}, bf16[8,4,128,128]{3,2,1,0:T(8,128)(2,1)}, bf16[8,256,256]{2,1,0:T(8,128)(2,1)}...) custom-call(f32[512,1664]{1,0:T(8,128)} %fusion.55.refs_0_.refs_1_.refs_2_, ...), custom_call_target="tpu_custom_call" | custom-call | tf_op jit(solution)/shard_map/mixer_forward/pallas_call | solution.py:328
  192.8 16.7 %all-gather.12.cloned.1.call-done = bf16[2048,1408]{0,1:T(8,128)(2,1)} async-done(((bf16[256,1408]{0,1:T(8,128)(2,1)}), bf16[2048,1408]{0,1:T(8,128)(2,1)}) %all-gather.12.cloned.1.call-update) | async-done | bytes 5767184 | tf_op jit(solution)/shard_map/all_gather | solution.py:513
  224.3 14.7 %collective-permute-done.21 = bf16[64,2048]{1,0:T(8,128)(2,1)S(1)} collective-permute-done((bf16[64,2048]{1,0:T(8,128)(2,1)S(1)}, bf16[64,2048]{1,0:T(8,128)(2,1)S(1)}, u32[]{:S(2)}, u32[]{:S(2)}) %collective-permute-start.21) | collective-permute-done | bytes 262176 | tf_op jit(solution)/shard_map/ppermute | solution.py:424
  246.8 11.8 %collective-permute-done.19 = bf16[64,2048]{1,0:T(8,128)(2,1)S(1)} collective-permute-done((bf16[64,2048]{1,0:T(8,128)(2,1)S(1)}, bf16[64,2048]{1,0:T(8,128)(2,1)S(1)}, u32[]{:S(2)}, u32[]{:S(2)}) %collective-permute-start.19) | collective-permute-done | bytes 262176 | tf_op jit(solution)/shard_map/ppermute | solution.py:424
  258.7 11.3 %fusion.57 = f32[512,2816]{1,0:T(8,128)} fusion(bf16[512,2048]{1,0:T(8,128)(2,1)S(1)} %constant_dynamic-update-slice_fusion.15, bf16[2048,2816]{1,0:T(8,128)(2,1)} %all-gather.10.cloned.1.call-done), kind=kOutput, calls=%fused_computation.230 | convolution fusion | flops 5905580032 | bytes 19398656 | tf_op jit(solution)/shard_map/dot_general | solution.py:507
  277.7 12.2 %collective-permute-done.23 = bf16[128,2048]{1,0:T(8,128)(2,1)S(1)} collective-permute-done((bf16[128,2048]{1,0:T(8,128)(2,1)S(1)}, bf16[128,2048]{1,0:T(8,128)(2,1)S(1)}, u32[]{:S(2)}, u32[]{:S(2)}) %collective-permute-start.23) | collective-permute-done | bytes 524320 | tf_op jit(solution)/shard_map/ppermute | solution.py:424
  299.4 9.0 %fusion.58 = bf16[512,2048]{1,0:T(8,128)(2,1)S(1)} fusion(bf16[512,2816]{1,0:T(8,128)(2,1)S(1)} %pad_maximum_fusion, bf16[2048,2816]{1,0:T(8,128)(2,1)} %all-gather.10.cloned.1.call-done), kind=kOutput, calls=%fused_computation.231 | convolution fusion | flops 5905580032 | bytes 16515072 | tf_op jit(solution)/shard_map/dot_general | solution.py:507
  328.6 9.0 %fusion.47 = bf16[2048,2816]{1,0:T(8,128)(2,1)} fusion(bf16[512,2048]{1,0:T(8,128)(2,1)S(1)} %constant_dynamic-update-slice_fusion.15, bf16[512,1408]{1,0:T(8,128)(2,1)S(1)} %get-tuple-element.160, bf16[512,1408]{1,0:T(8,128)(2,1)S(1)} %get-tuple-element.159), kind=kOutput, calls=%fused_computation.220 | convolution fusion | flops 5911347200 | bytes 16515072 | tf_op jit(solution)/shard_map/dot_general | solution.py:507
  353.4 11.1 %fusion.61 = f32[512,2816]{1,0:T(8,128)} fusion(bf16[512,2048]{1,0:T(8,128)(2,1)S(1)} %constant_dynamic-update-slice_fusion.10, bf16[2048,2816]{1,0:T(8,128)(2,1)} %all-gather.10.cloned.1.call-done), kind=kOutput, calls=%fused_computation.234 | convolution fusion | flops 5905580032 | bytes 19398656 | tf_op jit(solution)/shard_map/dot_general | solution.py:507
  364.6 9.4 %multiply_convert_fusion.2 = (bf16[512,1408]{1,0:T(8,128)(2,1)S(1)}, bf16[512,1408]{1,0:T(8,128)(2,1)S(1)}, bf16[512,1408]{1,0:T(8,128)(2,1)S(1)}) fusion(f32[512,2816]{1,0:T(8,128)} %fusion.61, bf16[512,2048]{1,0:T(8,128)(2,1)} %all-gather.14.cloned.1.call-done, bf16[2048,1408]{0,1:T(8,128)(2,1)} %all-gather.12.cloned.1.call-done), kind=kOutput, calls=%fused_computation.20 | convolution fusion | flops 2963603456 | bytes 17956864 | tf_op jit(solution)/shard_map/dot_general | solution.py:507
  384.6 10.0 %fusion.62 = bf16[512,2048]{1,0:T(8,128)(2,1)} fusion(bf16[512,2816]{1,0:T(8,128)(2,1)S(1)} %pad_maximum_fusion.1, bf16[2048,2816]{1,0:T(8,128)(2,1)} %all-gather.10.cloned.1.call-done), kind=kOutput, calls=%fused_computation.235 | convolution fusion | flops 5905580032 | bytes 16515072 | tf_op jit(solution)/shard_map/dot_general | solution.py:507
  420.4 12.8 %collective-permute-done.40 = bf16[64,2048]{1,0:T(8,128)(2,1)S(1)} collective-permute-done((bf16[64,2048]{1,0:T(8,128)(2,1)S(1)}, bf16[64,2048]{1,0:T(8,128)(2,1)S(1)}, u32[]{:S(2)}, u32[]{:S(2)}) %collective-permute-start.40) | collective-permute-done | bytes 262176 | tf_op jit(solution)/shard_map/ppermute | solution.py:424
  437.0 11.6 %add_convert_fusion = bf16[2048,2816]{1,0:T(8,128)(2,1)} fusion(bf16[2048,2816]{1,0:T(8,128)(2,1)} %fusion.47, bf16[512,2048]{1,0:T(8,128)(2,1)S(1)} %copy-done.18, bf16[512,1408]{1,0:T(8,128)(2,1)S(1)} %copy-done.28, bf16[512,1408]{1,0:T(8,128)(2,1)S(1)} %copy-done.26), kind=kOutput, calls=%fused_computation | convolution fusion | flops 5928648704 | bytes 28049408 | tf_op jit(solution)/shard_map/dot_general | solution.py:507
  454.0 10.7 %collective-permute-done.39 = bf16[128,2048]{1,0:T(8,128)(2,1)S(1)} collective-permute-done((bf16[128,2048]{1,0:T(8,128)(2,1)S(1)}, bf16[128,2048]{1,0:T(8,128)(2,1)S(1)}, u32[]{:S(2)}, u32[]{:S(2)}) %collective-permute-start.39) | collective-permute-done | bytes 524320 | tf_op jit(solution)/shard_map/ppermute | solution.py:424
  464.7 10.2 %collective-permute-done.37 = bf16[128,2048]{1,0:T(8,128)(2,1)S(1)} collective-permute-done((bf16[128,2048]{1,0:T(8,128)(2,1)S(1)}, bf16[128,2048]{1,0:T(8,128)(2,1)S(1)}, u32[]{:S(2)}, u32[]{:S(2)}) %collective-permute-start.37) | collective-permute-done | bytes 524320 | tf_op jit(solution)/shard_map/ppermute | solution.py:424
  479.9 8.9 %fusion.63 = bf16[512,2048]{1,0:T(8,128)(2,1)} fusion(bf16[512,1408]{1,0:T(8,128)(2,1)S(1)} %copy-done.61, bf16[2048,1408]{0,1:T(8,128)(2,1)} %all-gather.12.cloned.1.call-done), kind=kOutput, calls=%fused_computation.236 | convolution fusion | flops 2952790016 | bytes 9306112 | tf_op jit(solution)/shard_map/dot_general | solution.py:507
  513.0 22.7 %mixer_backward.2 = (bf16[512,1664]{1,0:T(8,128)(2,1)}, f32[12,512]{1,0:T(8,128)}, f32[1,128]{1,0:T(1,128)}) custom-call(f32[512,1664]{1,0:T(8,128)} %fusion.53.refs_0_.refs_1_.refs_2_, f32[512,1664]{1,0:T(8,128)} %fusion.53.refs_0_.refs_1_.refs_2_, f32[512,1664]{1,0:T(8,128)} %fusion.53.refs_0_.refs_1_.refs_2_, f32[512,1]{1,0:T(8,128)} %fusion.39.refs_3_, ...), custom_call_target="tpu_custom_call" | custom-call | tf_op jit(solution)/shard_map/mixer_backward/pallas_call | solution.py:373
  570.5 22.7 %mixer_backward.3 = (bf16[512,1664]{1,0:T(8,128)(2,1)}, f32[12,512]{1,0:T(8,128)}, f32[1,128]{1,0:T(1,128)}) custom-call(f32[512,1664]{1,0:T(8,128)} %fusion.55.refs_0_.refs_1_.refs_2_, f32[512,1664]{1,0:T(8,128)} %fusion.55.refs_0_.refs_1_.refs_2_, f32[512,1664]{1,0:T(8,128)} %fusion.55.refs_0_.refs_1_.refs_2_, f32[512,1]{1,0:T(8,128)} %fusion.38.refs_3_, ...), custom_call_target="tpu_custom_call" | custom-call | tf_op jit(solution)/shard_map/mixer_backward/pallas_call | solution.py:373
  596.9 12.8 %pad_add_fusion = bf16[2048,1664]{1,0:T(8,128)(2,1)} fusion(bf16[2048,4]{1,0:T(8,128)(2,1)} %convert_element_type.411, bf16[512,2048]{1,0:T(8,128)(2,1)} %copy-done.16, bf16[512,2048]{1,0:T(8,128)(2,1)} %constant_dynamic-update-slice_fusion.30, bf16[512,1664]{1,0:T(8,128)(2,1)} %get-tuple-element.111, bf16[512,1664]{1,0:T(8,128)(2,1)} %get-tuple-element.106), kind=kOutput, calls=%fused_computation.2 | convolution fusion | flops 7008157696 | bytes 14434304 | tf_op jit(solution)/shard_map/dot_general | solution.py:507
  609.7 8.8 %fusion.67 = bf16[512,2048]{1,0:T(8,128)(2,1)} fusion(bf16[512,1664]{1,0:T(8,128)(2,1)} %get-tuple-element.111, bf16[2048,1664]{1,0:T(8,128)(2,1)} %all-gather.6.cloned.1.call-done), kind=kOutput, calls=%fused_computation.240 | convolution fusion | flops 3489660928 | bytes 10616832 | tf_op jit(solution)/shard_map/dot_general | solution.py:507
  627.3 9.4 %collective-permute-done.54 = bf16[64,2048]{1,0:T(8,128)(2,1)} collective-permute-done((bf16[64,2048]{1,0:T(8,128)(2,1)}, bf16[64,2048]{1,0:T(8,128)(2,1)}, u32[]{:S(2)}, u32[]{:S(2)}) %collective-permute-start.54) | collective-permute-done | bytes 262176 | tf_op jit(solution)/shard_map/ppermute | solution.py:424
  (467 shorter events, 379.2 us)
Async XLA Ops:
  7.2 56.1 %all-gather.6.cloned.1.call-start = ((), (), s32[]{:S(2)}) async-start(), calls=%async_computation.4 | async-start | bytes 7667712 | tf_op jit(solution)/shard_map/all_gather | solution.py:513
  12.8 107.9 %all-gather.8.cloned.1.call-start = ((), (), s32[]{:S(2)}) async-start(), calls=%async_computation.5 | async-start | bytes 2359296 | tf_op jit(solution)/shard_map/all_gather | solution.py:513
  13.6 175.3 %all-gather.10.cloned.1.call-start = ((), (), s32[]{:S(2)}) async-start(), calls=%async_computation.6 | async-start | bytes 12976128 | tf_op jit(solution)/shard_map/all_gather | solution.py:513
  17.3 192.2 %all-gather.12.cloned.1.call-start = ((), (), s32[]{:S(2)}) async-start(), calls=%async_computation.7 | async-start | bytes 6488064 | tf_op jit(solution)/shard_map/all_gather | solution.py:513
  23.7 340.9 %all-gather.14.cloned.1.call-start = ((), (), s32[]{:S(2)}) async-start(), calls=%async_computation.8 | async-start | bytes 2621440 | tf_op jit(solution)/shard_map/all_gather | solution.py:615
  63.3 50.3 %collective-permute-start.4 = (bf16[128,2048]{1,0:T(8,128)(2,1)}, bf16[128,2048]{1,0:T(8,128)(2,1)}, u32[]{:S(2)}, u32[]{:S(2)}) collective-permute-start(bf16[128,2048]{1,0:T(8,128)(2,1)} %get-tuple-element.68), channel_id=1, source_target_pairs={{0,1},{1,2},{2,3},{3,0},{4,5},{5,6},{6,7},{7,4},{8,9},{9,10},{10,1... | collective-permute-start | bytes 1572872 | tf_op jit(solution)/shard_map/ppermute | solution.py:424
  64.8 50.5 %collective-permute-start.5 = (bf16[128,2048]{1,0:T(8,128)(2,1)}, bf16[128,2048]{1,0:T(8,128)(2,1)}, u32[]{:S(2)}, u32[]{:S(2)}) collective-permute-start(bf16[128,2048]{1,0:T(8,128)(2,1)} %get-tuple-element.68), channel_id=1, source_target_pairs={{0,3},{1,0},{2,1},{3,2},{4,7},{5,4},{6,5},{7,6},{8,11},{9,8},{10,9... | collective-permute-start | bytes 1572872 | tf_op jit(solution)/shard_map/ppermute | solution.py:424
  67.1 53.6 %collective-permute-start.6 = (bf16[128,2048]{1,0:T(8,128)(2,1)}, bf16[128,2048]{1,0:T(8,128)(2,1)}, u32[]{:S(2)}, u32[]{:S(2)}) collective-permute-start(bf16[128,2048]{1,0:T(8,128)(2,1)} %get-tuple-element.69), channel_id=1, source_target_pairs={{0,1},{1,2},{2,3},{3,0},{4,5},{5,6},{6,7},{7,4},{8,9},{9,10},{10,1... | collective-permute-start | bytes 1572872 | tf_op jit(solution)/shard_map/ppermute | solution.py:424
  67.1 53.6 %collective-permute-start.7 = (bf16[128,2048]{1,0:T(8,128)(2,1)}, bf16[128,2048]{1,0:T(8,128)(2,1)}, u32[]{:S(2)}, u32[]{:S(2)}) collective-permute-start(bf16[128,2048]{1,0:T(8,128)(2,1)} %get-tuple-element.69), channel_id=1, source_target_pairs={{0,3},{1,0},{2,1},{3,2},{4,7},{5,4},{6,5},{7,6},{8,11},{9,8},{10,9... | collective-permute-start | bytes 1572872 | tf_op jit(solution)/shard_map/ppermute | solution.py:424
  129.7 51.2 %collective-permute-start.14 = (bf16[64,2048]{1,0:T(8,128)(2,1)}, bf16[64,2048]{1,0:T(8,128)(2,1)}, u32[]{:S(2)}, u32[]{:S(2)}) collective-permute-start(bf16[64,2048]{1,0:T(8,128)(2,1)} %slice.404), channel_id=1, source_target_pairs={{0,1},{1,2},{2,3},{3,0},{4,5},{5,6},{6,7},{7,4},{8,9},{9,10},{10,1... | collective-permute-start | bytes 786440 | tf_op jit(solution)/shard_map/ppermute | solution.py:424
  137.7 45.0 %collective-permute-start.15 = (bf16[64,2048]{1,0:T(8,128)(2,1)}, bf16[64,2048]{1,0:T(8,128)(2,1)}, u32[]{:S(2)}, u32[]{:S(2)}) collective-permute-start(bf16[64,2048]{1,0:T(8,128)(2,1)} %slice.405), channel_id=1, source_target_pairs={{0,3},{1,0},{2,1},{3,2},{4,7},{5,4},{6,5},{7,6},{8,11},{9,8},{10,9... | collective-permute-start | bytes 786440 | tf_op jit(solution)/shard_map/ppermute | solution.py:424
  144.3 40.0 %collective-permute-start.9 = (bf16[128,2048]{1,0:T(8,128)(2,1)}, bf16[128,2048]{1,0:T(8,128)(2,1)}, u32[]{:S(2)}, u32[]{:S(2)}) collective-permute-start(bf16[128,2048]{1,0:T(8,128)(2,1)} %pad_maximum_fusion.5), channel_id=1, source_target_pairs={{0,1},{1,2},{2,3},{3,0},{4,5},{5,6},{6,7},{7,4},{8,9},{9,10},{10,1... | collective-permute-start | bytes 1572872 | tf_op jit(solution)/shard_map/ppermute | solution.py:424
  145.7 38.6 %collective-permute-start.11 = (bf16[128,2048]{1,0:T(8,128)(2,1)}, bf16[128,2048]{1,0:T(8,128)(2,1)}, u32[]{:S(2)}, u32[]{:S(2)}) collective-permute-start(bf16[128,2048]{1,0:T(8,128)(2,1)} %pad_maximum_fusion.6), channel_id=1, source_target_pairs={{0,3},{1,0},{2,1},{3,2},{4,7},{5,4},{6,5},{7,6},{8,11},{9,8},{10,9... | collective-permute-start | bytes 1572872 | tf_op jit(solution)/shard_map/ppermute | solution.py:424
  209.5 409.0 %reduce-scatter.5.cloned.1.call-start = ((), (), s32[]{:S(2)}) async-start(), calls=%async_computation.9 | async-start | bytes 6488064 | tf_op jit(solution)/shard_map/reduce_scatter | solution.py:517
  218.0 40.7 %collective-permute-start.19 = (bf16[64,2048]{1,0:T(8,128)(2,1)S(1)}, bf16[64,2048]{1,0:T(8,128)(2,1)S(1)}, u32[]{:S(2)}, u32[]{:S(2)}) collective-permute-start(bf16[64,2048]{1,0:T(8,128)(2,1)S(1)} %slice.407), channel_id=1, source_target_pairs={{0,3},{1,0},{2,1},{3,2},{4,7},{5,4},{6,5},{7,6},{8,11},{9,8},{10,9... | collective-permute-start | bytes 786440 | tf_op jit(solution)/shard_map/ppermute | solution.py:424
  239.2 50.8 %collective-permute-start.23 = (bf16[128,2048]{1,0:T(8,128)(2,1)S(1)}, bf16[128,2048]{1,0:T(8,128)(2,1)S(1)}, u32[]{:S(2)}, u32[]{:S(2)}) collective-permute-start(bf16[128,2048]{1,0:T(8,128)(2,1)S(1)} %pad_maximum_fusion.8), channel_id=1, source_target_pairs={{0,3},{1,0},{2,1},{3,2},{4,7},{5,4},{6,5},{7,6},{8,11},{9,8},{10,9... | collective-permute-start | bytes 1572872 | tf_op jit(solution)/shard_map/ppermute | solution.py:424
  239.3 55.4 %collective-permute-start.22 = (bf16[128,2048]{1,0:T(8,128)(2,1)S(1)}, bf16[128,2048]{1,0:T(8,128)(2,1)S(1)}, u32[]{:S(2)}, u32[]{:S(2)}) collective-permute-start(bf16[128,2048]{1,0:T(8,128)(2,1)S(1)} %pad_maximum_fusion.7), channel_id=1, source_target_pairs={{0,1},{1,2},{2,3},{3,0},{4,5},{5,6},{6,7},{7,4},{8,9},{9,10},{10,1... | collective-permute-start | bytes 1572872 | tf_op jit(solution)/shard_map/ppermute | solution.py:424
  349.6 35.0 %collective-permute-start.28 = (bf16[64,2048]{1,0:T(8,128)(2,1)}, bf16[64,2048]{1,0:T(8,128)(2,1)}, u32[]{:S(2)}, u32[]{:S(2)}) collective-permute-start(bf16[64,2048]{1,0:T(8,128)(2,1)} %get-tuple-element.183), channel_id=1, source_target_pairs={{0,1},{1,2},{2,3},{3,0},{4,5},{5,6},{6,7},{7,4},{8,9},{9,10},{10,1... | collective-permute-start | bytes 786440 | tf_op jit(solution)/shard_map/ppermute | solution.py:424
  349.6 35.0 %collective-permute-start.29 = (bf16[64,2048]{1,0:T(8,128)(2,1)}, bf16[64,2048]{1,0:T(8,128)(2,1)}, u32[]{:S(2)}, u32[]{:S(2)}) collective-permute-start(bf16[64,2048]{1,0:T(8,128)(2,1)} %get-tuple-element.182), channel_id=1, source_target_pairs={{0,3},{1,0},{2,1},{3,2},{4,7},{5,4},{6,5},{7,6},{8,11},{9,8},{10,9... | collective-permute-start | bytes 786440 | tf_op jit(solution)/shard_map/ppermute | solution.py:424
  408.3 210.2 %reduce-scatter.7.cloned.1.call-start = ((), (), s32[]{:S(2)}) async-start(), calls=%async_computation.10 | async-start | bytes 12976128 | tf_op jit(solution)/shard_map/reduce_scatter | solution.py:517
  448.7 176.6 %reduce-scatter.9.cloned.1.call-start = ((), (), s32[]{:S(2)}) async-start(), calls=%async_computation.11 | async-start | bytes 2359296 | tf_op jit(solution)/shard_map/reduce_scatter | solution.py:517
  495.8 40.0 %collective-permute-start.46 = (bf16[64,2048]{1,0:T(8,128)(2,1)}, bf16[64,2048]{1,0:T(8,128)(2,1)}, u32[]{:S(2)}, u32[]{:S(2)}) collective-permute-start(bf16[64,2048]{1,0:T(8,128)(2,1)} %slice.416), channel_id=1, source_target_pairs={{0,1},{1,2},{2,3},{3,0},{4,5},{5,6},{6,7},{7,4},{8,9},{9,10},{10,1... | collective-permute-start | bytes 786440 | tf_op jit(solution)/shard_map/ppermute | solution.py:424
  500.5 37.0 %collective-permute-start.47 = (bf16[64,2048]{1,0:T(8,128)(2,1)}, bf16[64,2048]{1,0:T(8,128)(2,1)}, u32[]{:S(2)}, u32[]{:S(2)}) collective-permute-start(bf16[64,2048]{1,0:T(8,128)(2,1)} %slice.417), channel_id=1, source_target_pairs={{0,3},{1,0},{2,1},{3,2},{4,7},{5,4},{6,5},{7,6},{8,11},{9,8},{10,9... | collective-permute-start | bytes 786440 | tf_op jit(solution)/shard_map/ppermute | solution.py:424
  559.1 125.3 %reduce-scatter.11.cloned.1.call-start = ((), (), s32[]{:S(2)}) async-start(), calls=%async_computation.12 | async-start | bytes 7667712 | tf_op jit(solution)/shard_map/reduce_scatter | solution.py:517
  (116 other events, 1669.0 us)
Sparse Core Ops, SparseCore 0:
  12.9 50.3 all-gather.5
  65.2 28.0 all-gather.7
  95.8 67.6 all-gather.9
  165.2 44.2 all-gather.11
  211.5 75.7 all-gather.13
  408.4 58.9 reduce-scatter.4
  470.9 87.0 reduce-scatter.6
  561.4 41.1 reduce-scatter.8
  609.8 62.5 reduce-scatter.10

commit v5 on v4

--- a/solution.py
+++ b/solution.py
@@ -612,12 +612,12 @@
     proj_1 = dot(attn_1, full_proj, 1, 0)
     mixed_1, kept_1, part_1 = mix(1, held(proj_1, first), last, cot_0)
     hidden_0, ffn_in = after_mixer(0, branch)
-    cot_1 = lax.all_gather(held(cotangent[1], full_down, part_1), "tensor", axis=0, tiled=True)
 
     ffn_0, ffn_first, _ = gather_rows(ffn_in, part_1, full_gate_up)
     branch, first, last = scatter_rows(part_1, ffn_first)
     gate_up_0, act_0 = feed(held(ffn_0, first))
     grad_gate_up_0, part_0 = feed_back(gate_up_0, cot_0, last)
+    cot_1 = lax.all_gather(held(cotangent[1], gate_up_0), "tensor", axis=0, tiled=True)
     hidden_1, ffn_in = after_mixer(1, branch)
 
     ffn_1, ffn_first, _ = gather_rows(ffn_in)

time: 718 us -> 719 us (level)
  waiting for transfers between devices: 167 us -> 136 us
  starting transfers between devices: 117 us -> 144 us
    ppermute x63, starting transfers between devices: 116 us -> 143 us  [ring_shift(): lax.ppermute(value, 'tensor', [(place, (place + step) % size) for place i...]
    all_gather x4, waiting for transfers between devices: 21.1 us -> 4.41 us  [gather_dp(): return lax.all_gather(value, 'dp', axis=0, tiled=True)]
    ppermute x63, waiting for transfers between devices: 145 us -> 131 us  [ring_shift(): lax.ppermute(value, 'tensor', [(place, (place + step) % size) for place i...]
    unnamed x143 -> x137, local copies, waits for them, and re-layouts: 17.9 us -> 14.3 us
  transfers between devices with their start and end apart: 72 -> 72, of which waited for: 30 -> 33; matrix products, arithmetic and copies ran while one was open for 41% -> 42% of each run, Pallas kernels for 13% -> 13%
where the time goes in v5:
time: 719 us; the launch traced here: 710 us
  matrix products  173 us (24%)
  starting transfers between devices  144 us (20%)
  waiting for transfers between devices  136 us (19%)
  Pallas kernels  94.3 us (13%)
  local copies, waits for them, and re-layouts  89.1 us (12%)
  other arithmetic  54.9 us (8%)
  between operations  18.1 us (3%)
    dot_general x22, matrix products, dot(): lax.dot_general(left, right, (((left_dim,), (right_dim,)), ((), ())), pre...  173 us
    ppermute x63, starting transfers between devices, ring_shift(): lax.ppermute(value, 'tensor', [(place, (place + step) % size) for place i...  143 us
    ppermute x63, waiting for transfers between devices, ring_shift(): lax.ppermute(value, 'tensor', [(place, (place + step) % size) for place i...  131 us
    pallas_call x2, Pallas kernels, mixer_forward(): pl.pallas_call(lambda *refs: forward_kernel(*refs, heads=heads, head_dim=...  49.2 us
    pallas_call x2, Pallas kernels, mixer_backward(): pl.pallas_call(lambda *refs: backward_kernel(*refs, heads=heads, head_dim...  45.1 us
    dynamic_update_slice x35, local copies, waits for them, and re-layouts, put(): lax.dynamic_update_slice(full, piece, (piece_start(step, count) + at, 0))  29.9 us
  transfers between devices with their start and end apart: 72, of which 33 were waited for; matrix products, arithmetic and copies ran while one was open for 42% of the time, Pallas kernels for 13%

profile of v5, /device:TPU:0, one launch (start us, length us, event | category | flops | bytes accessed | tf_op | source)
XLA Modules:
  0.0 709.8 jit_solution(2358507728292946052)
XLA Ops:
  36.6 10.0 %collective-permute-done.1 = bf16[128,2048]{1,0:T(8,128)(2,1)} collective-permute-done((bf16[128,2048]{1,0:T(8,128)(2,1)S(1)}, bf16[128,2048]{1,0:T(8,128)(2,1)}, u32[]{:S(2)}, u32[]{:S(2)}) %collective-permute-start.1) | collective-permute-done | bytes 524320 | tf_op jit(solution)/shard_map/ppermute | solution.py:424
  71.5 9.4 %fusion.53.refs_0_.refs_1_.refs_2_ = f32[512,1664]{1,0:T(8,128)} fusion(bf16[512,2048]{1,0:T(8,128)(2,1)} %constant_dynamic-update-slice_fusion.30, bf16[2048,1664]{1,0:T(8,128)(2,1)} %all-gather.6.cloned.1.call-done), kind=kOutput, calls=%fused_computation.226 | convolution fusion | flops 3489660928 | bytes 12320768 | tf_op jit(solution)/shard_map/dot_general | solution.py:507
  84.4 24.6 %mixer_forward.2 = (bf16[512,512]{1,0:T(8,128)(2,1)}, f32[512,512]{1,0:T(8,128)}, bf16[8,4,128,128]{3,2,1,0:T(8,128)(2,1)}, bf16[8,256,256]{2,1,0:T(8,128)(2,1)}...) custom-call(f32[512,1664]{1,0:T(8,128)} %fusion.53.refs_0_.refs_1_.refs_2_, ...), custom_call_target="tpu_custom_call" | custom-call | tf_op jit(solution)/shard_map/mixer_forward/pallas_call | solution.py:328
  156.2 24.6 %mixer_forward.3 = (bf16[512,512]{1,0:T(8,128)(2,1)}, f32[512,512]{1,0:T(8,128)}, bf16[8,4,128,128]{3,2,1,0:T(8,128)(2,1)}, bf16[8,256,256]{2,1,0:T(8,128)(2,1)}...) custom-call(f32[512,1664]{1,0:T(8,128)} %fusion.55.refs_0_.refs_1_.refs_2_, ...), custom_call_target="tpu_custom_call" | custom-call | tf_op jit(solution)/shard_map/mixer_forward/pallas_call | solution.py:328
  193.1 12.5 %collective-permute-done.16 = bf16[128,2048]{1,0:T(8,128)(2,1)S(1)} collective-permute-done((bf16[128,2048]{1,0:T(8,128)(2,1)S(1)}, bf16[128,2048]{1,0:T(8,128)(2,1)S(1)}, u32[]{:S(2)}, u32[]{:S(2)}) %collective-permute-start.16) | collective-permute-done | bytes 524320 | tf_op jit(solution)/shard_map/ppermute | solution.py:424
  238.3 11.9 %fusion.57 = f32[512,2816]{1,0:T(8,128)} fusion(bf16[512,2048]{1,0:T(8,128)(2,1)S(1)} %constant_dynamic-update-slice_fusion.15, bf16[2048,2816]{1,0:T(8,128)(2,1)} %all-gather.10.cloned.1.call-done), kind=kOutput, calls=%fused_computation.230 | convolution fusion | flops 5905580032 | bytes 19398656 | tf_op jit(solution)/shard_map/dot_general | solution.py:507
  250.5 9.4 %multiply_convert_fusion.4 = (bf16[512,1408]{1,0:T(8,128)(2,1)S(1)}, bf16[512,1408]{1,0:T(8,128)(2,1)S(1)}, bf16[512,1408]{1,0:T(8,128)(2,1)S(1)}) fusion(f32[512,2816]{1,0:T(8,128)} %fusion.57, bf16[512,2048]{1,0:T(8,128)(2,1)} %constant_dynamic-update-slice_fusion.20, bf16[2048,1408]{0,1:T(8,128)(2,1)} %all-gather.12.cloned.1.call-done), kind=kOutput, calls=%fused_computation.24 | convolution fusion | flops 2963603456 | bytes 17956864 | tf_op jit(solution)/shard_map/dot_general | solution.py:507
  262.7 8.2 %collective-permute-start.24 = (bf16[128,2048]{1,0:T(8,128)(2,1)S(1)}, bf16[128,2048]{1,0:T(8,128)(2,1)S(1)}, u32[]{:S(2)}, u32[]{:S(2)}) collective-permute-start(bf16[128,2048]{1,0:T(8,128)(2,1)S(1)} %multiply_convert_fusion.7), channel_id=1, source_target_pairs={{0,1},{1,2},{2,3},{3,0},{4,5},{5,6},{6,7},{7,4},{8,9},{9,10},{10,1... | collective-permute-start | bytes 1572872 | tf_op jit(solution)/shard_map/ppermute | solution.py:424
  271.3 9.2 %fusion.58 = bf16[512,2048]{1,0:T(8,128)(2,1)S(1)} fusion(bf16[512,2816]{1,0:T(8,128)(2,1)S(1)} %pad_maximum_fusion, bf16[2048,2816]{1,0:T(8,128)(2,1)} %all-gather.10.cloned.1.call-done), kind=kOutput, calls=%fused_computation.231 | convolution fusion | flops 5905580032 | bytes 16515072 | tf_op jit(solution)/shard_map/dot_general | solution.py:507
  284.1 8.3 %fusion.60 = bf16[2048,1408]{1,0:T(8,128)(2,1)} fusion(bf16[512,2048]{1,0:T(8,128)(2,1)} %constant_dynamic-update-slice_fusion.20, bf16[512,1408]{1,0:T(8,128)(2,1)S(1)} %get-tuple-element.78), kind=kOutput, calls=%fused_computation.233 | convolution fusion | flops 2952790016 | bytes 9306112 | tf_op jit(solution)/shard_map/dot_general | solution.py:507
  294.5 23.2 %collective-permute-start.30 = (bf16[64,2048]{1,0:T(8,128)(2,1)S(1)}, bf16[64,2048]{1,0:T(8,128)(2,1)S(1)}, u32[]{:S(2)}, u32[]{:S(2)}) collective-permute-start(bf16[64,2048]{1,0:T(8,128)(2,1)S(1)} %slice.410), channel_id=1, source_target_pairs={{0,1},{1,2},{2,3},{3,0},{4,5},{5,6},{6,7},{7,4},{8,9},{9,10},{10,1... | collective-permute-start | bytes 786440 | tf_op jit(solution)/shard_map/ppermute | solution.py:424
  325.1 9.0 %fusion.47 = bf16[2048,2816]{1,0:T(8,128)(2,1)} fusion(bf16[512,2048]{1,0:T(8,128)(2,1)S(1)} %copy-done.16, bf16[512,1408]{1,0:T(8,128)(2,1)S(1)} %get-tuple-element.160, bf16[512,1408]{1,0:T(8,128)(2,1)S(1)} %get-tuple-element.159), kind=kOutput, calls=%fused_computation.220 | convolution fusion | flops 5911347200 | bytes 16515072 | tf_op jit(solution)/shard_map/dot_general | solution.py:507
  352.2 11.1 %fusion.61 = f32[512,2816]{1,0:T(8,128)} fusion(bf16[512,2048]{1,0:T(8,128)(2,1)S(1)} %constant_dynamic-update-slice_fusion.10, bf16[2048,2816]{1,0:T(8,128)(2,1)} %all-gather.10.cloned.1.call-done), kind=kOutput, calls=%fused_computation.234 | convolution fusion | flops 5905580032 | bytes 19398656 | tf_op jit(solution)/shard_map/dot_general | solution.py:507
  363.3 8.1 %collective-permute-done.33 = bf16[128,2048]{1,0:T(8,128)(2,1)S(1)} collective-permute-done((bf16[128,2048]{1,0:T(8,128)(2,1)S(1)}, bf16[128,2048]{1,0:T(8,128)(2,1)S(1)}, u32[]{:S(2)}, u32[]{:S(2)}) %collective-permute-start.33) | collective-permute-done | bytes 524320 | tf_op jit(solution)/shard_map/ppermute | solution.py:424
  377.3 9.4 %multiply_convert_fusion.2 = (bf16[512,1408]{1,0:T(8,128)(2,1)S(1)}, bf16[512,1408]{1,0:T(8,128)(2,1)S(1)}, bf16[512,1408]{1,0:T(8,128)(2,1)S(1)}) fusion(f32[512,2816]{1,0:T(8,128)} %fusion.61, bf16[512,2048]{1,0:T(8,128)(2,1)} %all-gather.14.cloned.1.call-done, bf16[2048,1408]{0,1:T(8,128)(2,1)} %all-gather.12.cloned.1.call-done), kind=kOutput, calls=%fused_computation.20 | convolution fusion | flops 2963603456 | bytes 17956864 | tf_op jit(solution)/shard_map/dot_general | solution.py:507
  388.2 11.3 %fusion.62 = bf16[512,2048]{1,0:T(8,128)(2,1)} fusion(bf16[512,2816]{1,0:T(8,128)(2,1)S(1)} %pad_maximum_fusion.1, bf16[2048,2816]{1,0:T(8,128)(2,1)} %all-gather.10.cloned.1.call-done), kind=kOutput, calls=%fused_computation.235 | convolution fusion | flops 5905580032 | bytes 16515072 | tf_op jit(solution)/shard_map/dot_general | solution.py:507
  434.6 11.6 %add_convert_fusion = bf16[2048,2816]{1,0:T(8,128)(2,1)} fusion(bf16[2048,2816]{1,0:T(8,128)(2,1)} %fusion.47, bf16[512,2048]{1,0:T(8,128)(2,1)S(1)} %copy-done.18, bf16[512,1408]{1,0:T(8,128)(2,1)S(1)} %copy-done.27, bf16[512,1408]{1,0:T(8,128)(2,1)S(1)} %copy-done.25), kind=kOutput, calls=%fused_computation | convolution fusion | flops 5928648704 | bytes 28049408 | tf_op jit(solution)/shard_map/dot_general | solution.py:507
  451.9 21.1 %collective-permute-done.39 = bf16[128,2048]{1,0:T(8,128)(2,1)S(1)} collective-permute-done((bf16[128,2048]{1,0:T(8,128)(2,1)S(1)}, bf16[128,2048]{1,0:T(8,128)(2,1)S(1)}, u32[]{:S(2)}, u32[]{:S(2)}) %collective-permute-start.39) | collective-permute-done | bytes 524320 | tf_op jit(solution)/shard_map/ppermute | solution.py:424
  477.7 8.8 %fusion.63 = bf16[512,2048]{1,0:T(8,128)(2,1)} fusion(bf16[512,1408]{1,0:T(8,128)(2,1)S(1)} %copy-done.58, bf16[2048,1408]{0,1:T(8,128)(2,1)} %all-gather.12.cloned.1.call-done), kind=kOutput, calls=%fused_computation.236 | convolution fusion | flops 2952790016 | bytes 9306112 | tf_op jit(solution)/shard_map/dot_general | solution.py:507
  512.3 22.5 %mixer_backward.2 = (bf16[512,1664]{1,0:T(8,128)(2,1)}, f32[12,512]{1,0:T(8,128)}, f32[1,128]{1,0:T(1,128)}) custom-call(f32[512,1664]{1,0:T(8,128)} %fusion.53.refs_0_.refs_1_.refs_2_, f32[512,1664]{1,0:T(8,128)} %fusion.53.refs_0_.refs_1_.refs_2_, f32[512,1664]{1,0:T(8,128)} %fusion.53.refs_0_.refs_1_.refs_2_, f32[512,1]{1,0:T(8,128)} %fusion.39.refs_3_, ...), custom_call_target="tpu_custom_call" | custom-call | tf_op jit(solution)/shard_map/mixer_backward/pallas_call | solution.py:373
  569.3 22.6 %mixer_backward.3 = (bf16[512,1664]{1,0:T(8,128)(2,1)}, f32[12,512]{1,0:T(8,128)}, f32[1,128]{1,0:T(1,128)}) custom-call(f32[512,1664]{1,0:T(8,128)} %fusion.55.refs_0_.refs_1_.refs_2_, f32[512,1664]{1,0:T(8,128)} %fusion.55.refs_0_.refs_1_.refs_2_, f32[512,1664]{1,0:T(8,128)} %fusion.55.refs_0_.refs_1_.refs_2_, f32[512,1]{1,0:T(8,128)} %fusion.38.refs_3_, ...), custom_call_target="tpu_custom_call" | custom-call | tf_op jit(solution)/shard_map/mixer_backward/pallas_call | solution.py:373
  595.8 12.8 %pad_add_fusion = bf16[2048,1664]{1,0:T(8,128)(2,1)} fusion(bf16[2048,4]{1,0:T(8,128)(2,1)} %convert_element_type.411, bf16[512,2048]{1,0:T(8,128)(2,1)} %copy-done.14, bf16[512,2048]{1,0:T(8,128)(2,1)} %constant_dynamic-update-slice_fusion.30, bf16[512,1664]{1,0:T(8,128)(2,1)} %get-tuple-element.111, bf16[512,1664]{1,0:T(8,128)(2,1)} %get-tuple-element.106), kind=kOutput, calls=%fused_computation.2 | convolution fusion | flops 7008157696 | bytes 14434304 | tf_op jit(solution)/shard_map/dot_general | solution.py:507
  608.6 9.3 %fusion.67 = bf16[512,2048]{1,0:T(8,128)(2,1)} fusion(bf16[512,1664]{1,0:T(8,128)(2,1)} %get-tuple-element.111, bf16[2048,1664]{1,0:T(8,128)(2,1)} %all-gather.6.cloned.1.call-done), kind=kOutput, calls=%fused_computation.240 | convolution fusion | flops 3489660928 | bytes 10616832 | tf_op jit(solution)/shard_map/dot_general | solution.py:507
  685.4 8.9 %collective-permute-done.58 = bf16[128,2048]{1,0:T(8,128)(2,1)} collective-permute-done((bf16[128,2048]{1,0:T(8,128)(2,1)S(1)}, bf16[128,2048]{1,0:T(8,128)(2,1)}, u32[]{:S(2)}, u32[]{:S(2)}) %collective-permute-start.58) | collective-permute-done | bytes 524320 | tf_op jit(solution)/shard_map/ppermute | solution.py:424
  (461 shorter events, 374.1 us)
Async XLA Ops:
  7.2 56.1 %all-gather.6.cloned.1.call-start = ((), (), s32[]{:S(2)}) async-start(), calls=%async_computation.4 | async-start | bytes 7667712 | tf_op jit(solution)/shard_map/all_gather | solution.py:513
  12.8 108.2 %all-gather.8.cloned.1.call-start = ((), (), s32[]{:S(2)}) async-start(), calls=%async_computation.5 | async-start | bytes 2359296 | tf_op jit(solution)/shard_map/all_gather | solution.py:513
  13.6 175.3 %all-gather.10.cloned.1.call-start = ((), (), s32[]{:S(2)}) async-start(), calls=%async_computation.6 | async-start | bytes 12976128 | tf_op jit(solution)/shard_map/all_gather | solution.py:513
  17.3 233.2 %all-gather.12.cloned.1.call-start = ((), (), s32[]{:S(2)}) async-start(), calls=%async_computation.7 | async-start | bytes 6488064 | tf_op jit(solution)/shard_map/all_gather | solution.py:513
  23.7 353.6 %all-gather.14.cloned.1.call-start = ((), (), s32[]{:S(2)}) async-start(), calls=%async_computation.8 | async-start | bytes 2621440 | tf_op jit(solution)/shard_map/all_gather | solution.py:620
  63.3 50.5 %collective-permute-start.4 = (bf16[128,2048]{1,0:T(8,128)(2,1)}, bf16[128,2048]{1,0:T(8,128)(2,1)}, u32[]{:S(2)}, u32[]{:S(2)}) collective-permute-start(bf16[128,2048]{1,0:T(8,128)(2,1)} %get-tuple-element.68), channel_id=1, source_target_pairs={{0,1},{1,2},{2,3},{3,0},{4,5},{5,6},{6,7},{7,4},{8,9},{9,10},{10,1... | collective-permute-start | bytes 1572872 | tf_op jit(solution)/shard_map/ppermute | solution.py:424
  64.8 50.7 %collective-permute-start.5 = (bf16[128,2048]{1,0:T(8,128)(2,1)}, bf16[128,2048]{1,0:T(8,128)(2,1)}, u32[]{:S(2)}, u32[]{:S(2)}) collective-permute-start(bf16[128,2048]{1,0:T(8,128)(2,1)} %get-tuple-element.68), channel_id=1, source_target_pairs={{0,3},{1,0},{2,1},{3,2},{4,7},{5,4},{6,5},{7,6},{8,11},{9,8},{10,9... | collective-permute-start | bytes 1572872 | tf_op jit(solution)/shard_map/ppermute | solution.py:424
  67.1 53.9 %collective-permute-start.6 = (bf16[128,2048]{1,0:T(8,128)(2,1)}, bf16[128,2048]{1,0:T(8,128)(2,1)}, u32[]{:S(2)}, u32[]{:S(2)}) collective-permute-start(bf16[128,2048]{1,0:T(8,128)(2,1)} %get-tuple-element.69), channel_id=1, source_target_pairs={{0,1},{1,2},{2,3},{3,0},{4,5},{5,6},{6,7},{7,4},{8,9},{9,10},{10,1... | collective-permute-start | bytes 1572872 | tf_op jit(solution)/shard_map/ppermute | solution.py:424
  67.1 53.9 %collective-permute-start.7 = (bf16[128,2048]{1,0:T(8,128)(2,1)}, bf16[128,2048]{1,0:T(8,128)(2,1)}, u32[]{:S(2)}, u32[]{:S(2)}) collective-permute-start(bf16[128,2048]{1,0:T(8,128)(2,1)} %get-tuple-element.69), channel_id=1, source_target_pairs={{0,3},{1,0},{2,1},{3,2},{4,7},{5,4},{6,5},{7,6},{8,11},{9,8},{10,9... | collective-permute-start | bytes 1572872 | tf_op jit(solution)/shard_map/ppermute | solution.py:424
  117.2 32.3 %collective-permute-start.13 = (bf16[64,2048]{1,0:T(8,128)(2,1)}, bf16[64,2048]{1,0:T(8,128)(2,1)}, u32[]{:S(2)}, u32[]{:S(2)}) collective-permute-start(bf16[64,2048]{1,0:T(8,128)(2,1)} %slice.403), channel_id=1, source_target_pairs={{0,3},{1,0},{2,1},{3,2},{4,7},{5,4},{6,5},{7,6},{8,11},{9,8},{10,9... | collective-permute-start | bytes 786440 | tf_op jit(solution)/shard_map/ppermute | solution.py:424
  129.9 50.9 %collective-permute-start.14 = (bf16[64,2048]{1,0:T(8,128)(2,1)}, bf16[64,2048]{1,0:T(8,128)(2,1)}, u32[]{:S(2)}, u32[]{:S(2)}) collective-permute-start(bf16[64,2048]{1,0:T(8,128)(2,1)} %slice.404), channel_id=1, source_target_pairs={{0,1},{1,2},{2,3},{3,0},{4,5},{5,6},{6,7},{7,4},{8,9},{9,10},{10,1... | collective-permute-start | bytes 786440 | tf_op jit(solution)/shard_map/ppermute | solution.py:424
  138.0 44.7 %collective-permute-start.15 = (bf16[64,2048]{1,0:T(8,128)(2,1)}, bf16[64,2048]{1,0:T(8,128)(2,1)}, u32[]{:S(2)}, u32[]{:S(2)}) collective-permute-start(bf16[64,2048]{1,0:T(8,128)(2,1)} %slice.405), channel_id=1, source_target_pairs={{0,3},{1,0},{2,1},{3,2},{4,7},{5,4},{6,5},{7,6},{8,11},{9,8},{10,9... | collective-permute-start | bytes 786440 | tf_op jit(solution)/shard_map/ppermute | solution.py:424
  144.6 39.7 %collective-permute-start.9 = (bf16[128,2048]{1,0:T(8,128)(2,1)}, bf16[128,2048]{1,0:T(8,128)(2,1)}, u32[]{:S(2)}, u32[]{:S(2)}) collective-permute-start(bf16[128,2048]{1,0:T(8,128)(2,1)} %pad_maximum_fusion.5), channel_id=1, source_target_pairs={{0,1},{1,2},{2,3},{3,0},{4,5},{5,6},{6,7},{7,4},{8,9},{9,10},{10,1... | collective-permute-start | bytes 1572872 | tf_op jit(solution)/shard_map/ppermute | solution.py:424
  146.0 38.3 %collective-permute-start.11 = (bf16[128,2048]{1,0:T(8,128)(2,1)}, bf16[128,2048]{1,0:T(8,128)(2,1)}, u32[]{:S(2)}, u32[]{:S(2)}) collective-permute-start(bf16[128,2048]{1,0:T(8,128)(2,1)} %pad_maximum_fusion.6), channel_id=1, source_target_pairs={{0,3},{1,0},{2,1},{3,2},{4,7},{5,4},{6,5},{7,6},{8,11},{9,8},{10,9... | collective-permute-start | bytes 1572872 | tf_op jit(solution)/shard_map/ppermute | solution.py:424
  250.2 367.7 %reduce-scatter.5.cloned.1.call-start = ((), (), s32[]{:S(2)}) async-start(), calls=%async_computation.9 | async-start | bytes 6488064 | tf_op jit(solution)/shard_map/reduce_scatter | solution.py:517
  270.9 46.7 %collective-permute-start.25 = (bf16[128,2048]{1,0:T(8,128)(2,1)S(1)}, bf16[128,2048]{1,0:T(8,128)(2,1)S(1)}, u32[]{:S(2)}, u32[]{:S(2)}) collective-permute-start(bf16[128,2048]{1,0:T(8,128)(2,1)S(1)} %multiply_convert_fusion.7), channel_id=1, source_target_pairs={{0,3},{1,0},{2,1},{3,2},{4,7},{5,4},{6,5},{7,6},{8,11},{9,8},{10,9... | collective-permute-start | bytes 1572872 | tf_op jit(solution)/shard_map/ppermute | solution.py:424
  294.5 39.7 %collective-permute-start.30 = (bf16[64,2048]{1,0:T(8,128)(2,1)S(1)}, bf16[64,2048]{1,0:T(8,128)(2,1)S(1)}, u32[]{:S(2)}, u32[]{:S(2)}) collective-permute-start(bf16[64,2048]{1,0:T(8,128)(2,1)S(1)} %slice.410), channel_id=1, source_target_pairs={{0,1},{1,2},{2,3},{3,0},{4,5},{5,6},{6,7},{7,4},{8,9},{9,10},{10,1... | collective-permute-start | bytes 786440 | tf_op jit(solution)/shard_map/ppermute | solution.py:424
  348.4 39.9 %collective-permute-start.28 = (bf16[64,2048]{1,0:T(8,128)(2,1)}, bf16[64,2048]{1,0:T(8,128)(2,1)}, u32[]{:S(2)}, u32[]{:S(2)}) collective-permute-start(bf16[64,2048]{1,0:T(8,128)(2,1)} %get-tuple-element.183), channel_id=1, source_target_pairs={{0,1},{1,2},{2,3},{3,0},{4,5},{5,6},{6,7},{7,4},{8,9},{9,10},{10,1... | collective-permute-start | bytes 786440 | tf_op jit(solution)/shard_map/ppermute | solution.py:424
  348.4 39.9 %collective-permute-start.29 = (bf16[64,2048]{1,0:T(8,128)(2,1)}, bf16[64,2048]{1,0:T(8,128)(2,1)}, u32[]{:S(2)}, u32[]{:S(2)}) collective-permute-start(bf16[64,2048]{1,0:T(8,128)(2,1)} %get-tuple-element.182), channel_id=1, source_target_pairs={{0,3},{1,0},{2,1},{3,2},{4,7},{5,4},{6,5},{7,6},{8,11},{9,8},{10,9... | collective-permute-start | bytes 786440 | tf_op jit(solution)/shard_map/ppermute | solution.py:424
  406.6 211.3 %reduce-scatter.7.cloned.1.call-start = ((), (), s32[]{:S(2)}) async-start(), calls=%async_computation.10 | async-start | bytes 12976128 | tf_op jit(solution)/shard_map/reduce_scatter | solution.py:517
  446.2 178.4 %reduce-scatter.9.cloned.1.call-start = ((), (), s32[]{:S(2)}) async-start(), calls=%async_computation.11 | async-start | bytes 2359296 | tf_op jit(solution)/shard_map/reduce_scatter | solution.py:517
  493.6 41.2 %collective-permute-start.46 = (bf16[64,2048]{1,0:T(8,128)(2,1)}, bf16[64,2048]{1,0:T(8,128)(2,1)}, u32[]{:S(2)}, u32[]{:S(2)}) collective-permute-start(bf16[64,2048]{1,0:T(8,128)(2,1)} %slice.416), channel_id=1, source_target_pairs={{0,1},{1,2},{2,3},{3,0},{4,5},{5,6},{6,7},{7,4},{8,9},{9,10},{10,1... | collective-permute-start | bytes 786440 | tf_op jit(solution)/shard_map/ppermute | solution.py:424
  501.1 35.3 %collective-permute-start.47 = (bf16[64,2048]{1,0:T(8,128)(2,1)}, bf16[64,2048]{1,0:T(8,128)(2,1)}, u32[]{:S(2)}, u32[]{:S(2)}) collective-permute-start(bf16[64,2048]{1,0:T(8,128)(2,1)} %slice.417), channel_id=1, source_target_pairs={{0,3},{1,0},{2,1},{3,2},{4,7},{5,4},{6,5},{7,6},{8,11},{9,8},{10,9... | collective-permute-start | bytes 786440 | tf_op jit(solution)/shard_map/ppermute | solution.py:424
  557.8 115.4 %reduce-scatter.11.cloned.1.call-start = ((), (), s32[]{:S(2)}) async-start(), calls=%async_computation.12 | async-start | bytes 7667712 | tf_op jit(solution)/shard_map/reduce_scatter | solution.py:517
  (113 other events, 1630.5 us)
Sparse Core Ops, SparseCore 0:
  12.9 50.3 all-gather.5
  65.2 28.0 all-gather.7
  95.8 67.6 all-gather.9
  165.2 44.2 all-gather.11
  250.3 82.3 all-gather.13
  406.7 58.1 reduce-scatter.4
  468.4 87.1 reduce-scatter.6
  558.8 41.1 reduce-scatter.8
  608.7 61.4 reduce-scatter.10
